TPU v7x, 32 devices: a whole 2x2x4 slice. The times are simulated.
32 devices in a mesh: groups: 2 (over y), pool: 16 (over z, x, core), tp: 1.
Axes of the slice: x: 2, y: 2, z: 4, core: 2. Of those that a mesh axis runs over, the one named last changes fastest.
Arguments:
- suffix_q: bfloat16 [16384, 4096], P(('groups', 'pool'), 'tp'), parts along dimension 0, may hold values from -140 to 140
- fresh_kv: bfloat16 [2048, 2, 8, 512], P(('groups', 'pool'), None, None, 'tp'), parts along dimension 0, may hold values from -6 to 6
- kv_pool: bfloat16 [16384, 2, 8, 512], P(('groups', 'pool'), None, None, 'tp'), parts along dimension 0, may hold values from -6 to 6
- dec_q: bfloat16 [1024, 4096], P(('groups', 'pool'), 'tp'), parts along dimension 0, may hold values from -140 to 140
- fetch_slots: int32 [32, 256], P(('groups', 'pool')), parts along dimension 0, may hold values from 0 to 511, as said below
- prefix_pages: int32 [32, 256], P(('groups', 'pool')), parts along dimension 0, may hold values from 0 to 255, as said below
- prefix_len: int32 [32], P(('groups', 'pool')), parts along dimension 0, may hold values from 8 to 2048, as said below
- suffix_route: int32 [32, 64], P(('groups', 'pool')), parts along dimension 0, may hold values from 0 to 63, as said below
- dec_pages: int32 [1024, 64], P(('groups', 'pool')), parts along dimension 0, may hold values from 0 to 575, as said below
- dec_len: int32 [1024], P(('groups', 'pool')), parts along dimension 0, may hold values from 72 to 512, as said below
Outputs:
- suffix_out: bfloat16 [16384, 4096], P(('groups', 'pool'), 'tp'), parts along dimension 0
- decode_out: bfloat16 [1024, 4096], P(('groups', 'pool'), 'tp'), parts along dimension 0
There are 2 independent parts, one for each index of `groups`. A program takes and returns all parts, laid end to end along the dimension named above; each array names one. Nothing has to cross between parts.
Inputs may be any that keep to these rules, and one draw needn't show every extreme that they name: `fetch_slots`: entry r * 16 + c of row s names the page of device s's pool that fills slot c of requester r from s. `prefix_pages`: each row is a permutation; entry k names the fetched slot s * 16 + c that holds prefix page k. `prefix_len`: some prompt has the most. `suffix_route`: each row is a permutation; entry o * 4 + c names the fresh page sent to owner o as its c-th page from that device. `dec_pages`: entries below 512 name pages of the owner's own pool; 512 + s * 4 + c names the c-th page received from device s; each of these 64 names stands exactly once among an owner's 32 rows, within their first 8 entries. `dec_len`: some request has the most.
All inputs are finite; a program needn't handle non-finite values.
Results may differ from a plain program's by a relative error of at most 0.008.
Values may be sent and summed in bfloat16 or wider, within the bound.
No kernel may reach another device: no remote copies, remote signals or barrier semaphores. Data moves between devices by JAX's collectives and lax.ppermute only.
A program may use at most 256 MiB of HBM per device.

v0:
```python
import functools

import jax
import jax.numpy as jnp
from jax import lax
from jax.experimental import pallas as pl
from jax.experimental.pallas import tpu as pltpu
from jax.sharding import PartitionSpec as P

GROUP = 8
HD = 128
LOG2E = 1.4426950408889634
CEXP = HD**-0.5 * LOG2E
NEG = -1e30
HUGE = 2.0**90
VMEM_LIMIT = 16 << 20
POOL_LIMIT = 56 << 20


HP_FIRST = 4

NT = (((1,), (1,)), ((), ()))
VM = pl.BlockSpec(memory_space=pltpu.VMEM)
SM = pl.BlockSpec(memory_space=pltpu.SMEM)
ANY = pl.BlockSpec(memory_space=pl.ANY)
HBM = pl.BlockSpec(memory_space=pltpu.HBM)
PARAMS = pltpu.CompilerParams(vmem_limit_bytes=VMEM_LIMIT)


def head_at(i):
    return pl.ds(pl.multiple_of(i * HD, HD), HD)


def partner(i, k, size):
    return i ^ k if size & (size - 1) == 0 else lax.rem(i + k, size)


def source(i, k, size):
    return i ^ k if size & (size - 1) == 0 else lax.rem(i - k + size, size)


def gather_pages(kv_pool, fresh_kv, fetch_slots, suffix_route, ks, size, after):
    _, _, page, width = kv_pool.shape
    n = len(ks)
    cap, caps = fetch_slots.shape[1] // size, suffix_route.shape[1] // size
    each = cap + caps

    def body(slots_ref, routes_ref, pool_ref, fresh_ref, *rest):
        outs, sem = rest[-n - 1 : -1], rest[-1]
        me = lax.axis_index("pool")
        for i, k in enumerate(ks):
            dest = partner(me, k, size)
            for c in range(cap):
                pltpu.make_async_copy(
                    pool_ref.at[slots_ref[0, dest * cap + c]], outs[i].at[:, c], sem.at[i]
                ).start()
            for c in range(caps):
                pltpu.make_async_copy(
                    fresh_ref.at[routes_ref[0, dest * caps + c]], outs[i].at[:, cap + c], sem.at[i]
                ).start()
        for i in range(n):
            pltpu.make_async_copy(outs[i], outs[i], sem.at[i]).wait()

    shape = (2, each, page, width)
    return pl.pallas_call(
        body,
        out_shape=[pltpu.VMEM(shape, kv_pool.dtype)] * n,
        in_specs=[SM, SM, HBM, HBM] + [ANY] * len(after),
        out_specs=[VM] * n,
        scratch_shapes=[pltpu.SemaphoreType.DMA((n,))],
        compiler_params=pltpu.CompilerParams(vmem_limit_bytes=POOL_LIMIT),
        cost_estimate=pl.CostEstimate(
            flops=0, transcendentals=0, bytes_accessed=2 * n * each * 2 * page * width * 2
        ),
        name="gather_pages",
    )(fetch_slots, suffix_route, kv_pool, fresh_kv, *after)


def mark_visible(vis_ref, at, k, cap, page, pages_ref, plen_ref, size):
    wanted = pages_ref[...]
    keys = cap * page
    order = lax.broadcasted_iota(jnp.int32, (keys, wanted.shape[1]), 1)
    token = lax.broadcasted_iota(jnp.int32, (keys, 1), 0)
    name = source(lax.axis_index("pool"), k, size) * cap + token // page
    place = jnp.sum(jnp.where(wanted == name, order, 0), axis=1, keepdims=True)
    seen = place * page + token % page < plen_ref[0]
    vis_ref[at : at + keys, :] = jnp.broadcast_to(jnp.where(seen, 1.0, 0.0), (keys, HD))


def place_keys(k_ref, v_ref, vis_ref, vis_at, at, g, piece, stand_in, cap, page):
    keys = cap * page
    rows = slice(at, at + keys)
    seen = vis_ref[vis_at : vis_at + keys, :] > 0
    key = piece[0, 0:cap, :, head_at(g)].reshape(keys, HD).astype(jnp.float32)
    val = piece[1, 0:cap, :, head_at(g)].reshape(keys, HD).astype(jnp.float32)
    k_ref[rows, 0:HD] = jnp.where(seen, key, stand_in).astype(jnp.bfloat16)
    v_ref[rows, 0:HD] = jnp.where(seen, val, 0.0).astype(jnp.bfloat16)


def prefill_first(q, fresh, after):
    tokens, qwidth = q.shape
    _, width = fresh.shape[2:]
    rows = min(256, tokens)

    def body(q_ref, f_ref, _, m_ref, acc_ref, l_ref, k_ref, v_ref):
        v_ref[:, HD:] = jnp.ones((tokens, HD), jnp.bfloat16)
        lane = lax.broadcasted_iota(jnp.int32, (rows, HD), 1)
        row = lax.broadcasted_iota(jnp.int32, (rows, rows), 0)
        col = lax.broadcasted_iota(jnp.int32, (rows, rows), 1)

        def group(g, carry):
            k_ref[...] = f_ref[:, 0, :, head_at(g)].reshape(tokens, HD)
            v_ref[:, 0:HD] = f_ref[:, 1, :, head_at(g)].reshape(tokens, HD)

            def heads(b, carry):
                for h in range(HP_FIRST):
                    cols = head_at(g * GROUP + b * HP_FIRST + h)
                    for r in range(0, tokens, rows):
                        rs = slice(r, r + rows)
                        s = lax.dot_general(
                            q_ref[rs, cols], k_ref[0 : r + rows, :], NT, preferred_element_type=jnp.float32
                        )
                        diag = jnp.where(col <= row, s[:, r:], NEG)
                        s = jnp.concatenate([s[:, :r], diag], 1) if r else diag
                        m = jnp.max(s, axis=1, keepdims=True).astype(jnp.bfloat16).astype(jnp.float32)
                        p = jnp.exp2((s - m) * CEXP).astype(jnp.bfloat16)
                        new = jnp.dot(p, v_ref[0 : r + rows, :], preferred_element_type=jnp.float32)
                        acc_ref[rs, cols] = new[:, :HD]
                        l_ref[rs, cols] = new[:, HD:]
                        m_ref[rs, cols] = jnp.where(lane == 0, m, 0.0).astype(jnp.bfloat16)
                return carry

            return lax.fori_loop(0, GROUP // HP_FIRST, heads, carry)

        lax.fori_loop(0, width // HD, group, 0)

    wide = pltpu.VMEM((tokens, qwidth), jnp.float32)
    work = tokens * tokens * (qwidth // HD) // 2
    return pl.pallas_call(
        body,
        out_shape=[pltpu.VMEM((tokens, qwidth), jnp.bfloat16), wide, wide],
        in_specs=[VM, VM, ANY],
        out_specs=[VM] * 3,
        scratch_shapes=[
            pltpu.VMEM((tokens, HD), jnp.bfloat16),
            pltpu.VMEM((tokens, 2 * HD), jnp.bfloat16),
        ],
        compiler_params=PARAMS,
        cost_estimate=pl.CostEstimate(flops=8 * HD * work, transcendentals=work, bytes_accessed=8 * work // HD),
        name="prefill_first",
    )(q, fresh, after)


def add_pages(k_ref, v_ref, q_ref, m_ref, g, emit):
    for h in range(GROUP):
        cols = head_at(g * GROUP + h)
        lhs = jnp.concatenate([q_ref[:, cols], m_ref[:, cols]], 1)
        s = lax.dot_general(lhs, k_ref[...], NT, preferred_element_type=jnp.float32)
        p = jnp.exp2(s * CEXP).astype(jnp.bfloat16)
        new = jnp.dot(p, v_ref[...], preferred_element_type=jnp.float32)
        emit(cols, new[:, :HD], new[:, HD:])


def start_pages(vis_ref, k_ref, v_ref, pages_ref, plen_ref, ks, cap, page, size):
    keys = k_ref.shape[0]
    for i, k in enumerate(ks):
        mark_visible(vis_ref, i * cap * page, k, cap, page, pages_ref, plen_ref, size)
    lane = lax.broadcasted_iota(jnp.int32, (keys, HD), 1)
    k_ref[:, HD:] = jnp.where(lane == 0, -1.0, 0.0).astype(jnp.bfloat16)
    v_ref[:, HD:] = vis_ref[...].astype(jnp.bfloat16)


def prefill_more(q, fresh, pieces, ks, pages, plen, state, cap, size):
    tokens, qwidth = q.shape
    page, width = fresh.shape[2:]
    n = len(pieces)
    keys = n * cap * page

    def body(*refs):
        plen_ref, pages_ref, q_ref, f_ref = refs[:4]
        piece_refs = refs[4 : 4 + n]
        m_ref, acc_in, l_in, acc_ref, l_ref, vis_ref, k_ref, v_ref = refs[4 + n :]
        start_pages(vis_ref, k_ref, v_ref, pages_ref, plen_ref, ks, cap, page, size)

        def group(g, carry):
            stand_in = f_ref[0, 0, :, head_at(g)][0:1].astype(jnp.float32)
            for i in range(n):
                at = i * cap * page
                place_keys(k_ref, v_ref, vis_ref, at, at, g, piece_refs[i], stand_in, cap, page)

            def emit(cols, acc, total):
                acc_ref[:, cols] = acc_in[:, cols] + acc
                l_ref[:, cols] = l_in[:, cols] + total

            add_pages(k_ref, v_ref, q_ref, m_ref, g, emit)
            return carry

        lax.fori_loop(0, width // HD, group, 0)

    work = tokens * keys * (qwidth // HD)
    wide = pltpu.VMEM((tokens, qwidth), jnp.float32)
    return pl.pallas_call(
        body,
        out_shape=[wide, wide],
        in_specs=[SM, VM, VM, VM] + [VM] * n + [VM] * 3,
        out_specs=[VM, VM],
        input_output_aliases={5 + n: 0, 6 + n: 1},
        scratch_shapes=[
            pltpu.VMEM((keys, HD), jnp.float32),
            pltpu.VMEM((keys, 2 * HD), jnp.bfloat16),
            pltpu.VMEM((keys, 2 * HD), jnp.bfloat16),
        ],
        compiler_params=PARAMS,
        cost_estimate=pl.CostEstimate(
            flops=8 * HD * work, transcendentals=work, bytes_accessed=8 * work // HD
        ),
        name="prefill_more",
    )(plen, pages, q, fresh, *pieces, *state)


def token_counts(full, part, rest, page):
    pages = full.shape[1]
    key = lax.broadcasted_iota(jnp.int32, (pages, pages * page), 1) // page
    row = lax.broadcasted_iota(jnp.int32, (pages, pages * page), 0)
    spread = jnp.where(key == row, 1.0, 0.0).astype(jnp.bfloat16)
    times = jnp.dot(full, spread, preferred_element_type=jnp.float32)
    edge = jnp.dot(part, spread, preferred_element_type=jnp.float32)
    token = lax.broadcasted_iota(jnp.int32, times.shape, 1) % page
    return times + jnp.where(token < rest, edge, 0.0)


def decode_fold(q_ref, g, key, val, times, m_old, l_old, acc_old):
    requests = times.shape[0]
    q = jnp.concatenate(
        [q_ref[:, (g * GROUP + h) * HD : (g * GROUP + h + 1) * HD] for h in range(GROUP)], 0
    )
    s = lax.dot_general(q, key, NT, preferred_element_type=jnp.float32)
    keys = s.shape[1]
    s = s.reshape(GROUP, requests, keys)
    s = jnp.where((times > 0)[None], s, NEG).reshape(GROUP * requests, keys)
    m = jnp.maximum(jnp.max(s, axis=1, keepdims=True), m_old)
    p = jnp.exp2((s - m) * CEXP).reshape(GROUP, requests, keys) * times[None]
    p = p.reshape(GROUP * requests, keys)
    total = jnp.sum(p, axis=1, keepdims=True)
    new = jnp.dot(p.astype(jnp.bfloat16), val, preferred_element_type=jnp.float32)
    alpha = jnp.exp2((m_old - m) * CEXP)
    return m, l_old * alpha + total, acc_old * alpha + new


def decode_pool(dec_q, kv_pool, full, part, rest):
    slots, _, page, width = kv_pool.shape
    requests = dec_q.shape[0]
    heads_kv = width // HD
    block = 128 if slots % 128 == 0 else slots
    steps = slots // block

    def body(q_ref, kv_ref, full_ref, part_ref, rest_ref, acc_ref, m_ref, l_ref):
        @pl.when(pl.program_id(0) == 0)
        def _():
            acc_ref[...] = jnp.zeros_like(acc_ref)
            m_ref[...] = jnp.full_like(m_ref, NEG)
            l_ref[...] = jnp.zeros_like(l_ref)

        times = token_counts(full_ref[...], part_ref[...], rest_ref[...], page)
        for g in range(heads_kv):
            cols = slice(g * HD, (g + 1) * HD)
            key = kv_ref[:, 0, :, cols].reshape(block * page, HD)
            val = kv_ref[:, 1, :, cols].reshape(block * page, HD)
            m, l, acc = decode_fold(
                q_ref, g, key, val, times, m_ref[g, :, 0:1], l_ref[g, :, 0:1], acc_ref[g]
            )
            m_ref[g] = jnp.broadcast_to(m, m_ref.shape[1:])
            l_ref[g] = jnp.broadcast_to(l, l_ref.shape[1:])
            acc_ref[g] = acc

    shape = (heads_kv, GROUP * requests, HD)
    whole = pl.BlockSpec(shape, lambda i: (0, 0, 0))
    return pl.pallas_call(
        body,
        grid=(steps,),
        out_shape=[jax.ShapeDtypeStruct(shape, jnp.float32)] * 3,
        in_specs=[
            pl.BlockSpec(dec_q.shape, lambda i: (0, 0)),
            pl.BlockSpec((block, 2, page, width), lambda i: (i, 0, 0, 0)),
            pl.BlockSpec((requests, block), lambda i: (0, i)),
            pl.BlockSpec((requests, block), lambda i: (0, i)),
            pl.BlockSpec(rest.shape, lambda i: (0, 0)),
        ],
        out_specs=[whole] * 3,
        compiler_params=pltpu.CompilerParams(vmem_limit_bytes=POOL_LIMIT),
        cost_estimate=pl.CostEstimate(
            flops=4 * HD * heads_kv * GROUP * requests * slots * page,
            transcendentals=heads_kv * GROUP * requests * slots * page,
            bytes_accessed=slots * 2 * page * width * 2,
        ),
        name="decode_pool",
    )(dec_q, kv_pool, full, part, rest)


def fresh_rows(piece, which, cap, cols):
    rows = piece[which, cap:, :, cols]
    return rows.reshape(rows.shape[0] * rows.shape[1], HD)


def decode_fresh(dec_q, pieces, state, full, part, rest, cap):
    page, width = pieces[0].shape[2:]
    caps = pieces[0].shape[1] - cap
    n = len(pieces)
    heads_kv = width // HD
    rows = state[0].shape[1]

    def body(*refs):
        q_ref, acc_in, m_in, l_in, full_ref, part_ref, rest_ref = refs[:7]
        piece_refs = refs[7 : 7 + n]
        acc_ref, m_ref, l_ref = refs[7 + n :]
        times = token_counts(full_ref[...], part_ref[...], rest_ref[...], page)
        for g in range(heads_kv):
            cols = slice(g * HD, (g + 1) * HD)
            key = jnp.concatenate([fresh_rows(p, 0, 0, cols) for p in piece_refs], 0)
            val = jnp.concatenate([fresh_rows(p, 1, 0, cols) for p in piece_refs], 0)
            m, l, acc = decode_fold(
                q_ref, g, key, val, times, m_in[g, :, 0:1], l_in[g, :, 0:1], acc_in[g]
            )
            m_ref[g] = jnp.broadcast_to(m, m_ref.shape[1:])
            l_ref[g] = jnp.broadcast_to(l, l_ref.shape[1:])
            acc_ref[g] = acc

    whole = lambda a: pl.BlockSpec(a.shape, lambda i: (0,) * a.ndim)
    each = pieces[0].shape[1]
    return pl.pallas_call(
        body,
        grid=(1,),
        out_shape=[jax.ShapeDtypeStruct(a.shape, a.dtype) for a in state],
        in_specs=[whole(a) for a in (dec_q, *state, full, part, rest)]
        + [pl.BlockSpec((2, caps, page, width), lambda i: (0, each // caps - 1, 0, 0))] * n,
        out_specs=[whole(a) for a in state],
        compiler_params=PARAMS,
        cost_estimate=pl.CostEstimate(
            flops=4 * HD * heads_kv * rows * n * caps * page,
            transcendentals=heads_kv * rows * n * caps * page,
            bytes_accessed=n * caps * 2 * page * width * 2,
        ),
        name="decode_fresh",
    )(dec_q, *state, full, part, rest, *pieces)


def finish(dec_q, dec_state, times, q, fresh, pages, plen, state, pieces, ks, last, cap, size):
    page, width = fresh.shape[2:]
    requests = dec_q.shape[0]
    heads_kv = width // HD
    tokens, qwidth = q.shape
    n, tail = len(pieces), len(last)
    keys = cap * page
    rows = min(128, tokens)
    held = n * keys

    def body(*refs):
        dq_ref, dacc_ref, dm_ref, dl_ref, times_ref, q_ref, f_ref, pages_ref, plen_ref = refs[:9]
        m_ref, acc_ref, l_ref = refs[9:12]
        last_refs = refs[12 : 12 + tail]
        piece_refs = refs[12 + tail : 12 + tail + n]
        (dec_ref, out_hbm, out_ref, sem, vis_ref, k_ref, v_ref, all_vis, all_k, all_v, page_ref, block_ref) = (
            refs[12 + tail + n :]
        )
        start_pages(vis_ref, k_ref, v_ref, pages_ref, plen_ref, last, cap, page, size)

        def out_copy(g):
            cols = pl.ds(pl.multiple_of(g * GROUP * HD, GROUP * HD), GROUP * HD)
            return pltpu.make_async_copy(out_ref.at[:, cols], out_hbm.at[:, cols], sem.at[g])

        def group(g, sums):
            stand_in = f_ref[0, 0, :, head_at(g)][0:1].astype(jnp.float32)
            for i in range(tail):
                place_keys(k_ref, v_ref, vis_ref, i * keys, i * keys, g, last_refs[i], stand_in, cap, page)
            partial = []

            def emit(cols, acc, total):
                total = l_ref[:, cols] + total
                out_ref[:, cols] = ((acc_ref[:, cols] + acc) / total).astype(out_ref.dtype)
                partial.append(jnp.sum(total.reshape(-1, 8, HD), axis=0))

            add_pages(k_ref, v_ref, q_ref, m_ref, g, emit)
            out_copy(g).start()
            return sum(partial, sums)

        sums = lax.fori_loop(0, heads_kv, group, jnp.zeros((8, HD), jnp.float32))

        times = times_ref[...]
        for g in range(heads_kv):
            cols = slice(g * HD, (g + 1) * HD)
            key = jnp.concatenate([fresh_rows(p, 0, cap, cols) for p in last_refs], 0)
            val = jnp.concatenate([fresh_rows(p, 1, cap, cols) for p in last_refs], 0)
            _, l, acc = decode_fold(
                dq_ref, g, key, val, times, dm_ref[g, :, 0:1], dl_ref[g, :, 0:1], dacc_ref[g]
            )
            done = (acc / l).astype(dec_ref.dtype)
            for h in range(GROUP):
                at = (g * GROUP + h) * HD
                dec_ref[:, at : at + HD] = done[h * requests : (h + 1) * requests]
        for g in range(heads_kv):
            out_copy(g).wait()

        @pl.when(jnp.logical_not(jnp.sum(sums) <= HUGE))
        def _():
            for i, k in enumerate(ks):
                mark_visible(all_vis, i * keys, k, cap, page, pages_ref, plen_ref, size)
            all_v[0:tokens, HD:] = jnp.ones((tokens, HD), jnp.bfloat16)
            all_v[tokens:, HD:] = all_vis[...].astype(jnp.bfloat16)
            col = lax.broadcasted_iota(jnp.int32, (rows, tokens), 1)
            row = lax.broadcasted_iota(jnp.int32, (rows, tokens), 0)

            def again(g, carry):
                all_k[0:tokens, :] = f_ref[:, 0, :, head_at(g)].reshape(tokens, HD)
                all_v[0:tokens, 0:HD] = f_ref[:, 1, :, head_at(g)].reshape(tokens, HD)
                stand_in = f_ref[0, 0, :, head_at(g)][0:1].astype(jnp.float32)
                for i in range(n):
                    pltpu.sync_copy(piece_refs[i].at[:, 0:cap], page_ref)
                    place_keys(all_k, all_v, all_vis, i * keys, tokens + i * keys, g, page_ref, stand_in, cap, page)

                def block(b, carry):
                    r = pl.multiple_of((b % (tokens // rows)) * rows, rows)
                    cols = head_at(g * GROUP + b // (tokens // rows))
                    qb = q_ref[pl.ds(r, rows), cols]
                    s = lax.dot_general(qb, all_k[...], NT, preferred_element_type=jnp.float32)
                    own = jnp.where(col <= row + r, s[:, :tokens], NEG)
                    s = jnp.concatenate([own, s[:, tokens:]], 1)
                    m = jnp.max(s, axis=1, keepdims=True)
                    p = jnp.exp2((s - m) * CEXP).astype(jnp.bfloat16)
                    new = jnp.dot(p, all_v[...], preferred_element_type=jnp.float32)
                    block_ref[...] = (new[:, :HD] / new[:, HD:]).astype(block_ref.dtype)
                    pltpu.sync_copy(block_ref, out_hbm.at[pl.ds(r, rows), cols])
                    return carry

                return lax.fori_loop(0, GROUP * (tokens // rows), block, carry)

            lax.fori_loop(0, heads_kv, again, 0)

    work = tokens * tail * keys * (qwidth // HD)
    return pl.pallas_call(
        body,
        out_shape=[
            jax.ShapeDtypeStruct(dec_q.shape, dec_q.dtype),
            jax.ShapeDtypeStruct(q.shape, q.dtype),
        ],
        in_specs=[VM] * 8 + [SM] + [VM] * (3 + tail) + [ANY] * n,
        out_specs=[VM, ANY],
        scratch_shapes=[
            pltpu.VMEM(q.shape, q.dtype),
            pltpu.SemaphoreType.DMA((heads_kv,)),
            pltpu.VMEM((tail * keys, HD), jnp.float32),
            pltpu.VMEM((tail * keys, 2 * HD), jnp.bfloat16),
            pltpu.VMEM((tail * keys, 2 * HD), jnp.bfloat16),
            pltpu.VMEM((held, HD), jnp.float32),
            pltpu.VMEM((tokens + held, HD), jnp.bfloat16),
            pltpu.VMEM((tokens + held, 2 * HD), jnp.bfloat16),
            pltpu.VMEM((2, cap, page, width), q.dtype),
            pltpu.VMEM((rows, HD), q.dtype),
        ],
        compiler_params=PARAMS,
        cost_estimate=pl.CostEstimate(
            flops=8 * HD * work, transcendentals=work, bytes_accessed=8 * work // HD
        ),
        name="finish",
    )(dec_q, *dec_state, times, q, fresh, pages, plen, *state, *[pieces[ks.index(k)] for k in last], *pieces)


def send_order(size):
    if size == 16:
        return [12, 8, 1, 2, 3, 4, 13, 5, 9, 6, 14, 7, 10, 15, 11]
    return list(range(1, size))


def shards(
    size,
    suffix_q,
    fresh_kv,
    kv_pool,
    dec_q,
    fetch_slots,
    prefix_pages,
    prefix_len,
    suffix_route,
    dec_pages,
    dec_len,
):
    page = kv_pool.shape[2]
    slots = kv_pool.shape[0]
    cap = fetch_slots.shape[1] // size
    caps = suffix_route.shape[1] // size
    sends = send_order(size)
    lead = max(1, size // 8)
    batches = [sends[:lead], sends[lead:] + [0]]
    outgoing, after = {}, []
    for ks in batches:
        outs = gather_pages(kv_pool, fresh_kv, fetch_slots, suffix_route, ks, size, after)
        after = outs[:1]
        outgoing |= dict(zip(ks, outs, strict=True))
    arrived = {0: outgoing[0]}
    for k in sends:
        pairs = [(i, i ^ k if size & (size - 1) == 0 else (i + k) % size) for i in range(size)]
        arrived[k] = lax.ppermute(outgoing[k], "pool", pairs)

    context = dec_pages.shape[1]
    position = jnp.arange(context, dtype=jnp.int32)[None, :]
    whole_pages = (position + 1) * page <= dec_len[:, None]
    edge_page = position == dec_len[:, None] // page
    rest = (dec_len % page)[:, None]

    def counts(names):
        same = dec_pages[:, :, None] == names[None, None, :]
        full = jnp.sum((same & whole_pages[:, :, None]).astype(jnp.float32), 1).astype(jnp.bfloat16)
        part = jnp.sum((same & edge_page[:, :, None]).astype(jnp.float32), 1).astype(jnp.bfloat16)
        return full, part

    groups = arrival_groups([0] + sends)
    order = [k for ks in groups for k in ks]
    early, last = order[: -len(groups[-1])], groups[-1]
    me = lax.axis_index("pool")

    def fresh_names(ks):
        srcs = source(jnp.full((len(ks),), me, jnp.int32), jnp.asarray(ks, jnp.int32), size)
        return slots + jnp.repeat(srcs, caps) * caps + jnp.tile(jnp.arange(caps, dtype=jnp.int32), len(ks))

    last_names = jnp.repeat(fresh_names(last), page)[None, None, :]
    last_token = (jnp.arange(last_names.shape[2], dtype=jnp.int32) % page)[None, None, :]
    last_seen = position[:, :, None] * page + last_token < dec_len[:, None, None]
    last_times = jnp.sum(((dec_pages[:, :, None] == last_names) & last_seen).astype(jnp.float32), 1)

    dec_state = decode_pool(dec_q, kv_pool, *counts(jnp.arange(slots, dtype=jnp.int32)), rest)
    state = prefill_first(suffix_q, fresh_kv, dec_state[1])
    for ks in groups[:-1]:
        new = prefill_more(
            suffix_q, fresh_kv, [arrived[k] for k in ks], ks, prefix_pages, prefix_len, state, cap, size
        )
        state = (state[0], *new)
    dec_state = decode_fresh(
        dec_q, [arrived[k] for k in early], dec_state, *counts(fresh_names(early)), rest, cap
    )
    decode_out, suffix_out = finish(
        dec_q,
        dec_state,
        last_times,
        suffix_q,
        fresh_kv,
        prefix_pages,
        prefix_len,
        state,
        [arrived[k] for k in order],
        order,
        last,
        cap,
        size,
    )
    return (suffix_out, decode_out)


def arrival_groups(order):
    size = len(order)
    if size == 16:
        return [[0, 1, 2, 3], [12, 4, 8, 5], [13, 6, 9, 7], [14, 10], [15], [11]]
    per = -(-size // 4)
    return [order[i : min(i + per, size - 1)] for i in range(0, size - 1, per)] + [order[-1:]]


def solution(mesh):
    size = mesh.shape["pool"]
    return jax.shard_map(
        functools.partial(shards, size),
        mesh=mesh,
        in_specs=(
            P(("groups", "pool"), "tp"),
            P(("groups", "pool"), None, None, "tp"),
            P(("groups", "pool"), None, None, "tp"),
            P(("groups", "pool"), "tp"),
            P(("groups", "pool"), None),
            P(("groups", "pool"), None),
            P(("groups", "pool")),
            P(("groups", "pool"), None),
            P(("groups", "pool"), None),
            P(("groups", "pool")),
        ),
        out_specs=(P(("groups", "pool"), "tp"), P(("groups", "pool"), "tp")),
        check_vma=False,
    )
```

profile of v0, /device:TPU:0, one launch (start us, length us, event | category | flops | bytes accessed | tf_op | source)
XLA Modules:
  0.0 178.0 jit_solution(15408240528358615655)
XLA Ops:
  0.6 0.0 copy-start.35
  0.7 2.7 %gather_pages.2 = (bf16[2,20,8,512]{3,2,1,0:T(8,128)(2,1)}, bf16[2,20,8,512]{3,2,1,0:T(8,128)(2,1)}) custom-call(s32[1,256]{1,0:T(1,128)} %slots_ref.3, s32[1,64]{1,0:T(1,128)} %routes_ref.3, bf16[512,2,8,512]{3,2,1,0:T(8,128)(2,1)} %pool_ref.3, bf16[64,2,8,512]{3,2,1,0:T(8,128)(2,1)} %refs_6_.1), custom_call_target="tpu_custom_call" | custom-call | bytes 1310720 | tf_op jit(solution)/shard_map/gather_pages/pallas_call | solution.py:65
  3.4 4.1 %collective-permute-start.5 = (bf16[2,20,8,512]{3,2,1,0:T(8,128)(2,1)}, bf16[2,20,8,512]{3,2,1,0:T(8,128)(2,1)}, u32[]{:S(2)}, u32[]{:S(2)}) collective-permute-start(bf16[2,20,8,512]{3,2,1,0:T(8,128)(2,1)} %get-tuple-element.48), channel_id=1, source_target_pairs={{0,8},{1,9},{2,10},{3,11},{4,12},{5,13},{6,14},{7,15},{8,0},{9,1},... | collective-permute-start | bytes 983048 | tf_op jit(solution)/shard_map/ppermute | solution.py:501
  7.5 1.3 collective-permute-start.3
  8.9 4.1 %gather_pages.3 = (bf16[2,20,8,512]{3,2,1,0:T(8,128)(2,1)}, bf16[2,20,8,512]{3,2,1,0:T(8,128)(2,1)}, bf16[2,20,8,512]{3,2,1,0:T(8,128)(2,1)}, bf16[2,20,8,512]{3...) custom-call(s32[1,256]{1,0:T(1,128)} %slots_ref.3, ...), custom_call_target="tpu_custom_call" | custom-call | bytes 9175040 | tf_op jit(solution)/shard_map/gather_pages/pallas_call | solution.py:65
  13.0 0.7 copy-done.5
  13.7 0.7 copy-done.13
  14.4 0.7 copy-done.15
  15.2 0.7 copy-done.17
  15.9 0.7 copy-done.19
  16.7 0.7 copy-done.21
  17.4 0.7 copy-done.23
  18.1 0.7 copy-done.25
  18.8 0.7 copy-done.27
  19.5 0.8 copy-done.29
  20.3 0.8 copy-done.31
  21.1 0.0 collective-permute-start
  21.1 1.5 collective-permute-start.1
  22.6 0.4 collective-permute-start.2
  23.7 0.1 broadcast_in_dim.14
  23.7 0.1 eq.71
  23.8 0.1 iota_add_fusion
  23.9 0.1 add.83
  24.0 0.7 copy.28.rest_ref.refs_6_
  24.7 0.1 iota_compare_fusion.1
  24.8 2.4 %convert_reduce_fusion = (bf16[32,512]{1,0:T(8,128)(2,1)}, bf16[32,512]{1,0:T(8,128)(2,1)}) fusion(s32[32,64]{1,0:T(8,128)S(1)} %copy-done.33, pred[32,64]{1,0:T(8,128)(4,1)S(1)} %get-tuple-element.82, pred[32,64]{1,0:T(8,128)(4,1)S(1)} %get-tuple-element.83), kind=kLoop, calls=%fused_computation | loop fusion | flops 7307264 | bytes 77824 | tf_op jit(solution)/shard_map/reduce_sum | solution.py:512
  27.2 0.7 convert_reduce_fusion.2
  27.8 0.1 copy.30.refs_5_
  27.9 0.1 copy.29.refs_4_
  28.0 0.1 broadcast_add_fusion
  28.1 0.3 convert_reduce_fusion.4.refs_4_
  28.4 13.8 %decode_pool.1 = (f32[4,256,128]{2,1,0:T(8,128)}, f32[4,256,128]{2,1,0:T(8,128)}, f32[4,256,128]{2,1,0:T(8,128)}) custom-call(bf16[32,4096]{1,0:T(8,128)(2,1)} %refs_0_.8, bf16[512,2,8,512]{3,2,1,0:T(8,128)(2,1)} %pool_ref.3, bf16[32,512]{1,0:T(8,128)(2,1)} %get-tuple-element.79.full_ref, bf16[32,512]{1,0:T(8,128)(2,1)} %get-tuple-element.78.part_ref, ...), custom_call_target="tpu_custom_call" | custom-call | flops 2147483648 | bytes 8388608 | tf_op jit(solution)/shard_map/decode_pool/pallas_call | solution.py:278
  42.2 2.2 %copy-done = bf16[512,4096]{1,0:T(8,128)(2,1)S(1)} copy-done((bf16[512,4096]{1,0:T(8,128)(2,1)S(1)}, bf16[512,4096]{1,0:T(8,128)(2,1)}, u32[]{:S(2)}) %copy-start) | copy-done | bytes 4194328
  44.4 1.2 copy-done.2
  45.7 1.0 copy-done.8
  46.7 15.8 %prefill_first.1 = (bf16[512,4096]{1,0:T(8,128)(2,1)S(1)}, f32[512,4096]{1,0:T(8,128)S(1)}, f32[512,4096]{1,0:T(8,128)S(1)}) custom-call(bf16[512,4096]{1,0:T(8,128)(2,1)S(1)} %copy-done, bf16[64,2,8,512]{3,2,1,0:T(8,128)(2,1)S(1)} %copy-done.2, f32[4,256,128]{2,1,0:T(8,128)S(1)} %copy-done.8), custom_call_target="tpu_custom_call" | custom-call | flops 4294967296 | bytes 262144 | tf_op jit(solution)/shard_map/prefill_first/pallas_call | solution.py:139
  62.6 0.0 collective-permute-done.refs_8_.refs_5_.refs_14_
  62.6 0.4 collective-permute-start.4
  63.0 0.0 collective-permute-done.1.refs_9_.refs_6_.refs_15_
  63.0 1.3 collective-permute-start.6
  64.3 0.0 collective-permute-done.2.refs_10_.refs_7_.refs_16_
  64.3 2.6 %collective-permute-start.7 = (bf16[2,20,8,512]{3,2,1,0:T(8,128)(2,1)S(1)}, bf16[2,20,8,512]{3,2,1,0:T(8,128)(2,1)S(1)}, u32[]{:S(2)}, u32[]{:S(2)}) collective-permute-start(bf16[2,20,8,512]{3,2,1,0:T(8,128)(2,1)S(1)} %copy-done.28), channel_id=1, source_target_pairs={{0,13},{1,12},{2,15},{3,14},{4,9},{5,8},{6,11},{7,10},{8,5},{9,4},... | collective-permute-start | bytes 983048 | tf_op jit(solution)/shard_map/ppermute | solution.py:501
  66.9 13.3 %prefill_more.5 = (f32[512,4096]{1,0:T(8,128)S(1)}, f32[512,4096]{1,0:T(8,128)S(1)}) custom-call(s32[1]{0:T(128)S(6)} %copy.42.refs_0_.refs_8_, s32[1,256]{1,0:T(1,128)S(1)} %copy-done.12, bf16[512,4096]{1,0:T(8,128)(2,1)S(1)} %copy-done.1, bf16[64,2,8,512]{3,2,1,0:T(8,128)(2,1)S(1)} %copy-done.3, ...), custom_call_target="tpu_custom_call", output_to_operand_aliasing={{0}: (9, {}), {1}: (10, {})} | custom-call | flops 8589934592 | bytes 524288 | tf_op jit(solution)/shard_map/prefill_more/pallas_call | solution.py:202
  80.3 0.0 collective-permute-done.5.refs_13_.refs_6_.refs_19_
  80.3 0.8 collective-permute-start.8
  81.1 0.0 collective-permute-done.3.refs_11_.refs_4_.refs_17_
  81.1 1.5 collective-permute-start.9
  82.6 0.0 collective-permute-done.4.refs_12_.refs_5_.refs_18_
  82.6 0.5 collective-permute-start.10
  83.1 3.0 %collective-permute-start.11 = (bf16[2,20,8,512]{3,2,1,0:T(8,128)(2,1)S(1)}, bf16[2,20,8,512]{3,2,1,0:T(8,128)(2,1)S(1)}, u32[]{:S(2)}, u32[]{:S(2)}) collective-permute-start(bf16[2,20,8,512]{3,2,1,0:T(8,128)(2,1)S(1)} %copy-done.20), channel_id=1, source_target_pairs={{0,14},{1,15},{2,12},{3,13},{4,10},{5,11},{6,8},{7,9},{8,6},{9,7},... | collective-permute-start | bytes 983048 | tf_op jit(solution)/shard_map/ppermute | solution.py:501
  86.1 13.4 %prefill_more.6 = (f32[512,4096]{1,0:T(8,128)S(1)}, f32[512,4096]{1,0:T(8,128)S(1)}) custom-call(s32[1]{0:T(128)S(6)} %copy.42.refs_0_.refs_8_, s32[1,256]{1,0:T(1,128)S(1)} %copy-done.12, bf16[512,4096]{1,0:T(8,128)(2,1)S(1)} %copy-done.1, bf16[64,2,8,512]{3,2,1,0:T(8,128)(2,1)S(1)} %copy-done.3, ...), custom_call_target="tpu_custom_call", output_to_operand_aliasing={{0}: (9, {}), {1}: (10, {})} | custom-call | flops 8589934592 | bytes 524288 | tf_op jit(solution)/shard_map/prefill_more/pallas_call | solution.py:202
  99.5 1.3 collective-permute-start.12
  100.8 2.0 %collective-permute-done.8.refs_16_.refs_5_.refs_22_ = bf16[2,20,8,512]{3,2,1,0:T(8,128)(2,1)S(1)} collective-permute-done((bf16[2,20,8,512]{3,2,1,0:T(8,128)(2,1)S(1)}, bf16[2,20,8,512]{3,2,1,0:T(8,128)(2,1)S(1)}, u32[]{:S(2)}, u32[]{:S(2)}) %collective-permute-start.8) | collective-permute-done | bytes 327712 | tf_op jit(solution)/shard_map/ppermute | solution.py:501
  102.8 7.5 %collective-permute-start.13 = (bf16[2,20,8,512]{3,2,1,0:T(8,128)(2,1)S(1)}, bf16[2,20,8,512]{3,2,1,0:T(8,128)(2,1)S(1)}, u32[]{:S(2)}, u32[]{:S(2)}) collective-permute-start(bf16[2,20,8,512]{3,2,1,0:T(8,128)(2,1)S(1)} %copy-done.16), channel_id=1, source_target_pairs={{0,15},{1,14},{2,13},{3,12},{4,11},{5,10},{6,9},{7,8},{8,7},{9,6},... | collective-permute-start | bytes 983048 | tf_op jit(solution)/shard_map/ppermute | solution.py:501
  110.3 0.0 collective-permute-done.9.refs_17_.refs_6_.refs_23_
  110.3 3.2 %collective-permute-start.14 = (bf16[2,20,8,512]{3,2,1,0:T(8,128)(2,1)S(1)}, bf16[2,20,8,512]{3,2,1,0:T(8,128)(2,1)S(1)}, u32[]{:S(2)}, u32[]{:S(2)}) collective-permute-start(bf16[2,20,8,512]{3,2,1,0:T(8,128)(2,1)S(1)} %copy-done.14), channel_id=1, source_target_pairs={{0,11},{1,10},{2,9},{3,8},{4,15},{5,14},{6,13},{7,12},{8,3},{9,2},... | collective-permute-start | bytes 983048 | tf_op jit(solution)/shard_map/ppermute | solution.py:501
  113.5 12.1 %prefill_more.7 = (f32[512,4096]{1,0:T(8,128)S(1)}, f32[512,4096]{1,0:T(8,128)S(1)}) custom-call(s32[1]{0:T(128)S(6)} %copy.42.refs_0_.refs_8_, s32[1,256]{1,0:T(1,128)S(1)} %copy-done.12, bf16[512,4096]{1,0:T(8,128)(2,1)S(1)} %copy-done.1, bf16[64,2,8,512]{3,2,1,0:T(8,128)(2,1)S(1)} %copy-done.3, ...), custom_call_target="tpu_custom_call", output_to_operand_aliasing={{0}: (9, {}), {1}: (10, {})} | custom-call | flops 8589934592 | bytes 524288 | tf_op jit(solution)/shard_map/prefill_more/pallas_call | solution.py:202
  125.6 0.0 collective-permute-done.11.refs_19_.refs_4_.refs_25_
  125.6 24.2 %collective-permute-done.12.refs_20_.refs_5_.refs_26_ = bf16[2,20,8,512]{3,2,1,0:T(8,128)(2,1)S(1)} collective-permute-done((bf16[2,20,8,512]{3,2,1,0:T(8,128)(2,1)S(1)}, bf16[2,20,8,512]{3,2,1,0:T(8,128)(2,1)S(1)}, u32[]{:S(2)}, u32[]{:S(2)}) %collective-permute-start.12) | collective-permute-done | bytes 327712 | tf_op jit(solution)/shard_map/ppermute | solution.py:501
  149.9 8.4 %prefill_more.8 = (f32[512,4096]{1,0:T(8,128)S(1)}, f32[512,4096]{1,0:T(8,128)S(1)}) custom-call(s32[1]{0:T(128)S(6)} %copy.42.refs_0_.refs_8_, s32[1,256]{1,0:T(1,128)S(1)} %copy-done.12, bf16[512,4096]{1,0:T(8,128)(2,1)S(1)} %copy-done.1, bf16[64,2,8,512]{3,2,1,0:T(8,128)(2,1)S(1)} %copy-done.3, ...), custom_call_target="tpu_custom_call", output_to_operand_aliasing={{0}: (7, {}), {1}: (8, {})} | custom-call | flops 4294967296 | bytes 262144 | tf_op jit(solution)/shard_map/prefill_more/pallas_call | solution.py:202
  158.3 2.7 %decode_fresh.1 = (f32[4,256,128]{2,1,0:T(8,128)S(1)}, f32[4,256,128]{2,1,0:T(8,128)S(1)}, f32[4,256,128]{2,1,0:T(8,128)S(1)}) custom-call(bf16[32,4096]{1,0:T(8,128)(2,1)S(1)} %copy-done.4, f32[4,256,128]{2,1,0:T(8,128)S(1)} %copy-done.7, f32[4,256,128]{2,1,0:T(8,128)S(1)} %copy-done.9, f32[4,256,128]{2,1,0:T(8,128)S(1)} %copy-done.10, ...), custom_call_target="tpu_custom_call" | custom-call | flops 251658240 | bytes 983040 | tf_op jit(solution)/shard_map/decode_fresh/pallas_call | solution.py:330
  161.1 8.0 %prefill_more.9 = (f32[512,4096]{1,0:T(8,128)S(1)}, f32[512,4096]{1,0:T(8,128)S(1)}) custom-call(s32[1]{0:T(128)S(6)} %copy.42.refs_0_.refs_8_, s32[1,256]{1,0:T(1,128)S(1)} %copy-done.12, bf16[512,4096]{1,0:T(8,128)(2,1)S(1)} %copy-done.1, bf16[64,2,8,512]{3,2,1,0:T(8,128)(2,1)S(1)} %copy-done.3, ...), custom_call_target="tpu_custom_call", output_to_operand_aliasing={{0}: (6, {}), {1}: (7, {})} | custom-call | flops 2147483648 | bytes 131072 | tf_op jit(solution)/shard_map/prefill_more/pallas_call | solution.py:202
  169.0 0.0 collective-permute-done.14.refs_12_.refs_28_
  169.0 8.8 %finish.1 = (bf16[32,4096]{1,0:T(8,128)(2,1)}, bf16[512,4096]{1,0:T(8,128)(2,1)}) custom-call(bf16[32,4096]{1,0:T(8,128)(2,1)S(1)} %copy-done.4, f32[4,256,128]{2,1,0:T(8,128)S(1)} %get-tuple-element.57.refs_1_, f32[4,256,128]{2,1,0:T(8,128)S(1)} %get-tuple-element.58.refs_2_, f32[4,256,128]{2,1,0:T(8,128)S(1)} %get-tuple-element.59.refs_3_, ...), custom_call_target="tpu_custom_call" | custom-call | flops 2147483648 | bytes 131072 | tf_op jit(solution)/shard_map/finish/pallas_call | solution.py:439
  (67 shorter events, 0.2 us)
Async XLA Ops:
  0.6 23.0 %copy-start.35 = (s32[15]{0:T(128)S(1)}, s32[15]{0:T(128)}, u32[]{:S(2)}) copy-start(s32[15]{0:T(128)} %constant.58.clone) | copy-start | bytes 184
  0.6 23.0 %copy-start.34 = (s32[32]{0:T(128)S(1)}, s32[32]{0:T(128)}, u32[]{:S(2)}) copy-start(s32[32]{0:T(128)} %param.21) | copy-start | bytes 388
  0.7 24.1 %copy-start.33 = (s32[32,64]{1,0:T(8,128)S(1)}, s32[32,64]{1,0:T(8,128)}, u32[]{:S(2)}) copy-start(s32[32,64]{1,0:T(8,128)} %param.20) | copy-start | bytes 24580
  3.4 76.9 %collective-permute-start.5 = (bf16[2,20,8,512]{3,2,1,0:T(8,128)(2,1)}, bf16[2,20,8,512]{3,2,1,0:T(8,128)(2,1)}, u32[]{:S(2)}, u32[]{:S(2)}) collective-permute-start(bf16[2,20,8,512]{3,2,1,0:T(8,128)(2,1)} %get-tuple-element.48), channel_id=1, source_target_pairs={{0,8},{1,9},{2,10},{3,11},{4,12},{5,13},{6,14},{7,15},{8,0},{9,1},... | collective-permute-start | bytes 983048 | tf_op jit(solution)/shard_map/ppermute | solution.py:501
  7.5 73.6 %collective-permute-start.3 = (bf16[2,20,8,512]{3,2,1,0:T(8,128)(2,1)}, bf16[2,20,8,512]{3,2,1,0:T(8,128)(2,1)}, u32[]{:S(2)}, u32[]{:S(2)}) collective-permute-start(bf16[2,20,8,512]{3,2,1,0:T(8,128)(2,1)} %get-tuple-element.42.rest_0_), channel_id=1, source_target_pairs={{0,12},{1,13},{2,14},{3,15},{4,8},{5,9},{6,10},{7,11},{8,4},{9,5},... | collective-permute-start | bytes 983048 | tf_op jit(solution)/shard_map/ppermute | solution.py:501
  13.0 0.8 copy-start.5
  13.7 0.7 copy-start.13
  14.4 0.7 copy-start.15
  15.2 0.7 copy-start.17
  15.9 0.7 copy-start.19
  16.7 0.7 copy-start.21
  17.4 0.7 copy-start.23
  18.1 0.7 copy-start.25
  18.8 0.7 copy-start.27
  19.5 0.8 copy-start.29
  20.3 0.8 copy-start.31
  21.1 41.5 %collective-permute-start = (bf16[2,20,8,512]{3,2,1,0:T(8,128)(2,1)}, bf16[2,20,8,512]{3,2,1,0:T(8,128)(2,1)}, u32[]{:S(2)}, u32[]{:S(2)}) collective-permute-start(bf16[2,20,8,512]{3,2,1,0:T(8,128)(2,1)} %get-tuple-element.44), channel_id=1, source_target_pairs={{0,1},{1,0},{2,3},{3,2},{4,5},{5,4},{6,7},{7,6},{8,9},{9,8},{10,11... | collective-permute-start | bytes 983048 | tf_op jit(solution)/shard_map/ppermute | solution.py:501
  21.1 41.9 %collective-permute-start.1 = (bf16[2,20,8,512]{3,2,1,0:T(8,128)(2,1)}, bf16[2,20,8,512]{3,2,1,0:T(8,128)(2,1)}, u32[]{:S(2)}, u32[]{:S(2)}) collective-permute-start(bf16[2,20,8,512]{3,2,1,0:T(8,128)(2,1)} %get-tuple-element.45), channel_id=1, source_target_pairs={{0,2},{1,3},{2,0},{3,1},{4,6},{5,7},{6,4},{7,5},{8,10},{9,11},{10,... | collective-permute-start | bytes 983048 | tf_op jit(solution)/shard_map/ppermute | solution.py:501
  22.6 41.7 %collective-permute-start.2 = (bf16[2,20,8,512]{3,2,1,0:T(8,128)(2,1)}, bf16[2,20,8,512]{3,2,1,0:T(8,128)(2,1)}, u32[]{:S(2)}, u32[]{:S(2)}) collective-permute-start(bf16[2,20,8,512]{3,2,1,0:T(8,128)(2,1)} %get-tuple-element.46), channel_id=1, source_target_pairs={{0,3},{1,2},{2,1},{3,0},{4,7},{5,6},{6,5},{7,4},{8,11},{9,10},{10,... | collective-permute-start | bytes 983048 | tf_op jit(solution)/shard_map/ppermute | solution.py:501
  42.2 24.7 %copy-start.12 = (s32[1,256]{1,0:T(1,128)S(1)}, s32[1,256]{1,0:T(1,128)}, u32[]{:S(2)}) copy-start(s32[1,256]{1,0:T(1,128)} %refs_7_.1) | copy-start | bytes 3076
  42.2 2.2 %copy-start = (bf16[512,4096]{1,0:T(8,128)(2,1)S(1)}, bf16[512,4096]{1,0:T(8,128)(2,1)}, u32[]{:S(2)}) copy-start(bf16[512,4096]{1,0:T(8,128)(2,1)} %refs_5_.1) | copy-start | bytes 12582916
  44.4 1.2 copy-start.2
  45.7 1.0 copy-start.8
  46.7 15.9 %copy-start.32 = (bf16[2,20,8,512]{3,2,1,0:T(8,128)(2,1)S(1)}, bf16[2,20,8,512]{3,2,1,0:T(8,128)(2,1)}, u32[]{:S(2)}) copy-start(bf16[2,20,8,512]{3,2,1,0:T(8,128)(2,1)} %copy-done.31) | copy-start | bytes 983044
  46.7 16.3 %copy-start.30 = (bf16[2,20,8,512]{3,2,1,0:T(8,128)(2,1)S(1)}, bf16[2,20,8,512]{3,2,1,0:T(8,128)(2,1)}, u32[]{:S(2)}) copy-start(bf16[2,20,8,512]{3,2,1,0:T(8,128)(2,1)} %copy-done.29) | copy-start | bytes 983044
  46.7 17.6 %copy-start.28 = (bf16[2,20,8,512]{3,2,1,0:T(8,128)(2,1)S(1)}, bf16[2,20,8,512]{3,2,1,0:T(8,128)(2,1)}, u32[]{:S(2)}) copy-start(bf16[2,20,8,512]{3,2,1,0:T(8,128)(2,1)} %copy-done.27) | copy-start | bytes 983044
  46.7 20.2 %copy-start.1 = (bf16[512,4096]{1,0:T(8,128)(2,1)S(1)}, bf16[512,4096]{1,0:T(8,128)(2,1)}, u32[]{:S(2)}) copy-start(bf16[512,4096]{1,0:T(8,128)(2,1)} %refs_5_.1) | copy-start | bytes 12582916
  46.7 20.2 %copy-start.3 = (bf16[64,2,8,512]{3,2,1,0:T(8,128)(2,1)S(1)}, bf16[64,2,8,512]{3,2,1,0:T(8,128)(2,1)}, u32[]{:S(2)}) copy-start(bf16[64,2,8,512]{3,2,1,0:T(8,128)(2,1)} %refs_6_.1) | copy-start | bytes 3145732
  46.7 20.2 %copy-start.6 = (bf16[2,20,8,512]{3,2,1,0:T(8,128)(2,1)S(1)}, bf16[2,20,8,512]{3,2,1,0:T(8,128)(2,1)}, u32[]{:S(2)}) copy-start(bf16[2,20,8,512]{3,2,1,0:T(8,128)(2,1)} %copy-done.5) | copy-start | bytes 983044
  62.6 19.9 %collective-permute-start.4 = (bf16[2,20,8,512]{3,2,1,0:T(8,128)(2,1)S(1)}, bf16[2,20,8,512]{3,2,1,0:T(8,128)(2,1)S(1)}, u32[]{:S(2)}, u32[]{:S(2)}) collective-permute-start(bf16[2,20,8,512]{3,2,1,0:T(8,128)(2,1)S(1)} %copy-done.32), channel_id=1, source_target_pairs={{0,4},{1,5},{2,6},{3,7},{4,0},{5,1},{6,2},{7,3},{8,12},{9,13},{10,... | collective-permute-start | bytes 983048 | tf_op jit(solution)/shard_map/ppermute | solution.py:501
  63.0 20.1 %collective-permute-start.6 = (bf16[2,20,8,512]{3,2,1,0:T(8,128)(2,1)S(1)}, bf16[2,20,8,512]{3,2,1,0:T(8,128)(2,1)S(1)}, u32[]{:S(2)}, u32[]{:S(2)}) collective-permute-start(bf16[2,20,8,512]{3,2,1,0:T(8,128)(2,1)S(1)} %copy-done.30), channel_id=1, source_target_pairs={{0,5},{1,4},{2,7},{3,6},{4,1},{5,0},{6,3},{7,2},{8,13},{9,12},{10,... | collective-permute-start | bytes 983048 | tf_op jit(solution)/shard_map/ppermute | solution.py:501
  64.3 35.2 %collective-permute-start.7 = (bf16[2,20,8,512]{3,2,1,0:T(8,128)(2,1)S(1)}, bf16[2,20,8,512]{3,2,1,0:T(8,128)(2,1)S(1)}, u32[]{:S(2)}, u32[]{:S(2)}) collective-permute-start(bf16[2,20,8,512]{3,2,1,0:T(8,128)(2,1)S(1)} %copy-done.28), channel_id=1, source_target_pairs={{0,13},{1,12},{2,15},{3,14},{4,9},{5,8},{6,11},{7,10},{8,5},{9,4},... | collective-permute-start | bytes 983048 | tf_op jit(solution)/shard_map/ppermute | solution.py:501
  66.9 13.4 %copy-start.26 = (bf16[2,20,8,512]{3,2,1,0:T(8,128)(2,1)S(1)}, bf16[2,20,8,512]{3,2,1,0:T(8,128)(2,1)}, u32[]{:S(2)}) copy-start(bf16[2,20,8,512]{3,2,1,0:T(8,128)(2,1)} %copy-done.25) | copy-start | bytes 983044
  66.9 14.2 %copy-start.24 = (bf16[2,20,8,512]{3,2,1,0:T(8,128)(2,1)S(1)}, bf16[2,20,8,512]{3,2,1,0:T(8,128)(2,1)}, u32[]{:S(2)}) copy-start(bf16[2,20,8,512]{3,2,1,0:T(8,128)(2,1)} %copy-done.23) | copy-start | bytes 983044
  66.9 15.6 %copy-start.22 = (bf16[2,20,8,512]{3,2,1,0:T(8,128)(2,1)S(1)}, bf16[2,20,8,512]{3,2,1,0:T(8,128)(2,1)}, u32[]{:S(2)}) copy-start(bf16[2,20,8,512]{3,2,1,0:T(8,128)(2,1)} %copy-done.21) | copy-start | bytes 983044
  66.9 16.1 %copy-start.20 = (bf16[2,20,8,512]{3,2,1,0:T(8,128)(2,1)S(1)}, bf16[2,20,8,512]{3,2,1,0:T(8,128)(2,1)}, u32[]{:S(2)}) copy-start(bf16[2,20,8,512]{3,2,1,0:T(8,128)(2,1)} %copy-done.19) | copy-start | bytes 983044
  80.3 22.5 %collective-permute-start.8 = (bf16[2,20,8,512]{3,2,1,0:T(8,128)(2,1)S(1)}, bf16[2,20,8,512]{3,2,1,0:T(8,128)(2,1)S(1)}, u32[]{:S(2)}, u32[]{:S(2)}) collective-permute-start(bf16[2,20,8,512]{3,2,1,0:T(8,128)(2,1)S(1)} %copy-done.26), channel_id=1, source_target_pairs={{0,6},{1,7},{2,4},{3,5},{4,2},{5,3},{6,0},{7,1},{8,14},{9,15},{10,... | collective-permute-start | bytes 983048 | tf_op jit(solution)/shard_map/ppermute | solution.py:501
  81.1 29.2 %collective-permute-start.9 = (bf16[2,20,8,512]{3,2,1,0:T(8,128)(2,1)S(1)}, bf16[2,20,8,512]{3,2,1,0:T(8,128)(2,1)S(1)}, u32[]{:S(2)}, u32[]{:S(2)}) collective-permute-start(bf16[2,20,8,512]{3,2,1,0:T(8,128)(2,1)S(1)} %copy-done.24), channel_id=1, source_target_pairs={{0,9},{1,8},{2,11},{3,10},{4,13},{5,12},{6,15},{7,14},{8,1},{9,0},... | collective-permute-start | bytes 983048 | tf_op jit(solution)/shard_map/ppermute | solution.py:501
  82.6 31.0 %collective-permute-start.10 = (bf16[2,20,8,512]{3,2,1,0:T(8,128)(2,1)S(1)}, bf16[2,20,8,512]{3,2,1,0:T(8,128)(2,1)S(1)}, u32[]{:S(2)}, u32[]{:S(2)}) collective-permute-start(bf16[2,20,8,512]{3,2,1,0:T(8,128)(2,1)S(1)} %copy-done.22), channel_id=1, source_target_pairs={{0,7},{1,6},{2,5},{3,4},{4,3},{5,2},{6,1},{7,0},{8,15},{9,14},{10,... | collective-permute-start | bytes 983048 | tf_op jit(solution)/shard_map/ppermute | solution.py:501
  83.1 42.5 %collective-permute-start.11 = (bf16[2,20,8,512]{3,2,1,0:T(8,128)(2,1)S(1)}, bf16[2,20,8,512]{3,2,1,0:T(8,128)(2,1)S(1)}, u32[]{:S(2)}, u32[]{:S(2)}) collective-permute-start(bf16[2,20,8,512]{3,2,1,0:T(8,128)(2,1)S(1)} %copy-done.20), channel_id=1, source_target_pairs={{0,14},{1,15},{2,12},{3,13},{4,10},{5,11},{6,8},{7,9},{8,6},{9,7},... | collective-permute-start | bytes 983048 | tf_op jit(solution)/shard_map/ppermute | solution.py:501
  86.1 13.4 %copy-start.18 = (bf16[2,20,8,512]{3,2,1,0:T(8,128)(2,1)S(1)}, bf16[2,20,8,512]{3,2,1,0:T(8,128)(2,1)}, u32[]{:S(2)}) copy-start(bf16[2,20,8,512]{3,2,1,0:T(8,128)(2,1)} %copy-done.17) | copy-start | bytes 983044
  86.1 16.7 %copy-start.16 = (bf16[2,20,8,512]{3,2,1,0:T(8,128)(2,1)S(1)}, bf16[2,20,8,512]{3,2,1,0:T(8,128)(2,1)}, u32[]{:S(2)}) copy-start(bf16[2,20,8,512]{3,2,1,0:T(8,128)(2,1)} %copy-done.15) | copy-start | bytes 983044
  86.1 24.2 %copy-start.14 = (bf16[2,20,8,512]{3,2,1,0:T(8,128)(2,1)S(1)}, bf16[2,20,8,512]{3,2,1,0:T(8,128)(2,1)}, u32[]{:S(2)}) copy-start(bf16[2,20,8,512]{3,2,1,0:T(8,128)(2,1)} %copy-done.13) | copy-start | bytes 983044
  99.5 50.3 %collective-permute-start.12 = (bf16[2,20,8,512]{3,2,1,0:T(8,128)(2,1)S(1)}, bf16[2,20,8,512]{3,2,1,0:T(8,128)(2,1)S(1)}, u32[]{:S(2)}, u32[]{:S(2)}) collective-permute-start(bf16[2,20,8,512]{3,2,1,0:T(8,128)(2,1)S(1)} %copy-done.18), channel_id=1, source_target_pairs={{0,10},{1,11},{2,8},{3,9},{4,14},{5,15},{6,12},{7,13},{8,2},{9,3},... | collective-permute-start | bytes 983048 | tf_op jit(solution)/shard_map/ppermute | solution.py:501
  102.8 55.5 %collective-permute-start.13 = (bf16[2,20,8,512]{3,2,1,0:T(8,128)(2,1)S(1)}, bf16[2,20,8,512]{3,2,1,0:T(8,128)(2,1)S(1)}, u32[]{:S(2)}, u32[]{:S(2)}) collective-permute-start(bf16[2,20,8,512]{3,2,1,0:T(8,128)(2,1)S(1)} %copy-done.16), channel_id=1, source_target_pairs={{0,15},{1,14},{2,13},{3,12},{4,11},{5,10},{6,9},{7,8},{8,7},{9,6},... | collective-permute-start | bytes 983048 | tf_op jit(solution)/shard_map/ppermute | solution.py:501
  110.3 58.7 %collective-permute-start.14 = (bf16[2,20,8,512]{3,2,1,0:T(8,128)(2,1)S(1)}, bf16[2,20,8,512]{3,2,1,0:T(8,128)(2,1)S(1)}, u32[]{:S(2)}, u32[]{:S(2)}) collective-permute-start(bf16[2,20,8,512]{3,2,1,0:T(8,128)(2,1)S(1)} %copy-done.14), channel_id=1, source_target_pairs={{0,11},{1,10},{2,9},{3,8},{4,15},{5,14},{6,13},{7,12},{8,3},{9,2},... | collective-permute-start | bytes 983048 | tf_op jit(solution)/shard_map/ppermute | solution.py:501
  149.9 8.4 %copy-start.4 = (bf16[32,4096]{1,0:T(8,128)(2,1)S(1)}, bf16[32,4096]{1,0:T(8,128)(2,1)}, u32[]{:S(2)}) copy-start(bf16[32,4096]{1,0:T(8,128)(2,1)} %refs_0_.8) | copy-start | bytes 786436
  149.9 8.4 %copy-start.7 = (f32[4,256,128]{2,1,0:T(8,128)S(1)}, f32[4,256,128]{2,1,0:T(8,128)}, u32[]{:S(2)}) copy-start(f32[4,256,128]{2,1,0:T(8,128)} %get-tuple-element.39.refs_1_) | copy-start | bytes 1572868
  149.9 8.4 %copy-start.9 = (f32[4,256,128]{2,1,0:T(8,128)S(1)}, f32[4,256,128]{2,1,0:T(8,128)}, u32[]{:S(2)}) copy-start(f32[4,256,128]{2,1,0:T(8,128)} %get-tuple-element.40.refs_2_._) | copy-start | bytes 1572868
  149.9 8.4 %copy-start.10 = (f32[4,256,128]{2,1,0:T(8,128)S(1)}, f32[4,256,128]{2,1,0:T(8,128)}, u32[]{:S(2)}) copy-start(f32[4,256,128]{2,1,0:T(8,128)} %get-tuple-element.41.refs_3_) | copy-start | bytes 1572868
  149.9 8.4 %copy-start.11 = (s32[32,1]{1,0:T(8,128)S(1)}, s32[32,1]{1,0:T(8,128)}, u32[]{:S(2)}) copy-start(s32[32,1]{1,0:T(8,128)} %copy.28.rest_ref.refs_6_) | copy-start | bytes 388
where the time goes:
time: 179 us; the launch traced here: 178 us
  Pallas kernels  103 us (58%)
  starting transfers between devices  29.4 us (16%)
  waiting for transfers between devices  26.3 us (15%)
  local copies, waits for them, and re-layouts  13.8 us (8%)
  other arithmetic  3.66 us (2%)
  between operations  1.82 us (1%)
    pallas_call x5, Pallas kernels, prefill_more(): pl.pallas_call(body, out_shape=[wide, wide], in_specs=[SM, VM, VM, VM] +...  55.1 us
    ppermute x15, starting transfers between devices, shards(): arrived[k] = lax.ppermute(outgoing[k], 'pool', pairs)  29.4 us
    ppermute x15, waiting for transfers between devices, shards(): arrived[k] = lax.ppermute(outgoing[k], 'pool', pairs)  26.3 us
    pallas_call x1, Pallas kernels, prefill_first(): pl.pallas_call(body, out_shape=[pltpu.VMEM((tokens, qwidth), jnp.bfloat16...  15.8 us
    pallas_call x1, Pallas kernels, decode_pool(): pl.pallas_call(body, grid=(steps,), out_shape=[jax.ShapeDtypeStruct(shape...  13.8 us
    unnamed x72, local copies, waits for them, and re-layouts  12.6 us
    pallas_call x1, Pallas kernels, finish(): pl.pallas_call(body, out_shape=[jax.ShapeDtypeStruct(dec_q.shape, dec_q.d...  8.83 us
    pallas_call x2, Pallas kernels, gather_pages(): pl.pallas_call(body, out_shape=[pltpu.VMEM(shape, kv_pool.dtype)] * n, in...  6.8 us
  transfers between devices with their start and end apart: 15, of which 2 were waited for; matrix products, arithmetic and copies ran while one was open for 3% of the time, Pallas kernels for 51%

commit v1 on v0

--- a/solution.py
+++ b/solution.py
@@ -16,8 +16,6 @@
 VMEM_LIMIT = 16 << 20
 POOL_LIMIT = 56 << 20
 
-
-HP_FIRST = 4
 
 NT = (((1,), (1,)), ((), ()))
 VM = pl.BlockSpec(memory_space=pltpu.VMEM)
@@ -104,33 +102,33 @@
 
     def body(q_ref, f_ref, _, m_ref, acc_ref, l_ref, k_ref, v_ref):
         v_ref[:, HD:] = jnp.ones((tokens, HD), jnp.bfloat16)
-        lane = lax.broadcasted_iota(jnp.int32, (rows, HD), 1)
+        k_lane = lax.broadcasted_iota(jnp.int32, (tokens, HD), 1)
+        k_ref[:, HD:] = jnp.where(k_lane == 0, -1.0, 0.0).astype(jnp.bfloat16)
         row = lax.broadcasted_iota(jnp.int32, (rows, rows), 0)
         col = lax.broadcasted_iota(jnp.int32, (rows, rows), 1)
 
         def group(g, carry):
-            k_ref[...] = f_ref[:, 0, :, head_at(g)].reshape(tokens, HD)
+            key = f_ref[:, 0, :, head_at(g)].reshape(tokens, HD)
+            k_ref[:, 0:HD] = key
             v_ref[:, 0:HD] = f_ref[:, 1, :, head_at(g)].reshape(tokens, HD)
-
-            def heads(b, carry):
-                for h in range(HP_FIRST):
-                    cols = head_at(g * GROUP + b * HP_FIRST + h)
-                    for r in range(0, tokens, rows):
-                        rs = slice(r, r + rows)
-                        s = lax.dot_general(
-                            q_ref[rs, cols], k_ref[0 : r + rows, :], NT, preferred_element_type=jnp.float32
-                        )
-                        diag = jnp.where(col <= row, s[:, r:], NEG)
-                        s = jnp.concatenate([s[:, :r], diag], 1) if r else diag
-                        m = jnp.max(s, axis=1, keepdims=True).astype(jnp.bfloat16).astype(jnp.float32)
-                        p = jnp.exp2((s - m) * CEXP).astype(jnp.bfloat16)
-                        new = jnp.dot(p, v_ref[0 : r + rows, :], preferred_element_type=jnp.float32)
-                        acc_ref[rs, cols] = new[:, :HD]
-                        l_ref[rs, cols] = new[:, HD:]
-                        m_ref[rs, cols] = jnp.where(lane == 0, m, 0.0).astype(jnp.bfloat16)
-                return carry
-
-            return lax.fori_loop(0, GROUP // HP_FIRST, heads, carry)
+            key = key.astype(jnp.float32)
+            for h in range(GROUP):
+                cols = head_at(g * GROUP + h)
+                own = jnp.sum(q_ref[:, cols].astype(jnp.float32) * key, axis=1, keepdims=True)
+                m_ref[:, cols] = jnp.where(k_lane == 0, own, 0.0).astype(jnp.bfloat16)
+            for h in range(GROUP):
+                cols = head_at(g * GROUP + h)
+                for r in range(0, tokens, rows):
+                    rs = slice(r, r + rows)
+                    lhs = jnp.concatenate([q_ref[rs, cols], m_ref[rs, cols]], 1)
+                    s = lax.dot_general(lhs, k_ref[0 : r + rows, :], NT, preferred_element_type=jnp.float32)
+                    diag = jnp.where(col <= row, s[:, r:], NEG)
+                    s = jnp.concatenate([s[:, :r], diag], 1) if r else diag
+                    p = jnp.exp2(s * CEXP).astype(jnp.bfloat16)
+                    new = jnp.dot(p, v_ref[0 : r + rows, :], preferred_element_type=jnp.float32)
+                    acc_ref[rs, cols] = new[:, :HD]
+                    l_ref[rs, cols] = new[:, HD:]
+            return carry
 
         lax.fori_loop(0, width // HD, group, 0)
 
@@ -139,10 +137,10 @@
     return pl.pallas_call(
         body,
         out_shape=[pltpu.VMEM((tokens, qwidth), jnp.bfloat16), wide, wide],
-        in_specs=[VM, VM, ANY],
+        in_specs=[VM, VM, SM],
         out_specs=[VM] * 3,
         scratch_shapes=[
-            pltpu.VMEM((tokens, HD), jnp.bfloat16),
+            pltpu.VMEM((tokens, 2 * HD), jnp.bfloat16),
             pltpu.VMEM((tokens, 2 * HD), jnp.bfloat16),
         ],
         compiler_params=PARAMS,
@@ -254,7 +252,9 @@
     block = 128 if slots % 128 == 0 else slots
     steps = slots // block
 
-    def body(q_ref, kv_ref, full_ref, part_ref, rest_ref, acc_ref, m_ref, l_ref):
+    def body(q_ref, kv_ref, full_ref, part_ref, rest_ref, acc_ref, m_ref, l_ref, token_ref):
+        token_ref[0] = 0
+
         @pl.when(pl.program_id(0) == 0)
         def _():
             acc_ref[...] = jnp.zeros_like(acc_ref)
@@ -278,7 +278,7 @@
     return pl.pallas_call(
         body,
         grid=(steps,),
-        out_shape=[jax.ShapeDtypeStruct(shape, jnp.float32)] * 3,
+        out_shape=[jax.ShapeDtypeStruct(shape, jnp.float32)] * 3 + [jax.ShapeDtypeStruct((1,), jnp.int32)],
         in_specs=[
             pl.BlockSpec(dec_q.shape, lambda i: (0, 0)),
             pl.BlockSpec((block, 2, page, width), lambda i: (i, 0, 0, 0)),
@@ -286,7 +286,7 @@
             pl.BlockSpec((requests, block), lambda i: (0, i)),
             pl.BlockSpec(rest.shape, lambda i: (0, 0)),
         ],
-        out_specs=[whole] * 3,
+        out_specs=[whole] * 3 + [SM],
         compiler_params=pltpu.CompilerParams(vmem_limit_bytes=POOL_LIMIT),
         cost_estimate=pl.CostEstimate(
             flops=4 * HD * heads_kv * GROUP * requests * slots * page,
@@ -376,7 +376,7 @@
 
             def emit(cols, acc, total):
                 total = l_ref[:, cols] + total
-                out_ref[:, cols] = ((acc_ref[:, cols] + acc) / total).astype(out_ref.dtype)
+                out_ref[:, cols] = ((acc_ref[:, cols] + acc) * pl.reciprocal(total)).astype(out_ref.dtype)
                 partial.append(jnp.sum(total.reshape(-1, 8, HD), axis=0))
 
             add_pages(k_ref, v_ref, q_ref, m_ref, g, emit)
@@ -526,8 +526,8 @@
     last_seen = position[:, :, None] * page + last_token < dec_len[:, None, None]
     last_times = jnp.sum(((dec_pages[:, :, None] == last_names) & last_seen).astype(jnp.float32), 1)
 
-    dec_state = decode_pool(dec_q, kv_pool, *counts(jnp.arange(slots, dtype=jnp.int32)), rest)
-    state = prefill_first(suffix_q, fresh_kv, dec_state[1])
+    *dec_state, token = decode_pool(dec_q, kv_pool, *counts(jnp.arange(slots, dtype=jnp.int32)), rest)
+    state = prefill_first(suffix_q, fresh_kv, token)
     for ks in groups[:-1]:
         new = prefill_more(
             suffix_q, fresh_kv, [arrived[k] for k in ks], ks, prefix_pages, prefix_len, state, cap, size
@@ -557,7 +557,7 @@
 def arrival_groups(order):
     size = len(order)
     if size == 16:
-        return [[0, 1, 2, 3], [12, 4, 8, 5], [13, 6, 9, 7], [14, 10], [15], [11]]
+        return [[0, 1, 2, 3], [12, 4, 8, 5], [13, 6, 9, 7], [14, 10], [15, 11]]
     per = -(-size // 4)
     return [order[i : min(i + per, size - 1)] for i in range(0, size - 1, per)] + [order[-1:]]
 

time: 179 us -> 172 us (0.961)
  Pallas kernels: 103 us -> 94.2 us
  starting transfers between devices: 29.4 us -> 31.4 us
    pallas_call x5 -> x4, Pallas kernels: 55.1 us -> 47.1 us  [prefill_more(): pl.pallas_call(body, out_shape=[wide, wide], in_specs=[SM, VM, VM, VM] +...]
    ppermute x15, starting transfers between devices: 29.4 us -> 31.4 us  [shards(): arrived[k] = lax.ppermute(outgoing[k], 'pool', pairs)]
  transfers between devices with their start and end apart: 15 -> 15, of which waited for: 2 -> 2; matrix products, arithmetic and copies ran while one was open for 3% -> 3% of each run, Pallas kernels for 51% -> 48%
where the time goes in v1:
time: 172 us; the launch traced here: 171 us
  Pallas kernels  94.2 us (55%)
  starting transfers between devices  31.4 us (18%)
  waiting for transfers between devices  27.1 us (16%)
  local copies, waits for them, and re-layouts  12.6 us (7%)
  other arithmetic  3.85 us (2%)
  between operations  1.82 us (1%)
    pallas_call x4, Pallas kernels, prefill_more(): pl.pallas_call(body, out_shape=[wide, wide], in_specs=[SM, VM, VM, VM] +...  47.1 us
    ppermute x15, starting transfers between devices, shards(): arrived[k] = lax.ppermute(outgoing[k], 'pool', pairs)  31.4 us
    ppermute x15, waiting for transfers between devices, shards(): arrived[k] = lax.ppermute(outgoing[k], 'pool', pairs)  27.1 us
    pallas_call x1, Pallas kernels, prefill_first(): pl.pallas_call(body, out_shape=[pltpu.VMEM((tokens, qwidth), jnp.bfloat16...  14.4 us
    pallas_call x1, Pallas kernels, decode_pool(): pl.pallas_call(body, grid=(steps,), out_shape=[jax.ShapeDtypeStruct(shape...  13.9 us
    unnamed x72, local copies, waits for them, and re-layouts  11.6 us
    pallas_call x1, Pallas kernels, finish(): pl.pallas_call(body, out_shape=[jax.ShapeDtypeStruct(dec_q.shape, dec_q.d...  9.25 us
    pallas_call x2, Pallas kernels, gather_pages(): pl.pallas_call(body, out_shape=[pltpu.VMEM(shape, kv_pool.dtype)] * n, in...  6.8 us
  transfers between devices with their start and end apart: 15, of which 2 were waited for; matrix products, arithmetic and copies ran while one was open for 3% of the time, Pallas kernels for 48%

profile of v1, /device:TPU:0, one launch (start us, length us, event | category | flops | bytes accessed | tf_op | source)
XLA Modules:
  0.0 171.0 jit_solution(17424291698396668396)
XLA Ops:
  0.6 0.0 copy-start.35
  0.6 0.0 copy-start.34
  0.7 2.7 %gather_pages.2 = (bf16[2,20,8,512]{3,2,1,0:T(8,128)(2,1)}, bf16[2,20,8,512]{3,2,1,0:T(8,128)(2,1)}) custom-call(s32[1,256]{1,0:T(1,128)} %slots_ref.3, s32[1,64]{1,0:T(1,128)} %routes_ref.3, bf16[512,2,8,512]{3,2,1,0:T(8,128)(2,1)} %pool_ref.3, bf16[64,2,8,512]{3,2,1,0:T(8,128)(2,1)} %refs_6_.1), custom_call_target="tpu_custom_call" | custom-call | bytes 1310720 | tf_op jit(solution)/shard_map/gather_pages/pallas_call | solution.py:63
  3.4 4.1 %collective-permute-start.5 = (bf16[2,20,8,512]{3,2,1,0:T(8,128)(2,1)}, bf16[2,20,8,512]{3,2,1,0:T(8,128)(2,1)}, u32[]{:S(2)}, u32[]{:S(2)}) collective-permute-start(bf16[2,20,8,512]{3,2,1,0:T(8,128)(2,1)} %get-tuple-element.47), channel_id=1, source_target_pairs={{0,8},{1,9},{2,10},{3,11},{4,12},{5,13},{6,14},{7,15},{8,0},{9,1},... | collective-permute-start | bytes 983048 | tf_op jit(solution)/shard_map/ppermute | solution.py:501
  7.5 1.3 collective-permute-start.3
  8.9 4.1 %gather_pages.3 = (bf16[2,20,8,512]{3,2,1,0:T(8,128)(2,1)}, bf16[2,20,8,512]{3,2,1,0:T(8,128)(2,1)}, bf16[2,20,8,512]{3,2,1,0:T(8,128)(2,1)}, bf16[2,20,8,512]{3...) custom-call(s32[1,256]{1,0:T(1,128)} %slots_ref.3, ...), custom_call_target="tpu_custom_call" | custom-call | bytes 9175040 | tf_op jit(solution)/shard_map/gather_pages/pallas_call | solution.py:63
  13.0 0.7 copy-done.5
  13.7 0.7 copy-done.12
  14.5 0.7 copy-done.14
  15.2 0.7 copy-done.16
  15.9 0.7 copy-done.18
  16.7 0.7 copy-done.20
  17.4 0.7 copy-done.22
  18.1 0.7 copy-done.24
  18.8 0.7 copy-done.26
  19.6 0.8 copy-done.28
  20.3 0.8 copy-done.30
  21.1 0.0 collective-permute-start
  21.1 1.5 collective-permute-start.1
  22.6 0.4 collective-permute-start.2
  23.7 0.1 iota_add_fusion.1
  23.7 0.1 add.89
  23.8 0.1 broadcast_in_dim.17
  23.9 0.1 eq.72
  24.0 0.1 iota_add_fusion
  24.1 0.1 add.86
  24.1 0.7 copy.26.rest_ref.refs_6_
  24.8 0.1 iota_compare_fusion.1
  24.9 2.4 %convert_reduce_fusion = (bf16[32,512]{1,0:T(8,128)(2,1)}, bf16[32,512]{1,0:T(8,128)(2,1)}) fusion(s32[32,64]{1,0:T(8,128)S(1)} %copy-done.32, pred[32,64]{1,0:T(8,128)(4,1)S(1)} %get-tuple-element.80, pred[32,64]{1,0:T(8,128)(4,1)S(1)} %get-tuple-element.81), kind=kLoop, calls=%fused_computation | loop fusion | flops 7307264 | bytes 77824 | tf_op jit(solution)/shard_map/reduce_sum | solution.py:512
  27.3 0.6 convert_reduce_fusion.3
  28.0 0.1 broadcast_add_fusion
  28.0 0.5 convert_reduce_fusion.2.refs_4_
  28.5 13.9 %decode_pool.1 = (f32[4,256,128]{2,1,0:T(8,128)}, f32[4,256,128]{2,1,0:T(8,128)}, f32[4,256,128]{2,1,0:T(8,128)}, s32[1]{0:T(128)}) custom-call(bf16[32,4096]{1,0:T(8,128)(2,1)} %refs_0_.7, bf16[512,2,8,512]{3,2,1,0:T(8,128)(2,1)} %pool_ref.3, bf16[32,512]{1,0:T(8,128)(2,1)} %get-tuple-element.77.full_ref, bf16[32,512]{1,0:T(8,128)(2,1)} %get-tuple-element.76.part_ref, ...), custom_call_target="tpu_custom_call" | custom-call | flops 2147483648 | bytes 8388608 | tf_op jit(solution)/shard_map/decode_pool/pallas_call | solution.py:278
  42.4 0.0 copy-start.11
  42.4 0.0 copy-start
  42.4 2.2 %copy-done = bf16[512,4096]{1,0:T(8,128)(2,1)S(1)} copy-done((bf16[512,4096]{1,0:T(8,128)(2,1)S(1)}, bf16[512,4096]{1,0:T(8,128)(2,1)}, u32[]{:S(2)}) %copy-start) | copy-done | bytes 4194328
  44.6 1.2 copy-done.2
  45.9 14.4 %prefill_first.1 = (bf16[512,4096]{1,0:T(8,128)(2,1)S(1)}, f32[512,4096]{1,0:T(8,128)S(1)}, f32[512,4096]{1,0:T(8,128)S(1)}) custom-call(bf16[512,4096]{1,0:T(8,128)(2,1)S(1)} %copy-done, bf16[64,2,8,512]{3,2,1,0:T(8,128)(2,1)S(1)} %copy-done.2, s32[1]{0:T(128)} %get-tuple-element.58._), custom_call_target="tpu_custom_call" | custom-call | flops 4294967296 | bytes 262144 | tf_op jit(solution)/shard_map/prefill_first/pallas_call | solution.py:137
  60.2 0.0 collective-permute-done.refs_8_.refs_5_.refs_15_
  60.3 0.4 collective-permute-start.4
  60.6 0.0 collective-permute-done.1.refs_9_.refs_6_.refs_16_
  60.6 1.3 collective-permute-start.6
  62.0 0.0 collective-permute-done.2.refs_10_.refs_7_.refs_17_
  62.0 2.6 %collective-permute-start.7 = (bf16[2,20,8,512]{3,2,1,0:T(8,128)(2,1)S(1)}, bf16[2,20,8,512]{3,2,1,0:T(8,128)(2,1)S(1)}, u32[]{:S(2)}, u32[]{:S(2)}) collective-permute-start(bf16[2,20,8,512]{3,2,1,0:T(8,128)(2,1)S(1)} %copy-done.27), channel_id=1, source_target_pairs={{0,13},{1,12},{2,15},{3,14},{4,9},{5,8},{6,11},{7,10},{8,5},{9,4},... | collective-permute-start | bytes 983048 | tf_op jit(solution)/shard_map/ppermute | solution.py:501
  64.6 13.3 %prefill_more.4 = (f32[512,4096]{1,0:T(8,128)S(1)}, f32[512,4096]{1,0:T(8,128)S(1)}) custom-call(s32[1]{0:T(128)S(6)} %copy.36.refs_0_.refs_8_, s32[1,256]{1,0:T(1,128)S(1)} %copy-done.11, bf16[512,4096]{1,0:T(8,128)(2,1)S(1)} %copy-done.1, bf16[64,2,8,512]{3,2,1,0:T(8,128)(2,1)S(1)} %copy-done.3, ...), custom_call_target="tpu_custom_call", output_to_operand_aliasing={{0}: (9, {}), {1}: (10, {})} | custom-call | flops 8589934592 | bytes 524288 | tf_op jit(solution)/shard_map/prefill_more/pallas_call | solution.py:200
  78.0 0.8 collective-permute-start.8
  78.7 0.0 collective-permute-done.3.refs_11_.refs_4_.refs_18_
  78.7 1.5 collective-permute-start.9
  80.2 0.0 collective-permute-done.4.refs_12_.refs_5_.refs_19_
  80.2 0.5 collective-permute-start.10
  80.7 0.0 collective-permute-done.6.refs_14_.refs_7_.refs_21_
  80.7 3.1 %collective-permute-start.11 = (bf16[2,20,8,512]{3,2,1,0:T(8,128)(2,1)S(1)}, bf16[2,20,8,512]{3,2,1,0:T(8,128)(2,1)S(1)}, u32[]{:S(2)}, u32[]{:S(2)}) collective-permute-start(bf16[2,20,8,512]{3,2,1,0:T(8,128)(2,1)S(1)} %copy-done.19), channel_id=1, source_target_pairs={{0,14},{1,15},{2,12},{3,13},{4,10},{5,11},{6,8},{7,9},{8,6},{9,7},... | collective-permute-start | bytes 983048 | tf_op jit(solution)/shard_map/ppermute | solution.py:501
  83.8 13.4 %prefill_more.5 = (f32[512,4096]{1,0:T(8,128)S(1)}, f32[512,4096]{1,0:T(8,128)S(1)}) custom-call(s32[1]{0:T(128)S(6)} %copy.36.refs_0_.refs_8_, s32[1,256]{1,0:T(1,128)S(1)} %copy-done.11, bf16[512,4096]{1,0:T(8,128)(2,1)S(1)} %copy-done.1, bf16[64,2,8,512]{3,2,1,0:T(8,128)(2,1)S(1)} %copy-done.3, ...), custom_call_target="tpu_custom_call", output_to_operand_aliasing={{0}: (9, {}), {1}: (10, {})} | custom-call | flops 8589934592 | bytes 524288 | tf_op jit(solution)/shard_map/prefill_more/pallas_call | solution.py:200
  97.1 8.6 %collective-permute-start.12 = (bf16[2,20,8,512]{3,2,1,0:T(8,128)(2,1)S(1)}, bf16[2,20,8,512]{3,2,1,0:T(8,128)(2,1)S(1)}, u32[]{:S(2)}, u32[]{:S(2)}) collective-permute-start(bf16[2,20,8,512]{3,2,1,0:T(8,128)(2,1)S(1)} %copy-done.17), channel_id=1, source_target_pairs={{0,10},{1,11},{2,8},{3,9},{4,14},{5,15},{6,12},{7,13},{8,2},{9,3},... | collective-permute-start | bytes 983048 | tf_op jit(solution)/shard_map/ppermute | solution.py:501
  105.7 2.2 %collective-permute-start.13 = (bf16[2,20,8,512]{3,2,1,0:T(8,128)(2,1)S(1)}, bf16[2,20,8,512]{3,2,1,0:T(8,128)(2,1)S(1)}, u32[]{:S(2)}, u32[]{:S(2)}) collective-permute-start(bf16[2,20,8,512]{3,2,1,0:T(8,128)(2,1)S(1)} %copy-done.15), channel_id=1, source_target_pairs={{0,15},{1,14},{2,13},{3,12},{4,11},{5,10},{6,9},{7,8},{8,7},{9,6},... | collective-permute-start | bytes 983048 | tf_op jit(solution)/shard_map/ppermute | solution.py:501
  108.0 3.2 %collective-permute-start.14 = (bf16[2,20,8,512]{3,2,1,0:T(8,128)(2,1)S(1)}, bf16[2,20,8,512]{3,2,1,0:T(8,128)(2,1)S(1)}, u32[]{:S(2)}, u32[]{:S(2)}) collective-permute-start(bf16[2,20,8,512]{3,2,1,0:T(8,128)(2,1)S(1)} %copy-done.13), channel_id=1, source_target_pairs={{0,11},{1,10},{2,9},{3,8},{4,15},{5,14},{6,13},{7,12},{8,3},{9,2},... | collective-permute-start | bytes 983048 | tf_op jit(solution)/shard_map/ppermute | solution.py:501
  111.2 0.0 collective-permute-done.10.refs_18_.refs_7_.refs_25_
  111.3 12.1 %prefill_more.6 = (f32[512,4096]{1,0:T(8,128)S(1)}, f32[512,4096]{1,0:T(8,128)S(1)}) custom-call(s32[1]{0:T(128)S(6)} %copy.36.refs_0_.refs_8_, s32[1,256]{1,0:T(1,128)S(1)} %copy-done.11, bf16[512,4096]{1,0:T(8,128)(2,1)S(1)} %copy-done.1, bf16[64,2,8,512]{3,2,1,0:T(8,128)(2,1)S(1)} %copy-done.3, ...), custom_call_target="tpu_custom_call", output_to_operand_aliasing={{0}: (9, {}), {1}: (10, {})} | custom-call | flops 8589934592 | bytes 524288 | tf_op jit(solution)/shard_map/prefill_more/pallas_call | solution.py:200
  123.3 24.2 %collective-permute-done.12.refs_20_.refs_5_.refs_27_ = bf16[2,20,8,512]{3,2,1,0:T(8,128)(2,1)S(1)} collective-permute-done((bf16[2,20,8,512]{3,2,1,0:T(8,128)(2,1)S(1)}, bf16[2,20,8,512]{3,2,1,0:T(8,128)(2,1)S(1)}, u32[]{:S(2)}, u32[]{:S(2)}) %collective-permute-start.12) | collective-permute-done | bytes 327712 | tf_op jit(solution)/shard_map/ppermute | solution.py:501
  147.6 2.7 %decode_fresh.1 = (f32[4,256,128]{2,1,0:T(8,128)S(1)}, f32[4,256,128]{2,1,0:T(8,128)S(1)}, f32[4,256,128]{2,1,0:T(8,128)S(1)}) custom-call(bf16[32,4096]{1,0:T(8,128)(2,1)S(1)} %copy-done.4, f32[4,256,128]{2,1,0:T(8,128)S(1)} %copy-done.7, f32[4,256,128]{2,1,0:T(8,128)S(1)} %copy-done.8, f32[4,256,128]{2,1,0:T(8,128)S(1)} %copy-done.9, ...), custom_call_target="tpu_custom_call" | custom-call | flops 234881024 | bytes 917504 | tf_op jit(solution)/shard_map/decode_fresh/pallas_call | solution.py:330
  150.3 8.4 %prefill_more.7 = (f32[512,4096]{1,0:T(8,128)S(1)}, f32[512,4096]{1,0:T(8,128)S(1)}) custom-call(s32[1]{0:T(128)S(6)} %copy.36.refs_0_.refs_8_, s32[1,256]{1,0:T(1,128)S(1)} %copy-done.11, bf16[512,4096]{1,0:T(8,128)(2,1)S(1)} %copy-done.1, bf16[64,2,8,512]{3,2,1,0:T(8,128)(2,1)S(1)} %copy-done.3, ...), custom_call_target="tpu_custom_call", output_to_operand_aliasing={{0}: (7, {}), {1}: (8, {})} | custom-call | flops 4294967296 | bytes 262144 | tf_op jit(solution)/shard_map/prefill_more/pallas_call | solution.py:200
  158.7 0.0 collective-permute-done.13.refs_12_.refs_28_
  158.7 2.9 %collective-permute-done.14.refs_13_.refs_29_ = bf16[2,20,8,512]{3,2,1,0:T(8,128)(2,1)S(1)} collective-permute-done((bf16[2,20,8,512]{3,2,1,0:T(8,128)(2,1)S(1)}, bf16[2,20,8,512]{3,2,1,0:T(8,128)(2,1)S(1)}, u32[]{:S(2)}, u32[]{:S(2)}) %collective-permute-start.14) | collective-permute-done | bytes 327712 | tf_op jit(solution)/shard_map/ppermute | solution.py:501
  161.6 9.3 %finish.1 = (bf16[32,4096]{1,0:T(8,128)(2,1)}, bf16[512,4096]{1,0:T(8,128)(2,1)}) custom-call(bf16[32,4096]{1,0:T(8,128)(2,1)S(1)} %copy-done.4, f32[4,256,128]{2,1,0:T(8,128)S(1)} %get-tuple-element.55.refs_1_, f32[4,256,128]{2,1,0:T(8,128)S(1)} %get-tuple-element.56.refs_2_, f32[4,256,128]{2,1,0:T(8,128)S(1)} %get-tuple-element.57.refs_3_, ...), custom_call_target="tpu_custom_call" | custom-call | flops 4294967296 | bytes 262144 | tf_op jit(solution)/shard_map/finish/pallas_call | solution.py:439
  (65 shorter events, 0.2 us)
Async XLA Ops:
  0.6 23.0 %copy-start.35 = (s32[2]{0:T(128)S(1)}, s32[2]{0:T(128)}, u32[]{:S(2)}) copy-start(s32[2]{0:T(128)} %constant.56.clone) | copy-start | bytes 28
  0.6 23.0 %copy-start.34 = (s32[14]{0:T(128)S(1)}, s32[14]{0:T(128)}, u32[]{:S(2)}) copy-start(s32[14]{0:T(128)} %constant.57.clone) | copy-start | bytes 172
  0.7 23.2 %copy-start.33 = (s32[32]{0:T(128)S(1)}, s32[32]{0:T(128)}, u32[]{:S(2)}) copy-start(s32[32]{0:T(128)} %param.21) | copy-start | bytes 388
  0.7 24.2 %copy-start.32 = (s32[32,64]{1,0:T(8,128)S(1)}, s32[32,64]{1,0:T(8,128)}, u32[]{:S(2)}) copy-start(s32[32,64]{1,0:T(8,128)} %param.20) | copy-start | bytes 24580
  3.4 74.5 %collective-permute-start.5 = (bf16[2,20,8,512]{3,2,1,0:T(8,128)(2,1)}, bf16[2,20,8,512]{3,2,1,0:T(8,128)(2,1)}, u32[]{:S(2)}, u32[]{:S(2)}) collective-permute-start(bf16[2,20,8,512]{3,2,1,0:T(8,128)(2,1)} %get-tuple-element.47), channel_id=1, source_target_pairs={{0,8},{1,9},{2,10},{3,11},{4,12},{5,13},{6,14},{7,15},{8,0},{9,1},... | collective-permute-start | bytes 983048 | tf_op jit(solution)/shard_map/ppermute | solution.py:501
  7.5 71.2 %collective-permute-start.3 = (bf16[2,20,8,512]{3,2,1,0:T(8,128)(2,1)}, bf16[2,20,8,512]{3,2,1,0:T(8,128)(2,1)}, u32[]{:S(2)}, u32[]{:S(2)}) collective-permute-start(bf16[2,20,8,512]{3,2,1,0:T(8,128)(2,1)} %get-tuple-element.41.rest_0_), channel_id=1, source_target_pairs={{0,12},{1,13},{2,14},{3,15},{4,8},{5,9},{6,10},{7,11},{8,4},{9,5},... | collective-permute-start | bytes 983048 | tf_op jit(solution)/shard_map/ppermute | solution.py:501
  13.0 0.8 copy-start.5
  13.7 0.7 copy-start.12
  14.5 0.7 copy-start.14
  15.2 0.7 copy-start.16
  15.9 0.7 copy-start.18
  16.7 0.7 copy-start.20
  17.4 0.7 copy-start.22
  18.1 0.7 copy-start.24
  18.8 0.7 copy-start.26
  19.6 0.8 copy-start.28
  20.3 0.8 copy-start.30
  21.1 39.2 %collective-permute-start = (bf16[2,20,8,512]{3,2,1,0:T(8,128)(2,1)}, bf16[2,20,8,512]{3,2,1,0:T(8,128)(2,1)}, u32[]{:S(2)}, u32[]{:S(2)}) collective-permute-start(bf16[2,20,8,512]{3,2,1,0:T(8,128)(2,1)} %get-tuple-element.43), channel_id=1, source_target_pairs={{0,1},{1,0},{2,3},{3,2},{4,5},{5,4},{6,7},{7,6},{8,9},{9,8},{10,11... | collective-permute-start | bytes 983048 | tf_op jit(solution)/shard_map/ppermute | solution.py:501
  21.1 39.5 %collective-permute-start.1 = (bf16[2,20,8,512]{3,2,1,0:T(8,128)(2,1)}, bf16[2,20,8,512]{3,2,1,0:T(8,128)(2,1)}, u32[]{:S(2)}, u32[]{:S(2)}) collective-permute-start(bf16[2,20,8,512]{3,2,1,0:T(8,128)(2,1)} %get-tuple-element.44), channel_id=1, source_target_pairs={{0,2},{1,3},{2,0},{3,1},{4,6},{5,7},{6,4},{7,5},{8,10},{9,11},{10,... | collective-permute-start | bytes 983048 | tf_op jit(solution)/shard_map/ppermute | solution.py:501
  22.6 39.4 %collective-permute-start.2 = (bf16[2,20,8,512]{3,2,1,0:T(8,128)(2,1)}, bf16[2,20,8,512]{3,2,1,0:T(8,128)(2,1)}, u32[]{:S(2)}, u32[]{:S(2)}) collective-permute-start(bf16[2,20,8,512]{3,2,1,0:T(8,128)(2,1)} %get-tuple-element.45), channel_id=1, source_target_pairs={{0,3},{1,2},{2,1},{3,0},{4,7},{5,6},{6,5},{7,4},{8,11},{9,10},{10,... | collective-permute-start | bytes 983048 | tf_op jit(solution)/shard_map/ppermute | solution.py:501
  42.4 22.1 %copy-start.11 = (s32[1,256]{1,0:T(1,128)S(1)}, s32[1,256]{1,0:T(1,128)}, u32[]{:S(2)}) copy-start(s32[1,256]{1,0:T(1,128)} %refs_7_.1) | copy-start | bytes 3076
  42.4 2.2 %copy-start = (bf16[512,4096]{1,0:T(8,128)(2,1)S(1)}, bf16[512,4096]{1,0:T(8,128)(2,1)}, u32[]{:S(2)}) copy-start(bf16[512,4096]{1,0:T(8,128)(2,1)} %refs_5_.1) | copy-start | bytes 12582916
  44.6 1.2 copy-start.2
  45.8 14.4 %copy-start.31 = (bf16[2,20,8,512]{3,2,1,0:T(8,128)(2,1)S(1)}, bf16[2,20,8,512]{3,2,1,0:T(8,128)(2,1)}, u32[]{:S(2)}) copy-start(bf16[2,20,8,512]{3,2,1,0:T(8,128)(2,1)} %copy-done.30) | copy-start | bytes 983044
  45.8 14.8 %copy-start.29 = (bf16[2,20,8,512]{3,2,1,0:T(8,128)(2,1)S(1)}, bf16[2,20,8,512]{3,2,1,0:T(8,128)(2,1)}, u32[]{:S(2)}) copy-start(bf16[2,20,8,512]{3,2,1,0:T(8,128)(2,1)} %copy-done.28) | copy-start | bytes 983044
  45.8 16.1 %copy-start.27 = (bf16[2,20,8,512]{3,2,1,0:T(8,128)(2,1)S(1)}, bf16[2,20,8,512]{3,2,1,0:T(8,128)(2,1)}, u32[]{:S(2)}) copy-start(bf16[2,20,8,512]{3,2,1,0:T(8,128)(2,1)} %copy-done.26) | copy-start | bytes 983044
  45.8 18.7 %copy-start.1 = (bf16[512,4096]{1,0:T(8,128)(2,1)S(1)}, bf16[512,4096]{1,0:T(8,128)(2,1)}, u32[]{:S(2)}) copy-start(bf16[512,4096]{1,0:T(8,128)(2,1)} %refs_5_.1) | copy-start | bytes 12582916
  45.8 18.7 %copy-start.3 = (bf16[64,2,8,512]{3,2,1,0:T(8,128)(2,1)S(1)}, bf16[64,2,8,512]{3,2,1,0:T(8,128)(2,1)}, u32[]{:S(2)}) copy-start(bf16[64,2,8,512]{3,2,1,0:T(8,128)(2,1)} %refs_6_.1) | copy-start | bytes 3145732
  45.9 18.7 %copy-start.6 = (bf16[2,20,8,512]{3,2,1,0:T(8,128)(2,1)S(1)}, bf16[2,20,8,512]{3,2,1,0:T(8,128)(2,1)}, u32[]{:S(2)}) copy-start(bf16[2,20,8,512]{3,2,1,0:T(8,128)(2,1)} %copy-done.5) | copy-start | bytes 983044
  60.3 19.9 %collective-permute-start.4 = (bf16[2,20,8,512]{3,2,1,0:T(8,128)(2,1)S(1)}, bf16[2,20,8,512]{3,2,1,0:T(8,128)(2,1)S(1)}, u32[]{:S(2)}, u32[]{:S(2)}) collective-permute-start(bf16[2,20,8,512]{3,2,1,0:T(8,128)(2,1)S(1)} %copy-done.31), channel_id=1, source_target_pairs={{0,4},{1,5},{2,6},{3,7},{4,0},{5,1},{6,2},{7,3},{8,12},{9,13},{10,... | collective-permute-start | bytes 983048 | tf_op jit(solution)/shard_map/ppermute | solution.py:501
  60.6 20.1 %collective-permute-start.6 = (bf16[2,20,8,512]{3,2,1,0:T(8,128)(2,1)S(1)}, bf16[2,20,8,512]{3,2,1,0:T(8,128)(2,1)S(1)}, u32[]{:S(2)}, u32[]{:S(2)}) collective-permute-start(bf16[2,20,8,512]{3,2,1,0:T(8,128)(2,1)S(1)} %copy-done.29), channel_id=1, source_target_pairs={{0,5},{1,4},{2,7},{3,6},{4,1},{5,0},{6,3},{7,2},{8,13},{9,12},{10,... | collective-permute-start | bytes 983048 | tf_op jit(solution)/shard_map/ppermute | solution.py:501
  62.0 35.2 %collective-permute-start.7 = (bf16[2,20,8,512]{3,2,1,0:T(8,128)(2,1)S(1)}, bf16[2,20,8,512]{3,2,1,0:T(8,128)(2,1)S(1)}, u32[]{:S(2)}, u32[]{:S(2)}) collective-permute-start(bf16[2,20,8,512]{3,2,1,0:T(8,128)(2,1)S(1)} %copy-done.27), channel_id=1, source_target_pairs={{0,13},{1,12},{2,15},{3,14},{4,9},{5,8},{6,11},{7,10},{8,5},{9,4},... | collective-permute-start | bytes 983048 | tf_op jit(solution)/shard_map/ppermute | solution.py:501
  64.6 13.4 %copy-start.25 = (bf16[2,20,8,512]{3,2,1,0:T(8,128)(2,1)S(1)}, bf16[2,20,8,512]{3,2,1,0:T(8,128)(2,1)}, u32[]{:S(2)}) copy-start(bf16[2,20,8,512]{3,2,1,0:T(8,128)(2,1)} %copy-done.24) | copy-start | bytes 983044
  64.6 14.2 %copy-start.23 = (bf16[2,20,8,512]{3,2,1,0:T(8,128)(2,1)S(1)}, bf16[2,20,8,512]{3,2,1,0:T(8,128)(2,1)}, u32[]{:S(2)}) copy-start(bf16[2,20,8,512]{3,2,1,0:T(8,128)(2,1)} %copy-done.22) | copy-start | bytes 983044
  64.6 15.6 %copy-start.21 = (bf16[2,20,8,512]{3,2,1,0:T(8,128)(2,1)S(1)}, bf16[2,20,8,512]{3,2,1,0:T(8,128)(2,1)}, u32[]{:S(2)}) copy-start(bf16[2,20,8,512]{3,2,1,0:T(8,128)(2,1)} %copy-done.20) | copy-start | bytes 983044
  64.6 16.1 %copy-start.19 = (bf16[2,20,8,512]{3,2,1,0:T(8,128)(2,1)S(1)}, bf16[2,20,8,512]{3,2,1,0:T(8,128)(2,1)}, u32[]{:S(2)}) copy-start(bf16[2,20,8,512]{3,2,1,0:T(8,128)(2,1)} %copy-done.18) | copy-start | bytes 983044
  78.0 27.8 %collective-permute-start.8 = (bf16[2,20,8,512]{3,2,1,0:T(8,128)(2,1)S(1)}, bf16[2,20,8,512]{3,2,1,0:T(8,128)(2,1)S(1)}, u32[]{:S(2)}, u32[]{:S(2)}) collective-permute-start(bf16[2,20,8,512]{3,2,1,0:T(8,128)(2,1)S(1)} %copy-done.25), channel_id=1, source_target_pairs={{0,6},{1,7},{2,4},{3,5},{4,2},{5,3},{6,0},{7,1},{8,14},{9,15},{10,... | collective-permute-start | bytes 983048 | tf_op jit(solution)/shard_map/ppermute | solution.py:501
  78.7 29.3 %collective-permute-start.9 = (bf16[2,20,8,512]{3,2,1,0:T(8,128)(2,1)S(1)}, bf16[2,20,8,512]{3,2,1,0:T(8,128)(2,1)S(1)}, u32[]{:S(2)}, u32[]{:S(2)}) collective-permute-start(bf16[2,20,8,512]{3,2,1,0:T(8,128)(2,1)S(1)} %copy-done.23), channel_id=1, source_target_pairs={{0,9},{1,8},{2,11},{3,10},{4,13},{5,12},{6,15},{7,14},{8,1},{9,0},... | collective-permute-start | bytes 983048 | tf_op jit(solution)/shard_map/ppermute | solution.py:501
  80.2 31.0 %collective-permute-start.10 = (bf16[2,20,8,512]{3,2,1,0:T(8,128)(2,1)S(1)}, bf16[2,20,8,512]{3,2,1,0:T(8,128)(2,1)S(1)}, u32[]{:S(2)}, u32[]{:S(2)}) collective-permute-start(bf16[2,20,8,512]{3,2,1,0:T(8,128)(2,1)S(1)} %copy-done.21), channel_id=1, source_target_pairs={{0,7},{1,6},{2,5},{3,4},{4,3},{5,2},{6,1},{7,0},{8,15},{9,14},{10,... | collective-permute-start | bytes 983048 | tf_op jit(solution)/shard_map/ppermute | solution.py:501
  80.7 42.6 %collective-permute-start.11 = (bf16[2,20,8,512]{3,2,1,0:T(8,128)(2,1)S(1)}, bf16[2,20,8,512]{3,2,1,0:T(8,128)(2,1)S(1)}, u32[]{:S(2)}, u32[]{:S(2)}) collective-permute-start(bf16[2,20,8,512]{3,2,1,0:T(8,128)(2,1)S(1)} %copy-done.19), channel_id=1, source_target_pairs={{0,14},{1,15},{2,12},{3,13},{4,10},{5,11},{6,8},{7,9},{8,6},{9,7},... | collective-permute-start | bytes 983048 | tf_op jit(solution)/shard_map/ppermute | solution.py:501
  83.7 13.4 %copy-start.17 = (bf16[2,20,8,512]{3,2,1,0:T(8,128)(2,1)S(1)}, bf16[2,20,8,512]{3,2,1,0:T(8,128)(2,1)}, u32[]{:S(2)}) copy-start(bf16[2,20,8,512]{3,2,1,0:T(8,128)(2,1)} %copy-done.16) | copy-start | bytes 983044
  83.8 22.0 %copy-start.15 = (bf16[2,20,8,512]{3,2,1,0:T(8,128)(2,1)S(1)}, bf16[2,20,8,512]{3,2,1,0:T(8,128)(2,1)}, u32[]{:S(2)}) copy-start(bf16[2,20,8,512]{3,2,1,0:T(8,128)(2,1)} %copy-done.14) | copy-start | bytes 983044
  83.8 24.2 %copy-start.13 = (bf16[2,20,8,512]{3,2,1,0:T(8,128)(2,1)S(1)}, bf16[2,20,8,512]{3,2,1,0:T(8,128)(2,1)}, u32[]{:S(2)}) copy-start(bf16[2,20,8,512]{3,2,1,0:T(8,128)(2,1)} %copy-done.12) | copy-start | bytes 983044
  97.1 50.4 %collective-permute-start.12 = (bf16[2,20,8,512]{3,2,1,0:T(8,128)(2,1)S(1)}, bf16[2,20,8,512]{3,2,1,0:T(8,128)(2,1)S(1)}, u32[]{:S(2)}, u32[]{:S(2)}) collective-permute-start(bf16[2,20,8,512]{3,2,1,0:T(8,128)(2,1)S(1)} %copy-done.17), channel_id=1, source_target_pairs={{0,10},{1,11},{2,8},{3,9},{4,14},{5,15},{6,12},{7,13},{8,2},{9,3},... | collective-permute-start | bytes 983048 | tf_op jit(solution)/shard_map/ppermute | solution.py:501
  105.7 52.9 %collective-permute-start.13 = (bf16[2,20,8,512]{3,2,1,0:T(8,128)(2,1)S(1)}, bf16[2,20,8,512]{3,2,1,0:T(8,128)(2,1)S(1)}, u32[]{:S(2)}, u32[]{:S(2)}) collective-permute-start(bf16[2,20,8,512]{3,2,1,0:T(8,128)(2,1)S(1)} %copy-done.15), channel_id=1, source_target_pairs={{0,15},{1,14},{2,13},{3,12},{4,11},{5,10},{6,9},{7,8},{8,7},{9,6},... | collective-permute-start | bytes 983048 | tf_op jit(solution)/shard_map/ppermute | solution.py:501
  108.0 53.6 %collective-permute-start.14 = (bf16[2,20,8,512]{3,2,1,0:T(8,128)(2,1)S(1)}, bf16[2,20,8,512]{3,2,1,0:T(8,128)(2,1)S(1)}, u32[]{:S(2)}, u32[]{:S(2)}) collective-permute-start(bf16[2,20,8,512]{3,2,1,0:T(8,128)(2,1)S(1)} %copy-done.13), channel_id=1, source_target_pairs={{0,11},{1,10},{2,9},{3,8},{4,15},{5,14},{6,13},{7,12},{8,3},{9,2},... | collective-permute-start | bytes 983048 | tf_op jit(solution)/shard_map/ppermute | solution.py:501
  111.2 36.3 %copy-start.4 = (bf16[32,4096]{1,0:T(8,128)(2,1)S(1)}, bf16[32,4096]{1,0:T(8,128)(2,1)}, u32[]{:S(2)}) copy-start(bf16[32,4096]{1,0:T(8,128)(2,1)} %refs_0_.7) | copy-start | bytes 786436
  111.2 36.3 %copy-start.7 = (f32[4,256,128]{2,1,0:T(8,128)S(1)}, f32[4,256,128]{2,1,0:T(8,128)}, u32[]{:S(2)}) copy-start(f32[4,256,128]{2,1,0:T(8,128)} %get-tuple-element.38.refs_1_) | copy-start | bytes 1572868
  111.2 36.3 %copy-start.8 = (f32[4,256,128]{2,1,0:T(8,128)S(1)}, f32[4,256,128]{2,1,0:T(8,128)}, u32[]{:S(2)}) copy-start(f32[4,256,128]{2,1,0:T(8,128)} %get-tuple-element.39.refs_2_) | copy-start | bytes 1572868
  111.2 36.3 %copy-start.9 = (f32[4,256,128]{2,1,0:T(8,128)S(1)}, f32[4,256,128]{2,1,0:T(8,128)}, u32[]{:S(2)}) copy-start(f32[4,256,128]{2,1,0:T(8,128)} %get-tuple-element.40.refs_3_) | copy-start | bytes 1572868
  111.2 36.3 %copy-start.10 = (s32[32,1]{1,0:T(8,128)S(1)}, s32[32,1]{1,0:T(8,128)}, u32[]{:S(2)}) copy-start(s32[32,1]{1,0:T(8,128)} %copy.26.rest_ref.refs_6_) | copy-start | bytes 388

commit v2 on v1

--- a/solution.py
+++ b/solution.py
@@ -95,37 +95,51 @@
     v_ref[rows, 0:HD] = jnp.where(seen, val, 0.0).astype(jnp.bfloat16)
 
 
-def prefill_first(q, fresh, after):
+def prefill_first(q, fresh, pieces, ks, pages, plen, after, cap, size):
     tokens, qwidth = q.shape
-    _, width = fresh.shape[2:]
+    page, width = fresh.shape[2:]
     rows = min(256, tokens)
-
-    def body(q_ref, f_ref, _, m_ref, acc_ref, l_ref, k_ref, v_ref):
-        v_ref[:, HD:] = jnp.ones((tokens, HD), jnp.bfloat16)
-        k_lane = lax.broadcasted_iota(jnp.int32, (tokens, HD), 1)
+    n = len(pieces)
+    each = cap * page
+    held = n * each
+
+    def body(*refs):
+        plen_ref, pages_ref, q_ref, f_ref = refs[:4]
+        piece_refs = refs[4 : 4 + n]
+        _, m_ref, acc_ref, l_ref, vis_ref, k_ref, v_ref = refs[4 + n :]
+        for i, k in enumerate(ks):
+            mark_visible(vis_ref, i * each, k, cap, page, pages_ref, plen_ref, size)
+        v_ref[0:held, HD:] = vis_ref[...].astype(jnp.bfloat16)
+        v_ref[held:, HD:] = jnp.ones((tokens, HD), jnp.bfloat16)
+        k_lane = lax.broadcasted_iota(jnp.int32, (held + tokens, HD), 1)
         k_ref[:, HD:] = jnp.where(k_lane == 0, -1.0, 0.0).astype(jnp.bfloat16)
         row = lax.broadcasted_iota(jnp.int32, (rows, rows), 0)
         col = lax.broadcasted_iota(jnp.int32, (rows, rows), 1)
+        lane = lax.broadcasted_iota(jnp.int32, (tokens, HD), 1)
 
         def group(g, carry):
             key = f_ref[:, 0, :, head_at(g)].reshape(tokens, HD)
-            k_ref[:, 0:HD] = key
-            v_ref[:, 0:HD] = f_ref[:, 1, :, head_at(g)].reshape(tokens, HD)
+            k_ref[held:, 0:HD] = key
+            v_ref[held:, 0:HD] = f_ref[:, 1, :, head_at(g)].reshape(tokens, HD)
             key = key.astype(jnp.float32)
+            for i in range(n):
+                at = i * each
+                place_keys(k_ref, v_ref, vis_ref, at, at, g, piece_refs[i], key[0:1], cap, page)
             for h in range(GROUP):
                 cols = head_at(g * GROUP + h)
                 own = jnp.sum(q_ref[:, cols].astype(jnp.float32) * key, axis=1, keepdims=True)
-                m_ref[:, cols] = jnp.where(k_lane == 0, own, 0.0).astype(jnp.bfloat16)
+                m_ref[:, cols] = jnp.where(lane == 0, own, 0.0).astype(jnp.bfloat16)
             for h in range(GROUP):
                 cols = head_at(g * GROUP + h)
                 for r in range(0, tokens, rows):
                     rs = slice(r, r + rows)
+                    shown = held + r + rows
                     lhs = jnp.concatenate([q_ref[rs, cols], m_ref[rs, cols]], 1)
-                    s = lax.dot_general(lhs, k_ref[0 : r + rows, :], NT, preferred_element_type=jnp.float32)
-                    diag = jnp.where(col <= row, s[:, r:], NEG)
-                    s = jnp.concatenate([s[:, :r], diag], 1) if r else diag
+                    s = lax.dot_general(lhs, k_ref[0:shown, :], NT, preferred_element_type=jnp.float32)
+                    diag = jnp.where(col <= row, s[:, held + r :], NEG)
+                    s = jnp.concatenate([s[:, : held + r], diag], 1)
                     p = jnp.exp2(s * CEXP).astype(jnp.bfloat16)
-                    new = jnp.dot(p, v_ref[0 : r + rows, :], preferred_element_type=jnp.float32)
+                    new = jnp.dot(p, v_ref[0:shown, :], preferred_element_type=jnp.float32)
                     acc_ref[rs, cols] = new[:, :HD]
                     l_ref[rs, cols] = new[:, HD:]
             return carry
@@ -133,20 +147,21 @@
         lax.fori_loop(0, width // HD, group, 0)
 
     wide = pltpu.VMEM((tokens, qwidth), jnp.float32)
-    work = tokens * tokens * (qwidth // HD) // 2
+    work = tokens * (tokens // 2 + held) * (qwidth // HD)
     return pl.pallas_call(
         body,
         out_shape=[pltpu.VMEM((tokens, qwidth), jnp.bfloat16), wide, wide],
-        in_specs=[VM, VM, SM],
+        in_specs=[SM, VM, VM, VM] + [VM] * n + [SM],
         out_specs=[VM] * 3,
         scratch_shapes=[
-            pltpu.VMEM((tokens, 2 * HD), jnp.bfloat16),
-            pltpu.VMEM((tokens, 2 * HD), jnp.bfloat16),
+            pltpu.VMEM((held, HD), jnp.float32),
+            pltpu.VMEM((held + tokens, 2 * HD), jnp.bfloat16),
+            pltpu.VMEM((held + tokens, 2 * HD), jnp.bfloat16),
         ],
         compiler_params=PARAMS,
         cost_estimate=pl.CostEstimate(flops=8 * HD * work, transcendentals=work, bytes_accessed=8 * work // HD),
         name="prefill_first",
-    )(q, fresh, after)
+    )(plen, pages, q, fresh, *pieces, after)
 
 
 def add_pages(k_ref, v_ref, q_ref, m_ref, g, emit):
@@ -527,8 +542,18 @@
     last_times = jnp.sum(((dec_pages[:, :, None] == last_names) & last_seen).astype(jnp.float32), 1)
 
     *dec_state, token = decode_pool(dec_q, kv_pool, *counts(jnp.arange(slots, dtype=jnp.int32)), rest)
-    state = prefill_first(suffix_q, fresh_kv, token)
-    for ks in groups[:-1]:
+    state = prefill_first(
+        suffix_q,
+        fresh_kv,
+        [arrived[k] for k in groups[0]],
+        groups[0],
+        prefix_pages,
+        prefix_len,
+        token,
+        cap,
+        size,
+    )
+    for ks in groups[1:-1]:
         new = prefill_more(
             suffix_q, fresh_kv, [arrived[k] for k in ks], ks, prefix_pages, prefix_len, state, cap, size
         )
@@ -557,7 +582,7 @@
 def arrival_groups(order):
     size = len(order)
     if size == 16:
-        return [[0, 1, 2, 3], [12, 4, 8, 5], [13, 6, 9, 7], [14, 10], [15, 11]]
+        return [[0, 1, 2, 3, 12, 4, 8, 5], [13, 6, 9, 7], [14, 10], [15, 11]]
     per = -(-size // 4)
     return [order[i : min(i + per, size - 1)] for i in range(0, size - 1, per)] + [order[-1:]]
 

time: 172 us -> 161 us (0.936)
  Pallas kernels: 94.2 us -> 82.1 us
  local copies, waits for them, and re-layouts: 12.6 us -> 18.9 us
  starting transfers between devices: 31.4 us -> 27 us
    pallas_call x4 -> x2, Pallas kernels: 47.1 us -> 20.4 us  [prefill_more(): pl.pallas_call(body, out_shape=[wide, wide], in_specs=[SM, VM, VM, VM] +...]
    pallas_call x1, Pallas kernels: 14.4 us -> 30 us  [prefill_first(): pl.pallas_call(body, out_shape=[pltpu.VMEM((tokens, qwidth), jnp.bfloat16...]
    unnamed x72 -> x90, local copies, waits for them, and re-layouts: 11.6 us -> 17.9 us
    ppermute x15, starting transfers between devices: 31.4 us -> 27 us  [shards(): arrived[k] = lax.ppermute(outgoing[k], 'pool', pairs)]
  transfers between devices with their start and end apart: 15 -> 15, of which waited for: 2 -> 3; matrix products, arithmetic and copies ran while one was open for 3% -> 3% of each run, Pallas kernels for 48% -> 44%
where the time goes in v2:
time: 161 us; the launch traced here: 160 us
  Pallas kernels  82.1 us (51%)
  starting transfers between devices  27 us (17%)
  waiting for transfers between devices  25.8 us (16%)
  local copies, waits for them, and re-layouts  18.9 us (12%)
  other arithmetic  3.87 us (2%)
  between operations  1.87 us (1%)
    pallas_call x1, Pallas kernels, prefill_first(): pl.pallas_call(body, out_shape=[pltpu.VMEM((tokens, qwidth), jnp.bfloat16...  30 us
    ppermute x15, starting transfers between devices, shards(): arrived[k] = lax.ppermute(outgoing[k], 'pool', pairs)  27 us
    ppermute x15, waiting for transfers between devices, shards(): arrived[k] = lax.ppermute(outgoing[k], 'pool', pairs)  25.8 us
    pallas_call x2, Pallas kernels, prefill_more(): pl.pallas_call(body, out_shape=[wide, wide], in_specs=[SM, VM, VM, VM] +...  20.4 us
    unnamed x90, local copies, waits for them, and re-layouts  17.9 us
    pallas_call x1, Pallas kernels, decode_pool(): pl.pallas_call(body, grid=(steps,), out_shape=[jax.ShapeDtypeStruct(shape...  13.9 us
    pallas_call x1, Pallas kernels, finish(): pl.pallas_call(body, out_shape=[jax.ShapeDtypeStruct(dec_q.shape, dec_q.d...  9.05 us
    pallas_call x2, Pallas kernels, gather_pages(): pl.pallas_call(body, out_shape=[pltpu.VMEM(shape, kv_pool.dtype)] * n, in...  7.02 us
  transfers between devices with their start and end apart: 15, of which 3 were waited for; matrix products, arithmetic and copies ran while one was open for 3% of the time, Pallas kernels for 44%

profile of v2, /device:TPU:0, one launch (start us, length us, event | category | flops | bytes accessed | tf_op | source)
XLA Modules:
  0.0 159.6 jit_solution(16071738157276715047)
XLA Ops:
  0.6 0.0 copy-start.44
  0.6 0.0 copy-start.43
  0.7 2.6 %gather_pages.2 = (bf16[2,20,8,512]{3,2,1,0:T(8,128)(2,1)S(1)}, bf16[2,20,8,512]{3,2,1,0:T(8,128)(2,1)}) custom-call(s32[1,256]{1,0:T(1,128)} %slots_ref.3, s32[1,64]{1,0:T(1,128)} %routes_ref.3, bf16[512,2,8,512]{3,2,1,0:T(8,128)(2,1)} %pool_ref.3, bf16[64,2,8,512]{3,2,1,0:T(8,128)(2,1)} %refs_6_.1), custom_call_target="tpu_custom_call" | custom-call | bytes 1310720 | tf_op jit(solution)/shard_map/gather_pages/pallas_call | solution.py:63
  3.3 4.1 %collective-permute-start.5 = (bf16[2,20,8,512]{3,2,1,0:T(8,128)(2,1)}, bf16[2,20,8,512]{3,2,1,0:T(8,128)(2,1)S(1)}, u32[]{:S(2)}, u32[]{:S(2)}) collective-permute-start(bf16[2,20,8,512]{3,2,1,0:T(8,128)(2,1)} %get-tuple-element.43), channel_id=1, source_target_pairs={{0,8},{1,9},{2,10},{3,11},{4,12},{5,13},{6,14},{7,15},{8,0},{9,1},... | collective-permute-start | bytes 983048 | tf_op jit(solution)/shard_map/ppermute | solution.py:516
  7.4 1.3 collective-permute-start.3
  8.8 4.4 %gather_pages.3 = (bf16[2,20,8,512]{3,2,1,0:T(8,128)(2,1)}, bf16[2,20,8,512]{3,2,1,0:T(8,128)(2,1)S(1)}, bf16[2,20,8,512]{3,2,1,0:T(8,128)(2,1)S(1)}, bf16[2,20,...) custom-call(s32[1,256]{1,0:T(1,128)} %slots_ref.3, ...), custom_call_target="tpu_custom_call" | custom-call | bytes 9175040 | tf_op jit(solution)/shard_map/gather_pages/pallas_call | solution.py:63
  13.2 0.7 copy-done.11
  13.9 0.7 copy-done.35
  14.7 0.7 copy-done.37
  15.4 0.7 copy-done.39
  16.1 0.0 collective-permute-start
  16.1 1.5 collective-permute-start.1
  17.6 0.4 collective-permute-start.2
  18.7 0.1 iota_add_fusion.1
  18.8 0.1 add.89
  18.9 0.1 broadcast_in_dim.17
  18.9 0.1 eq.72
  19.0 0.1 iota_add_fusion
  19.1 0.1 add.86
  19.2 0.7 copy.22.rest_ref.refs_6_
  19.9 0.1 iota_compare_fusion.1
  20.0 0.1 broadcast_add_fusion
  20.0 0.6 convert_reduce_fusion.3
  20.7 2.4 %convert_reduce_fusion = (bf16[32,512]{1,0:T(8,128)(2,1)}, bf16[32,512]{1,0:T(8,128)(2,1)}) fusion(s32[32,64]{1,0:T(8,128)S(1)} %copy-done.41, pred[32,64]{1,0:T(8,128)(4,1)S(1)} %get-tuple-element.72, pred[32,64]{1,0:T(8,128)(4,1)S(1)} %get-tuple-element.73), kind=kLoop, calls=%fused_computation | loop fusion | flops 7307264 | bytes 77824 | tf_op jit(solution)/shard_map/reduce_sum | solution.py:527
  23.1 7.1 %collective-permute-done.5.refs_13_.refs_10_.refs_20_ = bf16[2,20,8,512]{3,2,1,0:T(8,128)(2,1)S(1)} collective-permute-done((bf16[2,20,8,512]{3,2,1,0:T(8,128)(2,1)}, bf16[2,20,8,512]{3,2,1,0:T(8,128)(2,1)S(1)}, u32[]{:S(2)}, u32[]{:S(2)}) %collective-permute-start.5) | collective-permute-done | bytes 327712 | tf_op jit(solution)/shard_map/ppermute | solution.py:516
  30.2 0.1 collective-permute-start.4
  30.3 6.4 %collective-permute-start.6 = (bf16[2,20,8,512]{3,2,1,0:T(8,128)(2,1)S(1)}, bf16[2,20,8,512]{3,2,1,0:T(8,128)(2,1)S(1)}, u32[]{:S(2)}, u32[]{:S(2)}) collective-permute-start(bf16[2,20,8,512]{3,2,1,0:T(8,128)(2,1)S(1)} %get-tuple-element.44), channel_id=1, source_target_pairs={{0,5},{1,4},{2,7},{3,6},{4,1},{5,0},{6,3},{7,2},{8,13},{9,12},{10,... | collective-permute-start | bytes 983048 | tf_op jit(solution)/shard_map/ppermute | solution.py:516
  36.8 0.5 convert_reduce_fusion.2.refs_4_
  37.2 13.9 %decode_pool.1 = (f32[4,256,128]{2,1,0:T(8,128)}, f32[4,256,128]{2,1,0:T(8,128)}, f32[4,256,128]{2,1,0:T(8,128)}, s32[1]{0:T(128)}) custom-call(bf16[32,4096]{1,0:T(8,128)(2,1)} %refs_0_.6, bf16[512,2,8,512]{3,2,1,0:T(8,128)(2,1)} %pool_ref.3, bf16[32,512]{1,0:T(8,128)(2,1)} %get-tuple-element.69.full_ref, bf16[32,512]{1,0:T(8,128)(2,1)} %get-tuple-element.68.part_ref, ...), custom_call_target="tpu_custom_call" | custom-call | flops 2147483648 | bytes 8388608 | tf_op jit(solution)/shard_map/decode_pool/pallas_call | solution.py:293
  51.1 0.0 collective-permute-done.refs_8_.refs_5_.refs_15_
  51.1 0.7 copy-done.14
  51.9 3.5 %collective-permute-start.7 = (bf16[2,20,8,512]{3,2,1,0:T(8,128)(2,1)}, bf16[2,20,8,512]{3,2,1,0:T(8,128)(2,1)S(1)}, u32[]{:S(2)}, u32[]{:S(2)}) collective-permute-start(bf16[2,20,8,512]{3,2,1,0:T(8,128)(2,1)} %get-tuple-element.45), channel_id=1, source_target_pairs={{0,13},{1,12},{2,15},{3,14},{4,9},{5,8},{6,11},{7,10},{8,5},{9,4},... | collective-permute-start | bytes 983048 | tf_op jit(solution)/shard_map/ppermute | solution.py:516
  55.4 0.7 copy-done.17
  56.1 0.7 copy-done.20
  56.8 1.3 collective-permute-start.9
  58.1 0.0 collective-permute-done.4.refs_12_.refs_9_.refs_19_
  58.1 0.7 copy-done.23
  58.8 1.0 collective-permute-start.10
  59.8 0.0 collective-permute-done.6.refs_14_.refs_11_.refs_21_
  59.8 0.7 copy-done.26
  60.6 2.7 %collective-permute-start.11 = (bf16[2,20,8,512]{3,2,1,0:T(8,128)(2,1)}, bf16[2,20,8,512]{3,2,1,0:T(8,128)(2,1)S(1)}, u32[]{:S(2)}, u32[]{:S(2)}) collective-permute-start(bf16[2,20,8,512]{3,2,1,0:T(8,128)(2,1)} %get-tuple-element.49), channel_id=1, source_target_pairs={{0,14},{1,15},{2,12},{3,13},{4,10},{5,11},{6,8},{7,9},{8,6},{9,7},... | collective-permute-start | bytes 983048 | tf_op jit(solution)/shard_map/ppermute | solution.py:516
  63.3 2.2 %copy-done = bf16[512,4096]{1,0:T(8,128)(2,1)S(1)} copy-done((bf16[512,4096]{1,0:T(8,128)(2,1)S(1)}, bf16[512,4096]{1,0:T(8,128)(2,1)}, u32[]{:S(2)}) %copy-start) | copy-done | bytes 4194328
  65.5 1.2 copy-done.2
  66.8 1.0 copy-done.6
  67.7 1.0 copy-done.9
  68.7 1.0 copy-done.12
  69.7 1.0 copy-done.15
  70.6 1.0 copy-done.18
  71.6 1.0 copy-done.21
  72.6 1.0 copy-done.24
  73.6 1.0 copy-done.27
  74.6 30.0 %prefill_first.1 = (bf16[512,4096]{1,0:T(8,128)(2,1)S(1)}, f32[512,4096]{1,0:T(8,128)S(1)}, f32[512,4096]{1,0:T(8,128)S(1)}) custom-call(s32[1]{0:T(128)S(6)} %copy.28.refs_0_.refs_8_, s32[1,256]{1,0:T(1,128)S(1)} %copy-done.34, bf16[512,4096]{1,0:T(8,128)(2,1)S(1)} %copy-done, bf16[64,2,8,512]{3,2,1,0:T(8,128)(2,1)S(1)} %copy-done.2, ...), custom_call_target="tpu_custom_call" | custom-call | flops 21474836480 | bytes 1310720 | tf_op jit(solution)/shard_map/prefill_first/pallas_call | solution.py:151
  104.5 0.0 collective-permute-done.7.refs_15_.refs_4_.refs_22_
  104.5 1.6 collective-permute-start.12
  106.1 2.6 %collective-permute-start.13 = (bf16[2,20,8,512]{3,2,1,0:T(8,128)(2,1)S(1)}, bf16[2,20,8,512]{3,2,1,0:T(8,128)(2,1)S(1)}, u32[]{:S(2)}, u32[]{:S(2)}) collective-permute-start(bf16[2,20,8,512]{3,2,1,0:T(8,128)(2,1)S(1)} %copy-done.38), channel_id=1, source_target_pairs={{0,15},{1,14},{2,13},{3,12},{4,11},{5,10},{6,9},{7,8},{8,7},{9,6},... | collective-permute-start | bytes 983048 | tf_op jit(solution)/shard_map/ppermute | solution.py:516
  108.7 0.5 collective-permute-start.14
  109.3 0.0 copy-start.4
  109.4 0.0 copy-start.29
  109.4 12.0 %prefill_more.2 = (f32[512,4096]{1,0:T(8,128)S(1)}, f32[512,4096]{1,0:T(8,128)S(1)}) custom-call(s32[1]{0:T(128)S(6)} %copy.28.refs_0_.refs_8_, s32[1,256]{1,0:T(1,128)S(1)} %copy-done.34, bf16[512,4096]{1,0:T(8,128)(2,1)S(1)} %copy-done.1, bf16[64,2,8,512]{3,2,1,0:T(8,128)(2,1)S(1)} %copy-done.3, ...), custom_call_target="tpu_custom_call", output_to_operand_aliasing={{0}: (9, {}), {1}: (10, {})} | custom-call | flops 8589934592 | bytes 524288 | tf_op jit(solution)/shard_map/prefill_more/pallas_call | solution.py:215
  121.5 16.6 %collective-permute-done.12.refs_20_.refs_5_.refs_27_ = bf16[2,20,8,512]{3,2,1,0:T(8,128)(2,1)S(1)} collective-permute-done((bf16[2,20,8,512]{3,2,1,0:T(8,128)(2,1)S(1)}, bf16[2,20,8,512]{3,2,1,0:T(8,128)(2,1)S(1)}, u32[]{:S(2)}, u32[]{:S(2)}) %collective-permute-start.12) | collective-permute-done | bytes 327712 | tf_op jit(solution)/shard_map/ppermute | solution.py:516
  138.2 1.8 %decode_fresh.1 = (f32[4,256,128]{2,1,0:T(8,128)S(1)}, f32[4,256,128]{2,1,0:T(8,128)S(1)}, f32[4,256,128]{2,1,0:T(8,128)S(1)}) custom-call(bf16[32,4096]{1,0:T(8,128)(2,1)S(1)} %copy-done.4, f32[4,256,128]{2,1,0:T(8,128)S(1)} %copy-done.29, f32[4,256,128]{2,1,0:T(8,128)S(1)} %copy-done.30, f32[4,256,128]{2,1,0:T(8,128)S(1)} %copy-done.31, ...), custom_call_target="tpu_custom_call" | custom-call | flops 234881024 | bytes 917504 | tf_op jit(solution)/shard_map/decode_fresh/pallas_call | solution.py:345
  140.0 8.4 %prefill_more.3 = (f32[512,4096]{1,0:T(8,128)S(1)}, f32[512,4096]{1,0:T(8,128)S(1)}) custom-call(s32[1]{0:T(128)S(6)} %copy.28.refs_0_.refs_8_, s32[1,256]{1,0:T(1,128)S(1)} %copy-done.34, bf16[512,4096]{1,0:T(8,128)(2,1)S(1)} %copy-done.1, bf16[64,2,8,512]{3,2,1,0:T(8,128)(2,1)S(1)} %copy-done.3, ...), custom_call_target="tpu_custom_call", output_to_operand_aliasing={{0}: (7, {}), {1}: (8, {})} | custom-call | flops 4294967296 | bytes 262144 | tf_op jit(solution)/shard_map/prefill_more/pallas_call | solution.py:215
  148.4 2.0 %collective-permute-done.14.refs_13_.refs_29_ = bf16[2,20,8,512]{3,2,1,0:T(8,128)(2,1)S(1)} collective-permute-done((bf16[2,20,8,512]{3,2,1,0:T(8,128)(2,1)S(1)}, bf16[2,20,8,512]{3,2,1,0:T(8,128)(2,1)S(1)}, u32[]{:S(2)}, u32[]{:S(2)}) %collective-permute-start.14) | collective-permute-done | bytes 327712 | tf_op jit(solution)/shard_map/ppermute | solution.py:516
  150.4 9.1 %finish.1 = (bf16[32,4096]{1,0:T(8,128)(2,1)}, bf16[512,4096]{1,0:T(8,128)(2,1)}) custom-call(bf16[32,4096]{1,0:T(8,128)(2,1)S(1)} %copy-done.4, f32[4,256,128]{2,1,0:T(8,128)S(1)} %get-tuple-element.51.refs_1_, f32[4,256,128]{2,1,0:T(8,128)S(1)} %get-tuple-element.52.refs_2_, f32[4,256,128]{2,1,0:T(8,128)S(1)} %get-tuple-element.53.refs_3_, ...), custom_call_target="tpu_custom_call" | custom-call | flops 4294967296 | bytes 262144 | tf_op jit(solution)/shard_map/finish/pallas_call | solution.py:454
  (81 shorter events, 0.2 us)
Async XLA Ops:
  0.6 18.0 %copy-start.44 = (s32[2]{0:T(128)S(1)}, s32[2]{0:T(128)}, u32[]{:S(2)}) copy-start(s32[2]{0:T(128)} %constant.56.clone) | copy-start | bytes 28
  0.6 18.0 %copy-start.43 = (s32[14]{0:T(128)S(1)}, s32[14]{0:T(128)}, u32[]{:S(2)}) copy-start(s32[14]{0:T(128)} %constant.57.clone) | copy-start | bytes 172
  0.7 18.2 %copy-start.42 = (s32[32]{0:T(128)S(1)}, s32[32]{0:T(128)}, u32[]{:S(2)}) copy-start(s32[32]{0:T(128)} %param.21) | copy-start | bytes 388
  0.7 19.4 %copy-start.41 = (s32[32,64]{1,0:T(8,128)S(1)}, s32[32,64]{1,0:T(8,128)}, u32[]{:S(2)}) copy-start(s32[32,64]{1,0:T(8,128)} %param.20) | copy-start | bytes 24580
  3.3 5.5 %copy-start.32 = (bf16[2,20,8,512]{3,2,1,0:T(8,128)(2,1)}, bf16[2,20,8,512]{3,2,1,0:T(8,128)(2,1)S(1)}, u32[]{:S(2)}) copy-start(bf16[2,20,8,512]{3,2,1,0:T(8,128)(2,1)S(1)} %get-tuple-element.37.rest_0_) | copy-start | bytes 983044
  3.3 26.9 %collective-permute-start.5 = (bf16[2,20,8,512]{3,2,1,0:T(8,128)(2,1)}, bf16[2,20,8,512]{3,2,1,0:T(8,128)(2,1)S(1)}, u32[]{:S(2)}, u32[]{:S(2)}) collective-permute-start(bf16[2,20,8,512]{3,2,1,0:T(8,128)(2,1)} %get-tuple-element.43), channel_id=1, source_target_pairs={{0,8},{1,9},{2,10},{3,11},{4,12},{5,13},{6,14},{7,15},{8,0},{9,1},... | collective-permute-start | bytes 983048 | tf_op jit(solution)/shard_map/ppermute | solution.py:516
  7.4 55.9 %copy-start.34 = (s32[1,256]{1,0:T(1,128)S(1)}, s32[1,256]{1,0:T(1,128)}, u32[]{:S(2)}) copy-start(s32[1,256]{1,0:T(1,128)} %refs_7_.1) | copy-start | bytes 3076
  7.4 22.9 %collective-permute-start.3 = (bf16[2,20,8,512]{3,2,1,0:T(8,128)(2,1)S(1)}, bf16[2,20,8,512]{3,2,1,0:T(8,128)(2,1)S(1)}, u32[]{:S(2)}, u32[]{:S(2)}) collective-permute-start(bf16[2,20,8,512]{3,2,1,0:T(8,128)(2,1)S(1)} %get-tuple-element.37.rest_0_), channel_id=1, source_target_pairs={{0,12},{1,13},{2,14},{3,15},{4,8},{5,9},{6,10},{7,11},{8,4},{9,5},... | collective-permute-start | bytes 983048 | tf_op jit(solution)/shard_map/ppermute | solution.py:516
  13.2 0.7 copy-start.11
  13.9 0.7 copy-start.35
  14.7 0.7 copy-start.37
  15.4 0.7 copy-start.39
  16.1 35.0 %collective-permute-start = (bf16[2,20,8,512]{3,2,1,0:T(8,128)(2,1)}, bf16[2,20,8,512]{3,2,1,0:T(8,128)(2,1)S(1)}, u32[]{:S(2)}, u32[]{:S(2)}) collective-permute-start(bf16[2,20,8,512]{3,2,1,0:T(8,128)(2,1)} %get-tuple-element.39), channel_id=1, source_target_pairs={{0,1},{1,0},{2,3},{3,2},{4,5},{5,4},{6,7},{7,6},{8,9},{9,8},{10,11... | collective-permute-start | bytes 983048 | tf_op jit(solution)/shard_map/ppermute | solution.py:516
  16.1 39.2 %collective-permute-start.1 = (bf16[2,20,8,512]{3,2,1,0:T(8,128)(2,1)S(1)}, bf16[2,20,8,512]{3,2,1,0:T(8,128)(2,1)S(1)}, u32[]{:S(2)}, u32[]{:S(2)}) collective-permute-start(bf16[2,20,8,512]{3,2,1,0:T(8,128)(2,1)S(1)} %get-tuple-element.40), channel_id=1, source_target_pairs={{0,2},{1,3},{2,0},{3,1},{4,6},{5,7},{6,4},{7,5},{8,10},{9,11},{10,... | collective-permute-start | bytes 983048 | tf_op jit(solution)/shard_map/ppermute | solution.py:516
  17.6 38.5 %collective-permute-start.2 = (bf16[2,20,8,512]{3,2,1,0:T(8,128)(2,1)S(1)}, bf16[2,20,8,512]{3,2,1,0:T(8,128)(2,1)S(1)}, u32[]{:S(2)}, u32[]{:S(2)}) collective-permute-start(bf16[2,20,8,512]{3,2,1,0:T(8,128)(2,1)S(1)} %get-tuple-element.41), channel_id=1, source_target_pairs={{0,3},{1,2},{2,1},{3,0},{4,7},{5,6},{6,5},{7,4},{8,11},{9,10},{10,... | collective-permute-start | bytes 983048 | tf_op jit(solution)/shard_map/ppermute | solution.py:516
  30.2 33.1 %copy-start.5 = (bf16[2,20,8,512]{3,2,1,0:T(8,128)(2,1)}, bf16[2,20,8,512]{3,2,1,0:T(8,128)(2,1)S(1)}, u32[]{:S(2)}) copy-start(bf16[2,20,8,512]{3,2,1,0:T(8,128)(2,1)S(1)} %collective-permute-done.5.refs_13_.refs_10_.refs_20_) | copy-start | bytes 983044
  30.2 27.9 %collective-permute-start.4 = (bf16[2,20,8,512]{3,2,1,0:T(8,128)(2,1)S(1)}, bf16[2,20,8,512]{3,2,1,0:T(8,128)(2,1)S(1)}, u32[]{:S(2)}, u32[]{:S(2)}) collective-permute-start(bf16[2,20,8,512]{3,2,1,0:T(8,128)(2,1)S(1)} %get-tuple-element.42), channel_id=1, source_target_pairs={{0,4},{1,5},{2,6},{3,7},{4,0},{5,1},{6,2},{7,3},{8,12},{9,13},{10,... | collective-permute-start | bytes 983048 | tf_op jit(solution)/shard_map/ppermute | solution.py:516
  30.3 33.0 %copy-start.8 = (bf16[2,20,8,512]{3,2,1,0:T(8,128)(2,1)}, bf16[2,20,8,512]{3,2,1,0:T(8,128)(2,1)S(1)}, u32[]{:S(2)}) copy-start(bf16[2,20,8,512]{3,2,1,0:T(8,128)(2,1)S(1)} %collective-permute-done.3.refs_11_.refs_8_.refs_18_) | copy-start | bytes 983044
  30.3 29.5 %collective-permute-start.6 = (bf16[2,20,8,512]{3,2,1,0:T(8,128)(2,1)S(1)}, bf16[2,20,8,512]{3,2,1,0:T(8,128)(2,1)S(1)}, u32[]{:S(2)}, u32[]{:S(2)}) collective-permute-start(bf16[2,20,8,512]{3,2,1,0:T(8,128)(2,1)S(1)} %get-tuple-element.44), channel_id=1, source_target_pairs={{0,5},{1,4},{2,7},{3,6},{4,1},{5,0},{6,3},{7,2},{8,13},{9,12},{10,... | collective-permute-start | bytes 983048 | tf_op jit(solution)/shard_map/ppermute | solution.py:516
  51.1 0.7 copy-start.14
  51.9 52.7 %collective-permute-start.7 = (bf16[2,20,8,512]{3,2,1,0:T(8,128)(2,1)}, bf16[2,20,8,512]{3,2,1,0:T(8,128)(2,1)S(1)}, u32[]{:S(2)}, u32[]{:S(2)}) collective-permute-start(bf16[2,20,8,512]{3,2,1,0:T(8,128)(2,1)} %get-tuple-element.45), channel_id=1, source_target_pairs={{0,13},{1,12},{2,15},{3,14},{4,9},{5,8},{6,11},{7,10},{8,5},{9,4},... | collective-permute-start | bytes 983048 | tf_op jit(solution)/shard_map/ppermute | solution.py:516
  55.3 0.7 copy-start.17
  56.1 50.0 %collective-permute-start.8 = (bf16[2,20,8,512]{3,2,1,0:T(8,128)(2,1)}, bf16[2,20,8,512]{3,2,1,0:T(8,128)(2,1)S(1)}, u32[]{:S(2)}, u32[]{:S(2)}) collective-permute-start(bf16[2,20,8,512]{3,2,1,0:T(8,128)(2,1)} %get-tuple-element.46), channel_id=1, source_target_pairs={{0,6},{1,7},{2,4},{3,5},{4,2},{5,3},{6,0},{7,1},{8,14},{9,15},{10,... | collective-permute-start | bytes 983048 | tf_op jit(solution)/shard_map/ppermute | solution.py:516
  56.1 0.7 copy-start.20
  56.8 51.9 %collective-permute-start.9 = (bf16[2,20,8,512]{3,2,1,0:T(8,128)(2,1)}, bf16[2,20,8,512]{3,2,1,0:T(8,128)(2,1)S(1)}, u32[]{:S(2)}, u32[]{:S(2)}) collective-permute-start(bf16[2,20,8,512]{3,2,1,0:T(8,128)(2,1)} %get-tuple-element.47), channel_id=1, source_target_pairs={{0,9},{1,8},{2,11},{3,10},{4,13},{5,12},{6,15},{7,14},{8,1},{9,0},... | collective-permute-start | bytes 983048 | tf_op jit(solution)/shard_map/ppermute | solution.py:516
  58.1 0.7 copy-start.23
  58.8 50.4 %collective-permute-start.10 = (bf16[2,20,8,512]{3,2,1,0:T(8,128)(2,1)}, bf16[2,20,8,512]{3,2,1,0:T(8,128)(2,1)S(1)}, u32[]{:S(2)}, u32[]{:S(2)}) collective-permute-start(bf16[2,20,8,512]{3,2,1,0:T(8,128)(2,1)} %get-tuple-element.48), channel_id=1, source_target_pairs={{0,7},{1,6},{2,5},{3,4},{4,3},{5,2},{6,1},{7,0},{8,15},{9,14},{10,... | collective-permute-start | bytes 983048 | tf_op jit(solution)/shard_map/ppermute | solution.py:516
  59.8 0.7 copy-start.26
  60.6 60.9 %collective-permute-start.11 = (bf16[2,20,8,512]{3,2,1,0:T(8,128)(2,1)}, bf16[2,20,8,512]{3,2,1,0:T(8,128)(2,1)S(1)}, u32[]{:S(2)}, u32[]{:S(2)}) collective-permute-start(bf16[2,20,8,512]{3,2,1,0:T(8,128)(2,1)} %get-tuple-element.49), channel_id=1, source_target_pairs={{0,14},{1,15},{2,12},{3,13},{4,10},{5,11},{6,8},{7,9},{8,6},{9,7},... | collective-permute-start | bytes 983048 | tf_op jit(solution)/shard_map/ppermute | solution.py:516
  63.3 2.2 %copy-start = (bf16[512,4096]{1,0:T(8,128)(2,1)S(1)}, bf16[512,4096]{1,0:T(8,128)(2,1)}, u32[]{:S(2)}) copy-start(bf16[512,4096]{1,0:T(8,128)(2,1)} %refs_5_.1) | copy-start | bytes 12582916
  65.5 1.2 copy-start.2
  66.7 1.0 copy-start.6
  67.7 1.0 copy-start.9
  68.7 1.0 copy-start.12
  69.7 1.0 copy-start.15
  70.6 1.0 copy-start.18
  71.6 1.0 copy-start.21
  72.6 1.0 copy-start.24
  73.6 1.0 copy-start.27
  74.5 30.0 %copy-start.40 = (bf16[2,20,8,512]{3,2,1,0:T(8,128)(2,1)S(1)}, bf16[2,20,8,512]{3,2,1,0:T(8,128)(2,1)}, u32[]{:S(2)}) copy-start(bf16[2,20,8,512]{3,2,1,0:T(8,128)(2,1)} %copy-done.39) | copy-start | bytes 983044
  74.5 31.6 %copy-start.38 = (bf16[2,20,8,512]{3,2,1,0:T(8,128)(2,1)S(1)}, bf16[2,20,8,512]{3,2,1,0:T(8,128)(2,1)}, u32[]{:S(2)}) copy-start(bf16[2,20,8,512]{3,2,1,0:T(8,128)(2,1)} %copy-done.37) | copy-start | bytes 983044
  74.5 34.2 %copy-start.36 = (bf16[2,20,8,512]{3,2,1,0:T(8,128)(2,1)S(1)}, bf16[2,20,8,512]{3,2,1,0:T(8,128)(2,1)}, u32[]{:S(2)}) copy-start(bf16[2,20,8,512]{3,2,1,0:T(8,128)(2,1)} %copy-done.35) | copy-start | bytes 983044
  74.5 34.7 %copy-start.1 = (bf16[512,4096]{1,0:T(8,128)(2,1)S(1)}, bf16[512,4096]{1,0:T(8,128)(2,1)}, u32[]{:S(2)}) copy-start(bf16[512,4096]{1,0:T(8,128)(2,1)} %refs_5_.1) | copy-start | bytes 12582916
  74.5 34.7 %copy-start.3 = (bf16[64,2,8,512]{3,2,1,0:T(8,128)(2,1)S(1)}, bf16[64,2,8,512]{3,2,1,0:T(8,128)(2,1)}, u32[]{:S(2)}) copy-start(bf16[64,2,8,512]{3,2,1,0:T(8,128)(2,1)} %refs_6_.1) | copy-start | bytes 3145732
  104.5 33.5 %collective-permute-start.12 = (bf16[2,20,8,512]{3,2,1,0:T(8,128)(2,1)S(1)}, bf16[2,20,8,512]{3,2,1,0:T(8,128)(2,1)S(1)}, u32[]{:S(2)}, u32[]{:S(2)}) collective-permute-start(bf16[2,20,8,512]{3,2,1,0:T(8,128)(2,1)S(1)} %copy-done.40), channel_id=1, source_target_pairs={{0,10},{1,11},{2,8},{3,9},{4,14},{5,15},{6,12},{7,13},{8,2},{9,3},... | collective-permute-start | bytes 983048 | tf_op jit(solution)/shard_map/ppermute | solution.py:516
  106.1 42.2 %collective-permute-start.13 = (bf16[2,20,8,512]{3,2,1,0:T(8,128)(2,1)S(1)}, bf16[2,20,8,512]{3,2,1,0:T(8,128)(2,1)S(1)}, u32[]{:S(2)}, u32[]{:S(2)}) collective-permute-start(bf16[2,20,8,512]{3,2,1,0:T(8,128)(2,1)S(1)} %copy-done.38), channel_id=1, source_target_pairs={{0,15},{1,14},{2,13},{3,12},{4,11},{5,10},{6,9},{7,8},{8,7},{9,6},... | collective-permute-start | bytes 983048 | tf_op jit(solution)/shard_map/ppermute | solution.py:516
  108.7 41.7 %collective-permute-start.14 = (bf16[2,20,8,512]{3,2,1,0:T(8,128)(2,1)S(1)}, bf16[2,20,8,512]{3,2,1,0:T(8,128)(2,1)S(1)}, u32[]{:S(2)}, u32[]{:S(2)}) collective-permute-start(bf16[2,20,8,512]{3,2,1,0:T(8,128)(2,1)S(1)} %copy-done.36), channel_id=1, source_target_pairs={{0,11},{1,10},{2,9},{3,8},{4,15},{5,14},{6,13},{7,12},{8,3},{9,2},... | collective-permute-start | bytes 983048 | tf_op jit(solution)/shard_map/ppermute | solution.py:516
  109.3 28.8 %copy-start.4 = (bf16[32,4096]{1,0:T(8,128)(2,1)S(1)}, bf16[32,4096]{1,0:T(8,128)(2,1)}, u32[]{:S(2)}) copy-start(bf16[32,4096]{1,0:T(8,128)(2,1)} %refs_0_.6) | copy-start | bytes 786436
  109.3 28.8 %copy-start.7 = (bf16[2,20,8,512]{3,2,1,0:T(8,128)(2,1)S(1)}, bf16[2,20,8,512]{3,2,1,0:T(8,128)(2,1)}, u32[]{:S(2)}) copy-start(bf16[2,20,8,512]{3,2,1,0:T(8,128)(2,1)} %copy-done.5) | copy-start | bytes 983044
  109.3 28.8 %copy-start.10 = (bf16[2,20,8,512]{3,2,1,0:T(8,128)(2,1)S(1)}, bf16[2,20,8,512]{3,2,1,0:T(8,128)(2,1)}, u32[]{:S(2)}) copy-start(bf16[2,20,8,512]{3,2,1,0:T(8,128)(2,1)} %copy-done.8) | copy-start | bytes 983044
  109.3 28.8 %copy-start.13 = (bf16[2,20,8,512]{3,2,1,0:T(8,128)(2,1)S(1)}, bf16[2,20,8,512]{3,2,1,0:T(8,128)(2,1)}, u32[]{:S(2)}) copy-start(bf16[2,20,8,512]{3,2,1,0:T(8,128)(2,1)} %copy-done.11) | copy-start | bytes 983044
  109.3 28.8 %copy-start.16 = (bf16[2,20,8,512]{3,2,1,0:T(8,128)(2,1)S(1)}, bf16[2,20,8,512]{3,2,1,0:T(8,128)(2,1)}, u32[]{:S(2)}) copy-start(bf16[2,20,8,512]{3,2,1,0:T(8,128)(2,1)} %copy-done.14) | copy-start | bytes 983044
  109.3 28.8 %copy-start.19 = (bf16[2,20,8,512]{3,2,1,0:T(8,128)(2,1)S(1)}, bf16[2,20,8,512]{3,2,1,0:T(8,128)(2,1)}, u32[]{:S(2)}) copy-start(bf16[2,20,8,512]{3,2,1,0:T(8,128)(2,1)} %copy-done.17) | copy-start | bytes 983044
  109.3 28.8 %copy-start.22 = (bf16[2,20,8,512]{3,2,1,0:T(8,128)(2,1)S(1)}, bf16[2,20,8,512]{3,2,1,0:T(8,128)(2,1)}, u32[]{:S(2)}) copy-start(bf16[2,20,8,512]{3,2,1,0:T(8,128)(2,1)} %copy-done.20) | copy-start | bytes 983044
  109.3 28.8 %copy-start.25 = (bf16[2,20,8,512]{3,2,1,0:T(8,128)(2,1)S(1)}, bf16[2,20,8,512]{3,2,1,0:T(8,128)(2,1)}, u32[]{:S(2)}) copy-start(bf16[2,20,8,512]{3,2,1,0:T(8,128)(2,1)} %copy-done.23) | copy-start | bytes 983044
  109.3 28.8 %copy-start.28 = (bf16[2,20,8,512]{3,2,1,0:T(8,128)(2,1)S(1)}, bf16[2,20,8,512]{3,2,1,0:T(8,128)(2,1)}, u32[]{:S(2)}) copy-start(bf16[2,20,8,512]{3,2,1,0:T(8,128)(2,1)} %copy-done.26) | copy-start | bytes 983044
  109.4 28.8 %copy-start.29 = (f32[4,256,128]{2,1,0:T(8,128)S(1)}, f32[4,256,128]{2,1,0:T(8,128)}, u32[]{:S(2)}) copy-start(f32[4,256,128]{2,1,0:T(8,128)} %get-tuple-element.34.refs_1_) | copy-start | bytes 1572868
  109.4 28.8 %copy-start.30 = (f32[4,256,128]{2,1,0:T(8,128)S(1)}, f32[4,256,128]{2,1,0:T(8,128)}, u32[]{:S(2)}) copy-start(f32[4,256,128]{2,1,0:T(8,128)} %get-tuple-element.35.refs_2_) | copy-start | bytes 1572868
  109.4 28.8 %copy-start.31 = (f32[4,256,128]{2,1,0:T(8,128)S(1)}, f32[4,256,128]{2,1,0:T(8,128)}, u32[]{:S(2)}) copy-start(f32[4,256,128]{2,1,0:T(8,128)} %get-tuple-element.36.refs_3_) | copy-start | bytes 1572868
  109.4 28.8 %copy-start.33 = (s32[32,1]{1,0:T(8,128)S(1)}, s32[32,1]{1,0:T(8,128)}, u32[]{:S(2)}) copy-start(s32[32,1]{1,0:T(8,128)} %copy.22.rest_ref.refs_6_) | copy-start | bytes 388

commit v3 on v2

--- a/solution.py
+++ b/solution.py
@@ -15,6 +15,7 @@
 HUGE = 2.0**90
 VMEM_LIMIT = 16 << 20
 POOL_LIMIT = 56 << 20
+FIRST_LIMIT = 22 << 20
 
 
 NT = (((1,), (1,)), ((), ()))
@@ -95,6 +96,15 @@
     v_ref[rows, 0:HD] = jnp.where(seen, val, 0.0).astype(jnp.bfloat16)
 
 
+def fetch_pages(piece_refs, held, sem, cap):
+    copies = [
+        pltpu.make_async_copy(ref.at[:, 0:cap], held.at[i], sem.at[i]) for i, ref in enumerate(piece_refs)
+    ]
+    for copy in copies:
+        copy.start()
+    return copies
+
+
 def prefill_first(q, fresh, pieces, ks, pages, plen, after, cap, size):
     tokens, qwidth = q.shape
     page, width = fresh.shape[2:]
@@ -106,7 +116,8 @@
     def body(*refs):
         plen_ref, pages_ref, q_ref, f_ref = refs[:4]
         piece_refs = refs[4 : 4 + n]
-        _, m_ref, acc_ref, l_ref, vis_ref, k_ref, v_ref = refs[4 + n :]
+        _, m_ref, acc_ref, l_ref, got_ref, sem, vis_ref, k_ref, v_ref = refs[4 + n :]
+        copies = fetch_pages(piece_refs, got_ref, sem, cap)
         for i, k in enumerate(ks):
             mark_visible(vis_ref, i * each, k, cap, page, pages_ref, plen_ref, size)
         v_ref[0:held, HD:] = vis_ref[...].astype(jnp.bfloat16)
@@ -116,6 +127,8 @@
         row = lax.broadcasted_iota(jnp.int32, (rows, rows), 0)
         col = lax.broadcasted_iota(jnp.int32, (rows, rows), 1)
         lane = lax.broadcasted_iota(jnp.int32, (tokens, HD), 1)
+        for copy in copies:
+            copy.wait()
 
         def group(g, carry):
             key = f_ref[:, 0, :, head_at(g)].reshape(tokens, HD)
@@ -124,7 +137,7 @@
             key = key.astype(jnp.float32)
             for i in range(n):
                 at = i * each
-                place_keys(k_ref, v_ref, vis_ref, at, at, g, piece_refs[i], key[0:1], cap, page)
+                place_keys(k_ref, v_ref, vis_ref, at, at, g, got_ref.at[i], key[0:1], cap, page)
             for h in range(GROUP):
                 cols = head_at(g * GROUP + h)
                 own = jnp.sum(q_ref[:, cols].astype(jnp.float32) * key, axis=1, keepdims=True)
@@ -151,14 +164,16 @@
     return pl.pallas_call(
         body,
         out_shape=[pltpu.VMEM((tokens, qwidth), jnp.bfloat16), wide, wide],
-        in_specs=[SM, VM, VM, VM] + [VM] * n + [SM],
+        in_specs=[SM, VM, VM, VM] + [ANY] * n + [SM],
         out_specs=[VM] * 3,
         scratch_shapes=[
+            pltpu.VMEM((n, 2, cap, page, width), q.dtype),
+            pltpu.SemaphoreType.DMA((n,)),
             pltpu.VMEM((held, HD), jnp.float32),
             pltpu.VMEM((held + tokens, 2 * HD), jnp.bfloat16),
             pltpu.VMEM((held + tokens, 2 * HD), jnp.bfloat16),
         ],
-        compiler_params=PARAMS,
+        compiler_params=pltpu.CompilerParams(vmem_limit_bytes=FIRST_LIMIT),
         cost_estimate=pl.CostEstimate(flops=8 * HD * work, transcendentals=work, bytes_accessed=8 * work // HD),
         name="prefill_first",
     )(plen, pages, q, fresh, *pieces, after)
@@ -192,14 +207,17 @@
     def body(*refs):
         plen_ref, pages_ref, q_ref, f_ref = refs[:4]
         piece_refs = refs[4 : 4 + n]
-        m_ref, acc_in, l_in, acc_ref, l_ref, vis_ref, k_ref, v_ref = refs[4 + n :]
+        m_ref, acc_in, l_in, acc_ref, l_ref, got_ref, sem, vis_ref, k_ref, v_ref = refs[4 + n :]
+        copies = fetch_pages(piece_refs, got_ref, sem, cap)
         start_pages(vis_ref, k_ref, v_ref, pages_ref, plen_ref, ks, cap, page, size)
+        for copy in copies:
+            copy.wait()
 
         def group(g, carry):
             stand_in = f_ref[0, 0, :, head_at(g)][0:1].astype(jnp.float32)
             for i in range(n):
                 at = i * cap * page
-                place_keys(k_ref, v_ref, vis_ref, at, at, g, piece_refs[i], stand_in, cap, page)
+                place_keys(k_ref, v_ref, vis_ref, at, at, g, got_ref.at[i], stand_in, cap, page)
 
             def emit(cols, acc, total):
                 acc_ref[:, cols] = acc_in[:, cols] + acc
@@ -215,10 +233,12 @@
     return pl.pallas_call(
         body,
         out_shape=[wide, wide],
-        in_specs=[SM, VM, VM, VM] + [VM] * n + [VM] * 3,
+        in_specs=[SM, VM, VM, VM] + [ANY] * n + [VM] * 3,
         out_specs=[VM, VM],
         input_output_aliases={5 + n: 0, 6 + n: 1},
         scratch_shapes=[
+            pltpu.VMEM((n, 2, cap, page, width), q.dtype),
+            pltpu.SemaphoreType.DMA((n,)),
             pltpu.VMEM((keys, HD), jnp.float32),
             pltpu.VMEM((keys, 2 * HD), jnp.bfloat16),
             pltpu.VMEM((keys, 2 * HD), jnp.bfloat16),
@@ -361,6 +381,7 @@
 
 def finish(dec_q, dec_state, times, q, fresh, pages, plen, state, pieces, ks, last, cap, size):
     page, width = fresh.shape[2:]
+    caps = pieces[0].shape[1] - cap
     requests = dec_q.shape[0]
     heads_kv = width // HD
     tokens, qwidth = q.shape
@@ -374,10 +395,13 @@
         m_ref, acc_ref, l_ref = refs[9:12]
         last_refs = refs[12 : 12 + tail]
         piece_refs = refs[12 + tail : 12 + tail + n]
-        (dec_ref, out_hbm, out_ref, sem, vis_ref, k_ref, v_ref, all_vis, all_k, all_v, page_ref, block_ref) = (
+        (dec_ref, out_hbm, out_ref, sem, got_ref, got_sem, vis_ref, k_ref, v_ref, all_vis, all_k, all_v, page_ref, block_ref) = (
             refs[12 + tail + n :]
         )
+        copies = fetch_pages(last_refs, got_ref, got_sem, cap + caps)
         start_pages(vis_ref, k_ref, v_ref, pages_ref, plen_ref, last, cap, page, size)
+        for copy in copies:
+            copy.wait()
 
         def out_copy(g):
             cols = pl.ds(pl.multiple_of(g * GROUP * HD, GROUP * HD), GROUP * HD)
@@ -386,7 +410,7 @@
         def group(g, sums):
             stand_in = f_ref[0, 0, :, head_at(g)][0:1].astype(jnp.float32)
             for i in range(tail):
-                place_keys(k_ref, v_ref, vis_ref, i * keys, i * keys, g, last_refs[i], stand_in, cap, page)
+                place_keys(k_ref, v_ref, vis_ref, i * keys, i * keys, g, got_ref.at[i], stand_in, cap, page)
             partial = []
 
             def emit(cols, acc, total):
@@ -403,8 +427,8 @@
         times = times_ref[...]
         for g in range(heads_kv):
             cols = slice(g * HD, (g + 1) * HD)
-            key = jnp.concatenate([fresh_rows(p, 0, cap, cols) for p in last_refs], 0)
-            val = jnp.concatenate([fresh_rows(p, 1, cap, cols) for p in last_refs], 0)
+            key = jnp.concatenate([fresh_rows(got_ref.at[i], 0, cap, cols) for i in range(tail)], 0)
+            val = jnp.concatenate([fresh_rows(got_ref.at[i], 1, cap, cols) for i in range(tail)], 0)
             _, l, acc = decode_fold(
                 dq_ref, g, key, val, times, dm_ref[g, :, 0:1], dl_ref[g, :, 0:1], dacc_ref[g]
             )
@@ -457,11 +481,13 @@
             jax.ShapeDtypeStruct(dec_q.shape, dec_q.dtype),
             jax.ShapeDtypeStruct(q.shape, q.dtype),
         ],
-        in_specs=[VM] * 8 + [SM] + [VM] * (3 + tail) + [ANY] * n,
+        in_specs=[VM] * 8 + [SM] + [VM] * 3 + [ANY] * (tail + n),
         out_specs=[VM, ANY],
         scratch_shapes=[
             pltpu.VMEM(q.shape, q.dtype),
             pltpu.SemaphoreType.DMA((heads_kv,)),
+            pltpu.VMEM((tail, 2, cap + caps, page, width), q.dtype),
+            pltpu.SemaphoreType.DMA((tail,)),
             pltpu.VMEM((tail * keys, HD), jnp.float32),
             pltpu.VMEM((tail * keys, 2 * HD), jnp.bfloat16),
             pltpu.VMEM((tail * keys, 2 * HD), jnp.bfloat16),

time: 161 us -> 150 us (0.932)
  local copies, waits for them, and re-layouts: 18.9 us -> 8.08 us
  Pallas kernels: 82.1 us -> 84.4 us
  waiting for transfers between devices: 25.8 us -> 24.1 us
    unnamed x90 -> x48, local copies, waits for them, and re-layouts: 17.9 us -> 7.07 us
    ppermute x15, waiting for transfers between devices: 25.8 us -> 24.1 us  [shards(): arrived[k] = lax.ppermute(outgoing[k], 'pool', pairs)]
  transfers between devices with their start and end apart: 15 -> 15, of which waited for: 3 -> 3; matrix products, arithmetic and copies ran while one was open for 3% -> 3% of each run, Pallas kernels for 44% -> 48%
where the time goes in v3:
time: 150 us; the launch traced here: 149 us
  Pallas kernels  84.4 us (56%)
  starting transfers between devices  27.1 us (18%)
  waiting for transfers between devices  24.1 us (16%)
  local copies, waits for them, and re-layouts  8.08 us (5%)
  other arithmetic  3.85 us (3%)
  between operations  1.7 us (1%)
    pallas_call x1, Pallas kernels, prefill_first(): pl.pallas_call(body, out_shape=[pltpu.VMEM((tokens, qwidth), jnp.bfloat16...  30.7 us
    ppermute x15, starting transfers between devices, shards(): arrived[k] = lax.ppermute(outgoing[k], 'pool', pairs)  27.1 us
    ppermute x15, waiting for transfers between devices, shards(): arrived[k] = lax.ppermute(outgoing[k], 'pool', pairs)  24.1 us
    pallas_call x2, Pallas kernels, prefill_more(): pl.pallas_call(body, out_shape=[wide, wide], in_specs=[SM, VM, VM, VM] +...  20.5 us
    pallas_call x1, Pallas kernels, decode_pool(): pl.pallas_call(body, grid=(steps,), out_shape=[jax.ShapeDtypeStruct(shape...  13.9 us
    pallas_call x1, Pallas kernels, finish(): pl.pallas_call(body, out_shape=[jax.ShapeDtypeStruct(dec_q.shape, dec_q.d...  9.32 us
    pallas_call x2, Pallas kernels, gather_pages(): pl.pallas_call(body, out_shape=[pltpu.VMEM(shape, kv_pool.dtype)] * n, in...  7.32 us
    unnamed x48, local copies, waits for them, and re-layouts  7.07 us
  transfers between devices with their start and end apart: 15, of which 3 were waited for; matrix products, arithmetic and copies ran while one was open for 3% of the time, Pallas kernels for 48%

profile of v3, /device:TPU:0, one launch (start us, length us, event | category | flops | bytes accessed | tf_op | source)
XLA Modules:
  0.0 149.2 jit_solution(7274404441563252635)
XLA Ops:
  0.6 0.0 copy-start.23
  0.6 0.0 copy-start.22
  0.7 2.7 %gather_pages.2 = (bf16[2,20,8,512]{3,2,1,0:T(8,128)(2,1)}, bf16[2,20,8,512]{3,2,1,0:T(8,128)(2,1)}) custom-call(s32[1,256]{1,0:T(1,128)} %slots_ref.3, s32[1,64]{1,0:T(1,128)} %routes_ref.3, bf16[512,2,8,512]{3,2,1,0:T(8,128)(2,1)} %pool_ref.3, bf16[64,2,8,512]{3,2,1,0:T(8,128)(2,1)} %refs_6_.1), custom_call_target="tpu_custom_call" | custom-call | bytes 1310720 | tf_op jit(solution)/shard_map/gather_pages/pallas_call | solution.py:64
  3.4 4.1 %collective-permute-start.5 = (bf16[2,20,8,512]{3,2,1,0:T(8,128)(2,1)}, bf16[2,20,8,512]{3,2,1,0:T(8,128)(2,1)S(1)}, u32[]{:S(2)}, u32[]{:S(2)}) collective-permute-start(bf16[2,20,8,512]{3,2,1,0:T(8,128)(2,1)} %get-tuple-element.43), channel_id=1, source_target_pairs={{0,8},{1,9},{2,10},{3,11},{4,12},{5,13},{6,14},{7,15},{8,0},{9,1},... | collective-permute-start | bytes 983048 | tf_op jit(solution)/shard_map/ppermute | solution.py:542
  7.5 1.3 collective-permute-start.3
  8.9 4.6 %gather_pages.3 = (bf16[2,20,8,512]{3,2,1,0:T(8,128)(2,1)}, bf16[2,20,8,512]{3,2,1,0:T(8,128)(2,1)}, bf16[2,20,8,512]{3,2,1,0:T(8,128)(2,1)}, bf16[2,20,8,512]{3...) custom-call(s32[1,256]{1,0:T(1,128)} %slots_ref.3, ...), custom_call_target="tpu_custom_call" | custom-call | bytes 9175040 | tf_op jit(solution)/shard_map/gather_pages/pallas_call | solution.py:64
  13.5 0.7 copy-done.12
  14.2 0.7 copy-done.14
  14.9 0.7 copy-done.16
  15.7 0.7 copy-done.18
  16.4 0.7 copy-done.19
  17.1 0.0 collective-permute-start
  17.1 1.5 %collective-permute-start.1 = (bf16[2,20,8,512]{3,2,1,0:T(8,128)(2,1)}, bf16[2,20,8,512]{3,2,1,0:T(8,128)(2,1)}, u32[]{:S(2)}, u32[]{:S(2)}) collective-permute-start(bf16[2,20,8,512]{3,2,1,0:T(8,128)(2,1)} %get-tuple-element.40), channel_id=1, source_target_pairs={{0,2},{1,3},{2,0},{3,1},{4,6},{5,7},{6,4},{7,5},{8,10},{9,11},{10,... | collective-permute-start | bytes 983048 | tf_op jit(solution)/shard_map/ppermute | solution.py:542
  18.6 0.4 collective-permute-start.2
  19.7 0.0 copy-done.22
  19.7 0.1 iota_add_fusion.1
  19.8 0.1 add.89
  19.9 0.1 broadcast_in_dim.17
  19.9 0.1 eq.72
  20.0 0.1 iota_add_fusion
  20.1 0.1 add.86
  20.2 0.7 copy.22.rest_ref.refs_6_
  20.9 0.1 iota_compare_fusion.1
  20.9 0.1 broadcast_add_fusion
  21.0 0.0 copy-done.20
  21.0 0.6 convert_reduce_fusion.3
  21.7 2.4 %convert_reduce_fusion = (bf16[32,512]{1,0:T(8,128)(2,1)}, bf16[32,512]{1,0:T(8,128)(2,1)}) fusion(s32[32,64]{1,0:T(8,128)S(1)} %copy-done.20, pred[32,64]{1,0:T(8,128)(4,1)S(1)} %get-tuple-element.72, pred[32,64]{1,0:T(8,128)(4,1)S(1)} %get-tuple-element.73), kind=kLoop, calls=%fused_computation | loop fusion | flops 7307264 | bytes 77824 | tf_op jit(solution)/shard_map/reduce_sum | solution.py:553
  24.1 6.3 %collective-permute-done.5.refs_13_.refs_10_.refs_20_ = bf16[2,20,8,512]{3,2,1,0:T(8,128)(2,1)S(1)} collective-permute-done((bf16[2,20,8,512]{3,2,1,0:T(8,128)(2,1)}, bf16[2,20,8,512]{3,2,1,0:T(8,128)(2,1)S(1)}, u32[]{:S(2)}, u32[]{:S(2)}) %collective-permute-start.5) | collective-permute-done | bytes 327712 | tf_op jit(solution)/shard_map/ppermute | solution.py:542
  30.3 0.1 collective-permute-start.4
  30.4 0.0 collective-permute-done.3.refs_11_.refs_8_.refs_18_
  30.4 6.5 %collective-permute-start.6 = (bf16[2,20,8,512]{3,2,1,0:T(8,128)(2,1)}, bf16[2,20,8,512]{3,2,1,0:T(8,128)(2,1)S(1)}, u32[]{:S(2)}, u32[]{:S(2)}) collective-permute-start(bf16[2,20,8,512]{3,2,1,0:T(8,128)(2,1)} %copy-done.18), channel_id=1, source_target_pairs={{0,5},{1,4},{2,7},{3,6},{4,1},{5,0},{6,3},{7,2},{8,13},{9,12},{10,... | collective-permute-start | bytes 983048 | tf_op jit(solution)/shard_map/ppermute | solution.py:542
  37.0 0.5 convert_reduce_fusion.2.refs_4_
  37.4 13.9 %decode_pool.1 = (f32[4,256,128]{2,1,0:T(8,128)}, f32[4,256,128]{2,1,0:T(8,128)}, f32[4,256,128]{2,1,0:T(8,128)}, s32[1]{0:T(128)}) custom-call(bf16[32,4096]{1,0:T(8,128)(2,1)} %refs_0_.6, bf16[512,2,8,512]{3,2,1,0:T(8,128)(2,1)} %pool_ref.3, bf16[32,512]{1,0:T(8,128)(2,1)} %get-tuple-element.69.full_ref, bf16[32,512]{1,0:T(8,128)(2,1)} %get-tuple-element.68.part_ref, ...), custom_call_target="tpu_custom_call" | custom-call | flops 2147483648 | bytes 8388608 | tf_op jit(solution)/shard_map/decode_pool/pallas_call | solution.py:313
  51.3 0.0 collective-permute-done.refs_8_.refs_5_.refs_15_
  51.3 3.4 %collective-permute-start.7 = (bf16[2,20,8,512]{3,2,1,0:T(8,128)(2,1)}, bf16[2,20,8,512]{3,2,1,0:T(8,128)(2,1)S(1)}, u32[]{:S(2)}, u32[]{:S(2)}) collective-permute-start(bf16[2,20,8,512]{3,2,1,0:T(8,128)(2,1)} %get-tuple-element.45), channel_id=1, source_target_pairs={{0,13},{1,12},{2,15},{3,14},{4,9},{5,8},{6,11},{7,10},{8,5},{9,4},... | collective-permute-start | bytes 983048 | tf_op jit(solution)/shard_map/ppermute | solution.py:542
  54.8 0.0 collective-permute-done.1.refs_9_.refs_6_.refs_16_
  54.8 0.0 collective-permute-start.8
  54.8 0.0 collective-permute-done.2.refs_10_.refs_7_.refs_17_
  54.8 1.4 collective-permute-start.9
  56.1 0.0 collective-permute-done.4.refs_12_.refs_9_.refs_19_
  56.2 0.7 copy-done.3
  56.9 0.9 collective-permute-start.10
  57.8 0.0 collective-permute-done.6.refs_14_.refs_11_.refs_21_
  57.8 0.7 copy-done.5
  58.5 2.8 %collective-permute-start.11 = (bf16[2,20,8,512]{3,2,1,0:T(8,128)(2,1)}, bf16[2,20,8,512]{3,2,1,0:T(8,128)(2,1)S(1)}, u32[]{:S(2)}, u32[]{:S(2)}) collective-permute-start(bf16[2,20,8,512]{3,2,1,0:T(8,128)(2,1)} %get-tuple-element.49), channel_id=1, source_target_pairs={{0,14},{1,15},{2,12},{3,13},{4,10},{5,11},{6,8},{7,9},{8,6},{9,7},... | collective-permute-start | bytes 983048 | tf_op jit(solution)/shard_map/ppermute | solution.py:542
  61.3 0.0 copy-done.11
  61.3 1.0 copy-done.4
  62.3 1.0 copy-done.6
  63.3 30.7 %prefill_first.1 = (bf16[512,4096]{1,0:T(8,128)(2,1)S(1)}, f32[512,4096]{1,0:T(8,128)S(1)}, f32[512,4096]{1,0:T(8,128)S(1)}) custom-call(s32[1]{0:T(128)S(6)} %copy.28.refs_0_.refs_8_, s32[1,256]{1,0:T(1,128)S(1)} %copy-done.11, bf16[512,4096]{1,0:T(8,128)(2,1)S(1)} %copy-done, bf16[64,2,8,512]{3,2,1,0:T(8,128)(2,1)S(1)} %copy-done.1, ...), custom_call_target="tpu_custom_call" | custom-call | flops 21474836480 | bytes 1310720 | tf_op jit(solution)/shard_map/prefill_first/pallas_call | solution.py:164
  93.9 0.0 collective-permute-done.7.refs_15_.refs_4_.refs_22_
  94.0 1.5 collective-permute-start.12
  95.4 0.0 collective-permute-done.8.refs_16_.refs_5_.refs_23_
  95.5 2.6 %collective-permute-start.13 = (bf16[2,20,8,512]{3,2,1,0:T(8,128)(2,1)S(1)}, bf16[2,20,8,512]{3,2,1,0:T(8,128)(2,1)S(1)}, u32[]{:S(2)}, u32[]{:S(2)}) collective-permute-start(bf16[2,20,8,512]{3,2,1,0:T(8,128)(2,1)S(1)} %copy-done.15), channel_id=1, source_target_pairs={{0,15},{1,14},{2,13},{3,12},{4,11},{5,10},{6,9},{7,8},{8,7},{9,6},... | collective-permute-start | bytes 983048 | tf_op jit(solution)/shard_map/ppermute | solution.py:542
  98.1 0.0 collective-permute-done.9.refs_17_.refs_6_.refs_24_
  98.1 0.5 collective-permute-start.14
  98.6 0.0 collective-permute-done.10.refs_18_.refs_7_.refs_25_
  98.6 12.1 %prefill_more.2 = (f32[512,4096]{1,0:T(8,128)S(1)}, f32[512,4096]{1,0:T(8,128)S(1)}) custom-call(s32[1]{0:T(128)S(6)} %copy.28.refs_0_.refs_8_, s32[1,256]{1,0:T(1,128)S(1)} %copy-done.11, bf16[512,4096]{1,0:T(8,128)(2,1)S(1)} %copy-done, bf16[64,2,8,512]{3,2,1,0:T(8,128)(2,1)S(1)} %copy-done.1, ...), custom_call_target="tpu_custom_call", output_to_operand_aliasing={{0}: (9, {}), {1}: (10, {})} | custom-call | flops 8589934592 | bytes 524288 | tf_op jit(solution)/shard_map/prefill_more/pallas_call | solution.py:233
  110.7 0.0 collective-permute-done.11.refs_19_.refs_4_.refs_26_
  110.8 16.7 %collective-permute-done.12.refs_20_.refs_5_.refs_27_ = bf16[2,20,8,512]{3,2,1,0:T(8,128)(2,1)S(1)} collective-permute-done((bf16[2,20,8,512]{3,2,1,0:T(8,128)(2,1)S(1)}, bf16[2,20,8,512]{3,2,1,0:T(8,128)(2,1)S(1)}, u32[]{:S(2)}, u32[]{:S(2)}) %collective-permute-start.12) | collective-permute-done | bytes 327712 | tf_op jit(solution)/shard_map/ppermute | solution.py:542
  127.5 2.7 %decode_fresh.1 = (f32[4,256,128]{2,1,0:T(8,128)S(1)}, f32[4,256,128]{2,1,0:T(8,128)S(1)}, f32[4,256,128]{2,1,0:T(8,128)S(1)}) custom-call(bf16[32,4096]{1,0:T(8,128)(2,1)S(1)} %copy-done.2, f32[4,256,128]{2,1,0:T(8,128)S(1)} %copy-done.7, f32[4,256,128]{2,1,0:T(8,128)S(1)} %copy-done.8, f32[4,256,128]{2,1,0:T(8,128)S(1)} %copy-done.9, ...), custom_call_target="tpu_custom_call" | custom-call | flops 234881024 | bytes 917504 | tf_op jit(solution)/shard_map/decode_fresh/pallas_call | solution.py:365
  130.2 8.4 %prefill_more.3 = (f32[512,4096]{1,0:T(8,128)S(1)}, f32[512,4096]{1,0:T(8,128)S(1)}) custom-call(s32[1]{0:T(128)S(6)} %copy.28.refs_0_.refs_8_, s32[1,256]{1,0:T(1,128)S(1)} %copy-done.11, bf16[512,4096]{1,0:T(8,128)(2,1)S(1)} %copy-done, bf16[64,2,8,512]{3,2,1,0:T(8,128)(2,1)S(1)} %copy-done.1, ...), custom_call_target="tpu_custom_call", output_to_operand_aliasing={{0}: (7, {}), {1}: (8, {})} | custom-call | flops 4294967296 | bytes 262144 | tf_op jit(solution)/shard_map/prefill_more/pallas_call | solution.py:233
  138.6 0.0 collective-permute-done.13.refs_12_.refs_28_
  138.6 1.1 collective-permute-done.14.refs_13_.refs_29_
  139.7 9.3 %finish.1 = (bf16[32,4096]{1,0:T(8,128)(2,1)}, bf16[512,4096]{1,0:T(8,128)(2,1)}) custom-call(bf16[32,4096]{1,0:T(8,128)(2,1)S(1)} %copy-done.2, f32[4,256,128]{2,1,0:T(8,128)S(1)} %get-tuple-element.51.refs_1_, f32[4,256,128]{2,1,0:T(8,128)S(1)} %get-tuple-element.52.refs_2_, f32[4,256,128]{2,1,0:T(8,128)S(1)} %get-tuple-element.53.refs_3_, ...), custom_call_target="tpu_custom_call" | custom-call | flops 4294967296 | bytes 262144 | tf_op jit(solution)/shard_map/finish/pallas_call | solution.py:478
  (39 shorter events, 0.1 us)
Async XLA Ops:
  0.6 19.0 %copy-start.23 = (s32[2]{0:T(128)S(1)}, s32[2]{0:T(128)}, u32[]{:S(2)}) copy-start(s32[2]{0:T(128)} %constant.56.clone) | copy-start | bytes 28
  0.6 19.0 %copy-start.22 = (s32[14]{0:T(128)S(1)}, s32[14]{0:T(128)}, u32[]{:S(2)}) copy-start(s32[14]{0:T(128)} %constant.57.clone) | copy-start | bytes 172
  0.7 19.2 %copy-start.21 = (s32[32]{0:T(128)S(1)}, s32[32]{0:T(128)}, u32[]{:S(2)}) copy-start(s32[32]{0:T(128)} %param.21) | copy-start | bytes 388
  0.7 20.4 %copy-start.20 = (s32[32,64]{1,0:T(8,128)S(1)}, s32[32,64]{1,0:T(8,128)}, u32[]{:S(2)}) copy-start(s32[32,64]{1,0:T(8,128)} %param.20) | copy-start | bytes 24580
  3.4 26.9 %collective-permute-start.5 = (bf16[2,20,8,512]{3,2,1,0:T(8,128)(2,1)}, bf16[2,20,8,512]{3,2,1,0:T(8,128)(2,1)S(1)}, u32[]{:S(2)}, u32[]{:S(2)}) collective-permute-start(bf16[2,20,8,512]{3,2,1,0:T(8,128)(2,1)} %get-tuple-element.43), channel_id=1, source_target_pairs={{0,8},{1,9},{2,10},{3,11},{4,12},{5,13},{6,14},{7,15},{8,0},{9,1},... | collective-permute-start | bytes 983048 | tf_op jit(solution)/shard_map/ppermute | solution.py:542
  7.5 53.8 %copy-start.1 = (bf16[64,2,8,512]{3,2,1,0:T(8,128)(2,1)S(1)}, bf16[64,2,8,512]{3,2,1,0:T(8,128)(2,1)}, u32[]{:S(2)}) copy-start(bf16[64,2,8,512]{3,2,1,0:T(8,128)(2,1)} %refs_6_.1) | copy-start | bytes 3145732
  7.5 53.8 %copy-start.11 = (s32[1,256]{1,0:T(1,128)S(1)}, s32[1,256]{1,0:T(1,128)}, u32[]{:S(2)}) copy-start(s32[1,256]{1,0:T(1,128)} %refs_7_.1) | copy-start | bytes 3076
  7.5 22.9 %collective-permute-start.3 = (bf16[2,20,8,512]{3,2,1,0:T(8,128)(2,1)}, bf16[2,20,8,512]{3,2,1,0:T(8,128)(2,1)S(1)}, u32[]{:S(2)}, u32[]{:S(2)}) collective-permute-start(bf16[2,20,8,512]{3,2,1,0:T(8,128)(2,1)} %get-tuple-element.37.rest_0_), channel_id=1, source_target_pairs={{0,12},{1,13},{2,14},{3,15},{4,8},{5,9},{6,10},{7,11},{8,4},{9,5},... | collective-permute-start | bytes 983048 | tf_op jit(solution)/shard_map/ppermute | solution.py:542
  13.5 0.7 copy-start.12
  14.2 0.7 copy-start.14
  14.9 0.7 copy-start.16
  15.6 0.7 copy-start.18
  16.4 0.7 copy-start.19
  17.1 34.2 %collective-permute-start = (bf16[2,20,8,512]{3,2,1,0:T(8,128)(2,1)}, bf16[2,20,8,512]{3,2,1,0:T(8,128)(2,1)S(1)}, u32[]{:S(2)}, u32[]{:S(2)}) collective-permute-start(bf16[2,20,8,512]{3,2,1,0:T(8,128)(2,1)} %get-tuple-element.39), channel_id=1, source_target_pairs={{0,1},{1,0},{2,3},{3,2},{4,5},{5,4},{6,7},{7,6},{8,9},{9,8},{10,11... | collective-permute-start | bytes 983048 | tf_op jit(solution)/shard_map/ppermute | solution.py:542
  17.1 37.6 %collective-permute-start.1 = (bf16[2,20,8,512]{3,2,1,0:T(8,128)(2,1)}, bf16[2,20,8,512]{3,2,1,0:T(8,128)(2,1)}, u32[]{:S(2)}, u32[]{:S(2)}) collective-permute-start(bf16[2,20,8,512]{3,2,1,0:T(8,128)(2,1)} %get-tuple-element.40), channel_id=1, source_target_pairs={{0,2},{1,3},{2,0},{3,1},{4,6},{5,7},{6,4},{7,5},{8,10},{9,11},{10,... | collective-permute-start | bytes 983048 | tf_op jit(solution)/shard_map/ppermute | solution.py:542
  18.6 36.2 %collective-permute-start.2 = (bf16[2,20,8,512]{3,2,1,0:T(8,128)(2,1)}, bf16[2,20,8,512]{3,2,1,0:T(8,128)(2,1)}, u32[]{:S(2)}, u32[]{:S(2)}) collective-permute-start(bf16[2,20,8,512]{3,2,1,0:T(8,128)(2,1)} %get-tuple-element.41), channel_id=1, source_target_pairs={{0,3},{1,2},{2,1},{3,0},{4,7},{5,6},{6,5},{7,4},{8,11},{9,10},{10,... | collective-permute-start | bytes 983048 | tf_op jit(solution)/shard_map/ppermute | solution.py:542
  20.9 40.4 %copy-start = (bf16[512,4096]{1,0:T(8,128)(2,1)S(1)}, bf16[512,4096]{1,0:T(8,128)(2,1)}, u32[]{:S(2)}) copy-start(bf16[512,4096]{1,0:T(8,128)(2,1)} %refs_5_.1) | copy-start | bytes 12582916
  30.3 25.8 %collective-permute-start.4 = (bf16[2,20,8,512]{3,2,1,0:T(8,128)(2,1)}, bf16[2,20,8,512]{3,2,1,0:T(8,128)(2,1)S(1)}, u32[]{:S(2)}, u32[]{:S(2)}) collective-permute-start(bf16[2,20,8,512]{3,2,1,0:T(8,128)(2,1)} %copy-done.19), channel_id=1, source_target_pairs={{0,4},{1,5},{2,6},{3,7},{4,0},{5,1},{6,2},{7,3},{8,12},{9,13},{10,... | collective-permute-start | bytes 983048 | tf_op jit(solution)/shard_map/ppermute | solution.py:542
  30.4 27.4 %collective-permute-start.6 = (bf16[2,20,8,512]{3,2,1,0:T(8,128)(2,1)}, bf16[2,20,8,512]{3,2,1,0:T(8,128)(2,1)S(1)}, u32[]{:S(2)}, u32[]{:S(2)}) collective-permute-start(bf16[2,20,8,512]{3,2,1,0:T(8,128)(2,1)} %copy-done.18), channel_id=1, source_target_pairs={{0,5},{1,4},{2,7},{3,6},{4,1},{5,0},{6,3},{7,2},{8,13},{9,12},{10,... | collective-permute-start | bytes 983048 | tf_op jit(solution)/shard_map/ppermute | solution.py:542
  51.3 42.6 %collective-permute-start.7 = (bf16[2,20,8,512]{3,2,1,0:T(8,128)(2,1)}, bf16[2,20,8,512]{3,2,1,0:T(8,128)(2,1)S(1)}, u32[]{:S(2)}, u32[]{:S(2)}) collective-permute-start(bf16[2,20,8,512]{3,2,1,0:T(8,128)(2,1)} %get-tuple-element.45), channel_id=1, source_target_pairs={{0,13},{1,12},{2,15},{3,14},{4,9},{5,8},{6,11},{7,10},{8,5},{9,4},... | collective-permute-start | bytes 983048 | tf_op jit(solution)/shard_map/ppermute | solution.py:542
  54.8 40.7 %collective-permute-start.8 = (bf16[2,20,8,512]{3,2,1,0:T(8,128)(2,1)}, bf16[2,20,8,512]{3,2,1,0:T(8,128)(2,1)S(1)}, u32[]{:S(2)}, u32[]{:S(2)}) collective-permute-start(bf16[2,20,8,512]{3,2,1,0:T(8,128)(2,1)} %get-tuple-element.46), channel_id=1, source_target_pairs={{0,6},{1,7},{2,4},{3,5},{4,2},{5,3},{6,0},{7,1},{8,14},{9,15},{10,... | collective-permute-start | bytes 983048 | tf_op jit(solution)/shard_map/ppermute | solution.py:542
  54.8 43.3 %collective-permute-start.9 = (bf16[2,20,8,512]{3,2,1,0:T(8,128)(2,1)}, bf16[2,20,8,512]{3,2,1,0:T(8,128)(2,1)S(1)}, u32[]{:S(2)}, u32[]{:S(2)}) collective-permute-start(bf16[2,20,8,512]{3,2,1,0:T(8,128)(2,1)} %get-tuple-element.47), channel_id=1, source_target_pairs={{0,9},{1,8},{2,11},{3,10},{4,13},{5,12},{6,15},{7,14},{8,1},{9,0},... | collective-permute-start | bytes 983048 | tf_op jit(solution)/shard_map/ppermute | solution.py:542
  56.1 0.7 copy-start.3
  56.9 41.7 %collective-permute-start.10 = (bf16[2,20,8,512]{3,2,1,0:T(8,128)(2,1)}, bf16[2,20,8,512]{3,2,1,0:T(8,128)(2,1)S(1)}, u32[]{:S(2)}, u32[]{:S(2)}) collective-permute-start(bf16[2,20,8,512]{3,2,1,0:T(8,128)(2,1)} %get-tuple-element.48), channel_id=1, source_target_pairs={{0,7},{1,6},{2,5},{3,4},{4,3},{5,2},{6,1},{7,0},{8,15},{9,14},{10,... | collective-permute-start | bytes 983048 | tf_op jit(solution)/shard_map/ppermute | solution.py:542
  57.8 0.7 copy-start.5
  58.5 52.3 %collective-permute-start.11 = (bf16[2,20,8,512]{3,2,1,0:T(8,128)(2,1)}, bf16[2,20,8,512]{3,2,1,0:T(8,128)(2,1)S(1)}, u32[]{:S(2)}, u32[]{:S(2)}) collective-permute-start(bf16[2,20,8,512]{3,2,1,0:T(8,128)(2,1)} %get-tuple-element.49), channel_id=1, source_target_pairs={{0,14},{1,15},{2,12},{3,13},{4,10},{5,11},{6,8},{7,9},{8,6},{9,7},... | collective-permute-start | bytes 983048 | tf_op jit(solution)/shard_map/ppermute | solution.py:542
  61.3 1.0 copy-start.4
  62.3 1.0 copy-start.6
  63.3 30.7 %copy-start.17 = (bf16[2,20,8,512]{3,2,1,0:T(8,128)(2,1)S(1)}, bf16[2,20,8,512]{3,2,1,0:T(8,128)(2,1)}, u32[]{:S(2)}) copy-start(bf16[2,20,8,512]{3,2,1,0:T(8,128)(2,1)} %copy-done.16) | copy-start | bytes 983044
  63.3 32.2 %copy-start.15 = (bf16[2,20,8,512]{3,2,1,0:T(8,128)(2,1)S(1)}, bf16[2,20,8,512]{3,2,1,0:T(8,128)(2,1)}, u32[]{:S(2)}) copy-start(bf16[2,20,8,512]{3,2,1,0:T(8,128)(2,1)} %copy-done.14) | copy-start | bytes 983044
  63.3 34.8 %copy-start.13 = (bf16[2,20,8,512]{3,2,1,0:T(8,128)(2,1)S(1)}, bf16[2,20,8,512]{3,2,1,0:T(8,128)(2,1)}, u32[]{:S(2)}) copy-start(bf16[2,20,8,512]{3,2,1,0:T(8,128)(2,1)} %copy-done.12) | copy-start | bytes 983044
  94.0 33.5 %collective-permute-start.12 = (bf16[2,20,8,512]{3,2,1,0:T(8,128)(2,1)S(1)}, bf16[2,20,8,512]{3,2,1,0:T(8,128)(2,1)S(1)}, u32[]{:S(2)}, u32[]{:S(2)}) collective-permute-start(bf16[2,20,8,512]{3,2,1,0:T(8,128)(2,1)S(1)} %copy-done.17), channel_id=1, source_target_pairs={{0,10},{1,11},{2,8},{3,9},{4,14},{5,15},{6,12},{7,13},{8,2},{9,3},... | collective-permute-start | bytes 983048 | tf_op jit(solution)/shard_map/ppermute | solution.py:542
  95.5 43.1 %collective-permute-start.13 = (bf16[2,20,8,512]{3,2,1,0:T(8,128)(2,1)S(1)}, bf16[2,20,8,512]{3,2,1,0:T(8,128)(2,1)S(1)}, u32[]{:S(2)}, u32[]{:S(2)}) collective-permute-start(bf16[2,20,8,512]{3,2,1,0:T(8,128)(2,1)S(1)} %copy-done.15), channel_id=1, source_target_pairs={{0,15},{1,14},{2,13},{3,12},{4,11},{5,10},{6,9},{7,8},{8,7},{9,6},... | collective-permute-start | bytes 983048 | tf_op jit(solution)/shard_map/ppermute | solution.py:542
  98.1 41.6 %collective-permute-start.14 = (bf16[2,20,8,512]{3,2,1,0:T(8,128)(2,1)S(1)}, bf16[2,20,8,512]{3,2,1,0:T(8,128)(2,1)S(1)}, u32[]{:S(2)}, u32[]{:S(2)}) collective-permute-start(bf16[2,20,8,512]{3,2,1,0:T(8,128)(2,1)S(1)} %copy-done.13), channel_id=1, source_target_pairs={{0,11},{1,10},{2,9},{3,8},{4,15},{5,14},{6,13},{7,12},{8,3},{9,2},... | collective-permute-start | bytes 983048 | tf_op jit(solution)/shard_map/ppermute | solution.py:542
  98.6 28.9 %copy-start.2 = (bf16[32,4096]{1,0:T(8,128)(2,1)S(1)}, bf16[32,4096]{1,0:T(8,128)(2,1)}, u32[]{:S(2)}) copy-start(bf16[32,4096]{1,0:T(8,128)(2,1)} %refs_0_.6) | copy-start | bytes 786436
  98.6 28.9 %copy-start.7 = (f32[4,256,128]{2,1,0:T(8,128)S(1)}, f32[4,256,128]{2,1,0:T(8,128)}, u32[]{:S(2)}) copy-start(f32[4,256,128]{2,1,0:T(8,128)} %get-tuple-element.34.refs_1_) | copy-start | bytes 1572868
  98.6 28.9 %copy-start.8 = (f32[4,256,128]{2,1,0:T(8,128)S(1)}, f32[4,256,128]{2,1,0:T(8,128)}, u32[]{:S(2)}) copy-start(f32[4,256,128]{2,1,0:T(8,128)} %get-tuple-element.35.refs_2_) | copy-start | bytes 1572868
  98.6 28.9 %copy-start.9 = (f32[4,256,128]{2,1,0:T(8,128)S(1)}, f32[4,256,128]{2,1,0:T(8,128)}, u32[]{:S(2)}) copy-start(f32[4,256,128]{2,1,0:T(8,128)} %get-tuple-element.36.refs_3_) | copy-start | bytes 1572868
  98.6 28.9 %copy-start.10 = (s32[32,1]{1,0:T(8,128)S(1)}, s32[32,1]{1,0:T(8,128)}, u32[]{:S(2)}) copy-start(s32[32,1]{1,0:T(8,128)} %copy.22.rest_ref.refs_6_) | copy-start | bytes 388

commit v4 on v3

--- a/solution.py
+++ b/solution.py
@@ -13,9 +13,9 @@
 CEXP = HD**-0.5 * LOG2E
 NEG = -1e30
 HUGE = 2.0**90
-VMEM_LIMIT = 16 << 20
+VMEM_LIMIT = 12 << 20
 POOL_LIMIT = 56 << 20
-FIRST_LIMIT = 22 << 20
+FIRST_LIMIT = 20 << 20
 
 
 NT = (((1,), (1,)), ((), ()))
@@ -38,32 +38,34 @@
     return i ^ k if size & (size - 1) == 0 else lax.rem(i - k + size, size)
 
 
-def gather_pages(kv_pool, fresh_kv, fetch_slots, suffix_route, ks, size, after):
+def gather_pages(kv_pool, fresh_kv, fetch_slots, suffix_route, entries, size, after, halves):
     _, _, page, width = kv_pool.shape
-    n = len(ks)
+    n = len(entries)
+    part = width // halves
     cap, caps = fetch_slots.shape[1] // size, suffix_route.shape[1] // size
     each = cap + caps
 
     def body(slots_ref, routes_ref, pool_ref, fresh_ref, *rest):
         outs, sem = rest[-n - 1 : -1], rest[-1]
         me = lax.axis_index("pool")
-        for i, k in enumerate(ks):
+        for i, (k, half) in enumerate(entries):
             dest = partner(me, k, size)
+            cols = slice(None) if half is None else slice(half * part, (half + 1) * part)
             for c in range(cap):
                 pltpu.make_async_copy(
-                    pool_ref.at[slots_ref[0, dest * cap + c]], outs[i].at[:, c], sem.at[i]
+                    pool_ref.at[slots_ref[0, dest * cap + c], :, :, cols], outs[i].at[:, c], sem.at[i]
                 ).start()
             for c in range(caps):
                 pltpu.make_async_copy(
-                    fresh_ref.at[routes_ref[0, dest * caps + c]], outs[i].at[:, cap + c], sem.at[i]
+                    fresh_ref.at[routes_ref[0, dest * caps + c], :, :, cols], outs[i].at[:, cap + c], sem.at[i]
                 ).start()
         for i in range(n):
             pltpu.make_async_copy(outs[i], outs[i], sem.at[i]).wait()
 
-    shape = (2, each, page, width)
+    shapes = [(2, each, page, width if half is None else part) for _, half in entries]
     return pl.pallas_call(
         body,
-        out_shape=[pltpu.VMEM(shape, kv_pool.dtype)] * n,
+        out_shape=[pltpu.VMEM(shape, kv_pool.dtype) for shape in shapes],
         in_specs=[SM, SM, HBM, HBM] + [ANY] * len(after),
         out_specs=[VM] * n,
         scratch_shapes=[pltpu.SemaphoreType.DMA((n,))],
@@ -86,12 +88,12 @@
     vis_ref[at : at + keys, :] = jnp.broadcast_to(jnp.where(seen, 1.0, 0.0), (keys, HD))
 
 
-def place_keys(k_ref, v_ref, vis_ref, vis_at, at, g, piece, stand_in, cap, page):
+def place_keys(k_ref, v_ref, vis_ref, vis_at, at, column, piece, stand_in, cap, page):
     keys = cap * page
     rows = slice(at, at + keys)
     seen = vis_ref[vis_at : vis_at + keys, :] > 0
-    key = piece[0, 0:cap, :, head_at(g)].reshape(keys, HD).astype(jnp.float32)
-    val = piece[1, 0:cap, :, head_at(g)].reshape(keys, HD).astype(jnp.float32)
+    key = piece[0, 0:cap, :, head_at(column)].reshape(keys, HD).astype(jnp.float32)
+    val = piece[1, 0:cap, :, head_at(column)].reshape(keys, HD).astype(jnp.float32)
     k_ref[rows, 0:HD] = jnp.where(seen, key, stand_in).astype(jnp.bfloat16)
     v_ref[rows, 0:HD] = jnp.where(seen, val, 0.0).astype(jnp.bfloat16)
 
@@ -198,10 +200,12 @@
     v_ref[:, HD:] = vis_ref[...].astype(jnp.bfloat16)
 
 
-def prefill_more(q, fresh, pieces, ks, pages, plen, state, cap, size):
+def prefill_more(q, fresh, pieces, ks, pages, plen, state, cap, size, lo, hi):
     tokens, qwidth = q.shape
     page, width = fresh.shape[2:]
     n = len(pieces)
+    piece_width = pieces[0].shape[3]
+    base = lo if piece_width < width else 0
     keys = n * cap * page
 
     def body(*refs):
@@ -217,7 +221,7 @@
             stand_in = f_ref[0, 0, :, head_at(g)][0:1].astype(jnp.float32)
             for i in range(n):
                 at = i * cap * page
-                place_keys(k_ref, v_ref, vis_ref, at, at, g, got_ref.at[i], stand_in, cap, page)
+                place_keys(k_ref, v_ref, vis_ref, at, at, g - base, got_ref.at[i], stand_in, cap, page)
 
             def emit(cols, acc, total):
                 acc_ref[:, cols] = acc_in[:, cols] + acc
@@ -226,9 +230,9 @@
             add_pages(k_ref, v_ref, q_ref, m_ref, g, emit)
             return carry
 
-        lax.fori_loop(0, width // HD, group, 0)
-
-    work = tokens * keys * (qwidth // HD)
+        lax.fori_loop(lo, hi, group, 0)
+
+    work = tokens * keys * (hi - lo) * GROUP
     wide = pltpu.VMEM((tokens, qwidth), jnp.float32)
     return pl.pallas_call(
         body,
@@ -237,7 +241,7 @@
         out_specs=[VM, VM],
         input_output_aliases={5 + n: 0, 6 + n: 1},
         scratch_shapes=[
-            pltpu.VMEM((n, 2, cap, page, width), q.dtype),
+            pltpu.VMEM((n, 2, cap, page, piece_width), q.dtype),
             pltpu.SemaphoreType.DMA((n,)),
             pltpu.VMEM((keys, HD), jnp.float32),
             pltpu.VMEM((keys, 2 * HD), jnp.bfloat16),
@@ -379,82 +383,103 @@
     )(dec_q, *state, full, part, rest, *pieces)
 
 
-def finish(dec_q, dec_state, times, q, fresh, pages, plen, state, pieces, ks, last, cap, size):
+def finish(dec_q, dec_state, times, q, fresh, pages, plen, state, sums, split, tail, lo, hi, before, arrived, cap, size):
     page, width = fresh.shape[2:]
-    caps = pieces[0].shape[1] - cap
+    ks = list(split)
+    piece_width = split[ks[0]].shape[3]
+    caps = split[ks[0]].shape[1] - cap
     requests = dec_q.shape[0]
     heads_kv = width // HD
-    tokens, qwidth = q.shape
-    n, tail = len(pieces), len(last)
+    tokens, _ = q.shape
+    n = len(ks)
     keys = cap * page
     rows = min(128, tokens)
-    held = n * keys
+    last = before is not None or hi - lo == heads_kv
+    names = list(arrived) if last else []
+    distances = sorted({k for k, _ in names})
+    held = len(distances) * keys
+    span = GROUP * HD
 
     def body(*refs):
         dq_ref, dacc_ref, dm_ref, dl_ref, times_ref, q_ref, f_ref, pages_ref, plen_ref = refs[:9]
-        m_ref, acc_ref, l_ref = refs[9:12]
-        last_refs = refs[12 : 12 + tail]
-        piece_refs = refs[12 + tail : 12 + tail + n]
-        (dec_ref, out_hbm, out_ref, sem, got_ref, got_sem, vis_ref, k_ref, v_ref, all_vis, all_k, all_v, page_ref, block_ref) = (
-            refs[12 + tail + n :]
-        )
-        copies = fetch_pages(last_refs, got_ref, got_sem, cap + caps)
-        start_pages(vis_ref, k_ref, v_ref, pages_ref, plen_ref, last, cap, page, size)
+        m_ref, acc_ref, l_ref, sums_ref = refs[9:13]
+        split_refs = refs[13 : 13 + n]
+        piece_refs = dict(zip(names, refs[13 + n : 13 + n + len(names)]))
+        refs = refs[13 + n + len(names) + (0 if before is None else 2) :]
+        dec_hbm, out_hbm, sums_out, dec_ref, out_ref, sem, got_ref, got_sem, vis_ref, k_ref, v_ref = refs[:11]
+        copies = fetch_pages(split_refs, got_ref, got_sem, cap + caps)
+        start_pages(vis_ref, k_ref, v_ref, pages_ref, plen_ref, tail, cap, page, size)
         for copy in copies:
             copy.wait()
 
         def out_copy(g):
-            cols = pl.ds(pl.multiple_of(g * GROUP * HD, GROUP * HD), GROUP * HD)
-            return pltpu.make_async_copy(out_ref.at[:, cols], out_hbm.at[:, cols], sem.at[g])
+            mine = pl.ds(pl.multiple_of((g - lo) * span, span), span)
+            cols = pl.ds(pl.multiple_of(g * span, span), span)
+            return pltpu.make_async_copy(out_ref.at[:, mine], out_hbm.at[:, cols], sem.at[g - lo])
 
         def group(g, sums):
             stand_in = f_ref[0, 0, :, head_at(g)][0:1].astype(jnp.float32)
-            for i in range(tail):
-                place_keys(k_ref, v_ref, vis_ref, i * keys, i * keys, g, got_ref.at[i], stand_in, cap, page)
+            for i, k in enumerate(tail):
+                place_keys(
+                    k_ref, v_ref, vis_ref, i * keys, i * keys, g - lo, got_ref.at[ks.index(k)], stand_in, cap, page
+                )
             partial = []
 
             def emit(cols, acc, total):
+                mine = head_at((g - lo) * GROUP + len(partial))
                 total = l_ref[:, cols] + total
-                out_ref[:, cols] = ((acc_ref[:, cols] + acc) * pl.reciprocal(total)).astype(out_ref.dtype)
+                out_ref[:, mine] = ((acc_ref[:, cols] + acc) * pl.reciprocal(total)).astype(out_ref.dtype)
                 partial.append(jnp.sum(total.reshape(-1, 8, HD), axis=0))
 
             add_pages(k_ref, v_ref, q_ref, m_ref, g, emit)
             out_copy(g).start()
             return sum(partial, sums)
 
-        sums = lax.fori_loop(0, heads_kv, group, jnp.zeros((8, HD), jnp.float32))
+        sums = lax.fori_loop(lo, hi, group, sums_ref[...])
+        sums_out[...] = sums
 
         times = times_ref[...]
-        for g in range(heads_kv):
-            cols = slice(g * HD, (g + 1) * HD)
-            key = jnp.concatenate([fresh_rows(got_ref.at[i], 0, cap, cols) for i in range(tail)], 0)
-            val = jnp.concatenate([fresh_rows(got_ref.at[i], 1, cap, cols) for i in range(tail)], 0)
+        for g in range(lo, hi):
+            cols = slice((g - lo) * HD, (g - lo + 1) * HD)
+            key = jnp.concatenate([fresh_rows(got_ref.at[i], 0, cap, cols) for i in range(n)], 0)
+            val = jnp.concatenate([fresh_rows(got_ref.at[i], 1, cap, cols) for i in range(n)], 0)
             _, l, acc = decode_fold(
                 dq_ref, g, key, val, times, dm_ref[g, :, 0:1], dl_ref[g, :, 0:1], dacc_ref[g]
             )
             done = (acc / l).astype(dec_ref.dtype)
             for h in range(GROUP):
-                at = (g * GROUP + h) * HD
+                at = ((g - lo) * GROUP + h) * HD
                 dec_ref[:, at : at + HD] = done[h * requests : (h + 1) * requests]
-        for g in range(heads_kv):
+        dec_copy = pltpu.make_async_copy(dec_ref, dec_hbm.at[:, lo * span : hi * span], sem.at[hi - lo])
+        dec_copy.start()
+        dec_copy.wait()
+        for g in range(lo, hi):
             out_copy(g).wait()
+        if not last:
+            return
+        all_vis, all_k, all_v, page_ref, half_ref, block_ref = refs[11:]
 
         @pl.when(jnp.logical_not(jnp.sum(sums) <= HUGE))
         def _():
-            for i, k in enumerate(ks):
+            for i, k in enumerate(distances):
                 mark_visible(all_vis, i * keys, k, cap, page, pages_ref, plen_ref, size)
             all_v[0:tokens, HD:] = jnp.ones((tokens, HD), jnp.bfloat16)
             all_v[tokens:, HD:] = all_vis[...].astype(jnp.bfloat16)
             col = lax.broadcasted_iota(jnp.int32, (rows, tokens), 1)
             row = lax.broadcasted_iota(jnp.int32, (rows, tokens), 0)
-
-            def again(g, carry):
+            step = hi - lo
+
+            def again(half, g, carry):
                 all_k[0:tokens, :] = f_ref[:, 0, :, head_at(g)].reshape(tokens, HD)
                 all_v[0:tokens, 0:HD] = f_ref[:, 1, :, head_at(g)].reshape(tokens, HD)
                 stand_in = f_ref[0, 0, :, head_at(g)][0:1].astype(jnp.float32)
-                for i in range(n):
-                    pltpu.sync_copy(piece_refs[i].at[:, 0:cap], page_ref)
-                    place_keys(all_k, all_v, all_vis, i * keys, tokens + i * keys, g, page_ref, stand_in, cap, page)
+                for i, k in enumerate(distances):
+                    whole = (k, None) in piece_refs
+                    ref = piece_refs[(k, None if whole else half)]
+                    into = page_ref if whole else half_ref
+                    pltpu.sync_copy(ref.at[:, 0:cap], into)
+                    column = g if whole else g - half * step
+                    place_keys(all_k, all_v, all_vis, i * keys, tokens + i * keys, column, into, stand_in, cap, page)
 
                 def block(b, carry):
                     r = pl.multiple_of((b % (tokens // rows)) * rows, rows)
@@ -470,45 +495,71 @@
                     pltpu.sync_copy(block_ref, out_hbm.at[pl.ds(r, rows), cols])
                     return carry
 
-                return lax.fori_loop(0, GROUP * (tokens // rows), block, carry)
-
-            lax.fori_loop(0, heads_kv, again, 0)
-
-    work = tokens * tail * keys * (qwidth // HD)
+                lax.fori_loop(0, GROUP * (tokens // rows), block, 0)
+                return carry
+
+            for half in range(heads_kv // step):
+                lax.fori_loop(half * step, (half + 1) * step, functools.partial(again, half), 0)
+
+    work = tokens * len(tail) * keys * (hi - lo) * GROUP
+    scratch = [
+        pltpu.VMEM((requests, (hi - lo) * span), dec_q.dtype),
+        pltpu.VMEM((tokens, (hi - lo) * span), q.dtype),
+        pltpu.SemaphoreType.DMA((hi - lo + 1,)),
+        pltpu.VMEM((n, 2, cap + caps, page, piece_width), q.dtype),
+        pltpu.SemaphoreType.DMA((n,)),
+        pltpu.VMEM((len(tail) * keys, HD), jnp.float32),
+        pltpu.VMEM((len(tail) * keys, 2 * HD), jnp.bfloat16),
+        pltpu.VMEM((len(tail) * keys, 2 * HD), jnp.bfloat16),
+    ]
+    if last:
+        scratch += [
+            pltpu.VMEM((held, HD), jnp.float32),
+            pltpu.VMEM((tokens + held, HD), jnp.bfloat16),
+            pltpu.VMEM((tokens + held, 2 * HD), jnp.bfloat16),
+            pltpu.VMEM((2, cap, page, width), q.dtype),
+            pltpu.VMEM((2, cap, page, piece_width), q.dtype),
+            pltpu.VMEM((rows, HD), q.dtype),
+        ]
+    operands = [dec_q, *dec_state, times, q, fresh, pages, plen, *state, sums, *split.values()]
+    operands += [arrived[name] for name in names]
+    aliases = {}
+    if before is not None:
+        aliases = {len(operands): 0, len(operands) + 1: 1}
+        operands += list(before)
     return pl.pallas_call(
         body,
         out_shape=[
             jax.ShapeDtypeStruct(dec_q.shape, dec_q.dtype),
             jax.ShapeDtypeStruct(q.shape, q.dtype),
+            jax.ShapeDtypeStruct(sums.shape, sums.dtype),
         ],
-        in_specs=[VM] * 8 + [SM] + [VM] * 3 + [ANY] * (tail + n),
-        out_specs=[VM, ANY],
-        scratch_shapes=[
-            pltpu.VMEM(q.shape, q.dtype),
-            pltpu.SemaphoreType.DMA((heads_kv,)),
-            pltpu.VMEM((tail, 2, cap + caps, page, width), q.dtype),
-            pltpu.SemaphoreType.DMA((tail,)),
-            pltpu.VMEM((tail * keys, HD), jnp.float32),
-            pltpu.VMEM((tail * keys, 2 * HD), jnp.bfloat16),
-            pltpu.VMEM((tail * keys, 2 * HD), jnp.bfloat16),
-            pltpu.VMEM((held, HD), jnp.float32),
-            pltpu.VMEM((tokens + held, HD), jnp.bfloat16),
-            pltpu.VMEM((tokens + held, 2 * HD), jnp.bfloat16),
-            pltpu.VMEM((2, cap, page, width), q.dtype),
-            pltpu.VMEM((rows, HD), q.dtype),
-        ],
+        in_specs=[VM] * 8 + [SM] + [VM] * 4 + [ANY] * (len(operands) - 13),
+        out_specs=[ANY, ANY, VM],
+        input_output_aliases=aliases,
+        scratch_shapes=scratch,
         compiler_params=PARAMS,
         cost_estimate=pl.CostEstimate(
             flops=8 * HD * work, transcendentals=work, bytes_accessed=8 * work // HD
         ),
         name="finish",
-    )(dec_q, *dec_state, times, q, fresh, pages, plen, *state, *[pieces[ks.index(k)] for k in last], *pieces)
+    )(*operands)
+
+
+def halves_of(width):
+    return 2 if (width // HD) % 2 == 0 else 1
 
 
 def send_order(size):
     if size == 16:
-        return [12, 8, 1, 2, 3, 4, 13, 5, 9, 6, 14, 7, 10, 15, 11]
-    return list(range(1, size))
+        return [12, 8, 1, 2, 3, 4, 13, 5, 9, 6, 7], [14, 10, 15, 11]
+    cut = size - max(1, size // 4)
+    return list(range(1, cut)), list(range(cut, size))
+
+
+def send_entries(size, halves):
+    sends, split = send_order(size)
+    return [(k, None) for k in sends] + [(k, half) for half in range(halves) for k in split]
 
 
 def shards(
@@ -528,18 +579,20 @@
     slots = kv_pool.shape[0]
     cap = fetch_slots.shape[1] // size
     caps = suffix_route.shape[1] // size
-    sends = send_order(size)
+    halves = halves_of(kv_pool.shape[3])
+    sends, split = send_order(size)
+    entries = send_entries(size, halves)
     lead = max(1, size // 8)
-    batches = [sends[:lead], sends[lead:] + [0]]
+    batches = [entries[:lead], entries[lead:] + [(0, None)]]
     outgoing, after = {}, []
-    for ks in batches:
-        outs = gather_pages(kv_pool, fresh_kv, fetch_slots, suffix_route, ks, size, after)
+    for batch in batches:
+        outs = gather_pages(kv_pool, fresh_kv, fetch_slots, suffix_route, batch, size, after, halves)
         after = outs[:1]
-        outgoing |= dict(zip(ks, outs, strict=True))
-    arrived = {0: outgoing[0]}
-    for k in sends:
+        outgoing |= dict(zip(batch, outs, strict=True))
+    arrived = {(0, None): outgoing[(0, None)]}
+    for k, half in entries:
         pairs = [(i, i ^ k if size & (size - 1) == 0 else (i + k) % size) for i in range(size)]
-        arrived[k] = lax.ppermute(outgoing[k], "pool", pairs)
+        arrived[(k, half)] = lax.ppermute(outgoing[(k, half)], "pool", pairs)
 
     context = dec_pages.shape[1]
     position = jnp.arange(context, dtype=jnp.int32)[None, :]
@@ -553,9 +606,8 @@
         part = jnp.sum((same & edge_page[:, :, None]).astype(jnp.float32), 1).astype(jnp.bfloat16)
         return full, part
 
-    groups = arrival_groups([0] + sends)
-    order = [k for ks in groups for k in ks]
-    early, last = order[: -len(groups[-1])], groups[-1]
+    groups = arrival_groups(sends)
+    early, last = [k for ks in groups for k in ks], split
     me = lax.axis_index("pool")
 
     def fresh_names(ks):
@@ -571,7 +623,7 @@
     state = prefill_first(
         suffix_q,
         fresh_kv,
-        [arrived[k] for k in groups[0]],
+        [arrived[(k, None)] for k in groups[0]],
         groups[0],
         prefix_pages,
         prefix_len,
@@ -579,38 +631,57 @@
         cap,
         size,
     )
-    for ks in groups[1:-1]:
+
+    def more(state, ks, half, lo, hi):
+        pieces = [arrived[(k, half)] for k in ks]
         new = prefill_more(
-            suffix_q, fresh_kv, [arrived[k] for k in ks], ks, prefix_pages, prefix_len, state, cap, size
+            suffix_q, fresh_kv, pieces, ks, prefix_pages, prefix_len, state, cap, size, lo, hi
         )
-        state = (state[0], *new)
+        return (state[0], *new)
+
+    heads_kv = kv_pool.shape[3] // HD
+    for ks in groups[1:]:
+        state = more(state, ks, None, 0, heads_kv)
     dec_state = decode_fresh(
-        dec_q, [arrived[k] for k in early], dec_state, *counts(fresh_names(early)), rest, cap
+        dec_q, [arrived[(k, None)] for k in early], dec_state, *counts(fresh_names(early)), rest, cap
     )
-    decode_out, suffix_out = finish(
-        dec_q,
-        dec_state,
-        last_times,
-        suffix_q,
-        fresh_kv,
-        prefix_pages,
-        prefix_len,
-        state,
-        [arrived[k] for k in order],
-        order,
-        last,
-        cap,
-        size,
-    )
+    before, sums = None, jnp.zeros((8, HD), jnp.float32)
+    per = heads_kv // halves
+    for half in range(halves):
+        lo, hi = half * per, (half + 1) * per
+        tail = split
+        if half == halves - 1 and len(split) > 1:
+            tail = split[len(split) // 2 :]
+            state = more(state, split[: len(split) // 2], half, lo, hi)
+        *before, sums = finish(
+            dec_q,
+            dec_state,
+            last_times,
+            suffix_q,
+            fresh_kv,
+            prefix_pages,
+            prefix_len,
+            state,
+            sums,
+            {k: arrived[(k, half)] for k in split},
+            tail,
+            lo,
+            hi,
+            before,
+            arrived,
+            cap,
+            size,
+        )
+    decode_out, suffix_out = before
     return (suffix_out, decode_out)
 
 
-def arrival_groups(order):
-    size = len(order)
-    if size == 16:
-        return [[0, 1, 2, 3, 12, 4, 8, 5], [13, 6, 9, 7], [14, 10], [15, 11]]
-    per = -(-size // 4)
-    return [order[i : min(i + per, size - 1)] for i in range(0, size - 1, per)] + [order[-1:]]
+def arrival_groups(sends):
+    if len(sends) == 11:
+        return [[0, 1, 2, 3, 12, 4, 8, 5], [13, 6, 9, 7]]
+    order = [0] + sends
+    cut = 2 * len(order) // 3
+    return [order[:cut], order[cut:]]
 
 
 def solution(mesh):

time: 150 us -> 165 us (1.10)
  starting transfers between devices: 27.1 us -> 43.4 us
  waiting for transfers between devices: 24.1 us -> 11.3 us
  local copies, waits for them, and re-layouts: 8.08 us -> 20.3 us
    ppermute x15 -> x19, starting transfers between devices: 27.1 us -> 43.4 us  [shards(): arrived[k, half] = lax.ppermute(outgoing[k, half], 'pool', pairs)]
    ppermute x15 -> x19, waiting for transfers between devices: 24.1 us -> 11.3 us  [shards(): arrived[k, half] = lax.ppermute(outgoing[k, half], 'pool', pairs)]
    unnamed x48 -> x84, local copies, waits for them, and re-layouts: 7.07 us -> 19.3 us
    pallas_call x1 -> x2, Pallas kernels: 9.32 us -> 14.2 us  [finish(): pl.pallas_call(body, out_shape=[jax.ShapeDtypeStruct(dec_q.shape, dec_q.d...]
    pallas_call x2, Pallas kernels: 20.5 us -> 16.8 us  [prefill_more(): pl.pallas_call(body, out_shape=[wide, wide], in_specs=[SM, VM, VM, VM] +...]
  transfers between devices with their start and end apart: 15 -> 19, of which waited for: 3 -> 4; matrix products, arithmetic and copies ran while one was open for 3% -> 3% of each run, Pallas kernels for 48% -> 46%
where the time goes in v4:
time: 165 us; the launch traced here: 164 us
  Pallas kernels  83.2 us (50%)
  starting transfers between devices  43.4 us (26%)
  local copies, waits for them, and re-layouts  20.3 us (12%)
  waiting for transfers between devices  11.3 us (7%)
  other arithmetic  3.8 us (2%)
  between operations  1.83 us (1%)
    ppermute x19, starting transfers between devices, shards(): arrived[k, half] = lax.ppermute(outgoing[k, half], 'pool', pairs)  43.4 us
    pallas_call x1, Pallas kernels, prefill_first(): pl.pallas_call(body, out_shape=[pltpu.VMEM((tokens, qwidth), jnp.bfloat16...  30.1 us
    unnamed x84, local copies, waits for them, and re-layouts  19.3 us
    pallas_call x2, Pallas kernels, prefill_more(): pl.pallas_call(body, out_shape=[wide, wide], in_specs=[SM, VM, VM, VM] +...  16.8 us
    pallas_call x2, Pallas kernels, finish(): pl.pallas_call(body, out_shape=[jax.ShapeDtypeStruct(dec_q.shape, dec_q.d...  14.2 us
    pallas_call x1, Pallas kernels, decode_pool(): pl.pallas_call(body, grid=(steps,), out_shape=[jax.ShapeDtypeStruct(shape...  13.8 us
    ppermute x19, waiting for transfers between devices, shards(): arrived[k, half] = lax.ppermute(outgoing[k, half], 'pool', pairs)  11.3 us
    pallas_call x2, Pallas kernels, gather_pages(): pl.pallas_call(body, out_shape=[pltpu.VMEM(shape, kv_pool.dtype) for shap...  6.46 us
  transfers between devices with their start and end apart: 19, of which 4 were waited for; matrix products, arithmetic and copies ran while one was open for 3% of the time, Pallas kernels for 46%

profile of v4, /device:TPU:0, one launch (start us, length us, event | category | flops | bytes accessed | tf_op | source)
XLA Modules:
  0.0 163.9 jit_solution(11941522757146949513)
XLA Ops:
  0.6 1.8 %gather_pages.2 = (bf16[2,20,8,512]{3,2,1,0:T(8,128)(2,1)S(1)}, bf16[2,20,8,512]{3,2,1,0:T(8,128)(2,1)S(1)}) custom-call(s32[1,256]{1,0:T(1,128)} %slots_ref.3, s32[1,64]{1,0:T(1,128)} %routes_ref.3, bf16[512,2,8,512]{3,2,1,0:T(8,128)(2,1)} %pool_ref.3, bf16[64,2,8,512]{3,2,1,0:T(8,128)(2,1)} %refs_6_.3), custom_call_target="tpu_custom_call" | custom-call | bytes 1310720 | tf_op jit(solution)/shard_map/gather_pages/pallas_call | solution.py:66
  2.4 4.1 %collective-permute-start.5 = (bf16[2,20,8,512]{3,2,1,0:T(8,128)(2,1)S(1)}, bf16[2,20,8,512]{3,2,1,0:T(8,128)(2,1)S(1)}, u32[]{:S(2)}, u32[]{:S(2)}) collective-permute-start(bf16[2,20,8,512]{3,2,1,0:T(8,128)(2,1)S(1)} %get-tuple-element.50), channel_id=1, source_target_pairs={{0,8},{1,9},{2,10},{3,11},{4,12},{5,13},{6,14},{7,15},{8,0},{9,1},... | collective-permute-start | bytes 983048 | tf_op jit(solution)/shard_map/ppermute | solution.py:595
  6.5 1.4 collective-permute-start.3
  8.0 4.7 %gather_pages.3 = (bf16[2,20,8,512]{3,2,1,0:T(8,128)(2,1)}, bf16[2,20,8,512]{3,2,1,0:T(8,128)(2,1)}, bf16[2,20,8,512]{3,2,1,0:T(8,128)(2,1)S(1)}, bf16[2,20,8,51...) custom-call(s32[1,256]{1,0:T(1,128)} %slots_ref.3, ...), custom_call_target="tpu_custom_call" | custom-call | bytes 11796480 | tf_op jit(solution)/shard_map/gather_pages/pallas_call | solution.py:66
  12.7 0.7 copy-done.6
  13.4 0.7 copy-done.24
  14.1 0.7 copy-done.26
  14.7 0.7 copy-done.28
  15.4 0.7 copy-done.30
  16.1 0.7 copy-done.32
  16.7 0.7 copy-done.34
  17.4 0.7 copy-done.36
  18.0 1.5 collective-permute-start.1
  19.5 0.4 collective-permute-start.2
  20.6 0.1 iota_add_fusion.1
  20.7 0.1 add.89
  20.8 0.1 broadcast_in_dim.19
  20.9 0.1 eq.72
  21.0 0.1 iota_add_fusion
  21.0 0.1 add.86
  21.1 0.7 copy.24.rest_ref.refs_6_
  21.8 0.1 iota_compare_fusion.1
  21.9 0.1 broadcast_add_fusion
  22.0 0.5 convert_reduce_fusion.2.refs_4_
  22.5 2.4 %convert_reduce_fusion = (bf16[32,512]{1,0:T(8,128)(2,1)}, bf16[32,512]{1,0:T(8,128)(2,1)}) fusion(s32[32,64]{1,0:T(8,128)S(1)} %copy-done.38, pred[32,64]{1,0:T(8,128)(4,1)S(1)} %get-tuple-element.86, pred[32,64]{1,0:T(8,128)(4,1)S(1)} %get-tuple-element.87), kind=kLoop, calls=%fused_computation | loop fusion | flops 7307264 | bytes 77824 | tf_op jit(solution)/shard_map/reduce_sum | solution.py:606
  24.9 4.2 %collective-permute-done.5.refs_13_.refs_10_.refs_19_ = bf16[2,20,8,512]{3,2,1,0:T(8,128)(2,1)S(1)} collective-permute-done((bf16[2,20,8,512]{3,2,1,0:T(8,128)(2,1)S(1)}, bf16[2,20,8,512]{3,2,1,0:T(8,128)(2,1)S(1)}, u32[]{:S(2)}, u32[]{:S(2)}) %collective-permute-start.5) | collective-permute-done | bytes 327712 | tf_op jit(solution)/shard_map/ppermute | solution.py:595
  29.1 6.5 %collective-permute-start.6 = (bf16[2,20,8,512]{3,2,1,0:T(8,128)(2,1)S(1)}, bf16[2,20,8,512]{3,2,1,0:T(8,128)(2,1)S(1)}, u32[]{:S(2)}, u32[]{:S(2)}) collective-permute-start(bf16[2,20,8,512]{3,2,1,0:T(8,128)(2,1)S(1)} %get-tuple-element.51), channel_id=1, source_target_pairs={{0,5},{1,4},{2,7},{3,6},{4,1},{5,0},{6,3},{7,2},{8,13},{9,12},{10,... | collective-permute-start | bytes 983048 | tf_op jit(solution)/shard_map/ppermute | solution.py:595
  35.7 0.6 convert_reduce_fusion.3
  36.2 13.8 %decode_pool.1 = (f32[4,256,128]{2,1,0:T(8,128)}, f32[4,256,128]{2,1,0:T(8,128)}, f32[4,256,128]{2,1,0:T(8,128)}, s32[1]{0:T(128)}) custom-call(bf16[32,4096]{1,0:T(8,128)(2,1)} %refs_0_.8, bf16[512,2,8,512]{3,2,1,0:T(8,128)(2,1)} %pool_ref.3, bf16[32,512]{1,0:T(8,128)(2,1)} %get-tuple-element.83.full_ref, bf16[32,512]{1,0:T(8,128)(2,1)} %get-tuple-element.82.part_ref, ...), custom_call_target="tpu_custom_call" | custom-call | flops 2147483648 | bytes 8388608 | tf_op jit(solution)/shard_map/decode_pool/pallas_call | solution.py:317
  50.1 0.7 copy-done.8
  50.8 4.3 %collective-permute-start.11 = (bf16[2,20,8,256]{3,2,1,0:T(8,128)(2,1)}, bf16[2,20,8,256]{3,2,1,0:T(8,128)(2,1)S(1)}, u32[]{:S(2)}, u32[]{:S(2)}) collective-permute-start(bf16[2,20,8,256]{3,2,1,0:T(8,128)(2,1)} %get-tuple-element.61), channel_id=1, source_target_pairs={{0,14},{1,15},{2,12},{3,13},{4,10},{5,11},{6,8},{7,9},{8,6},{9,7},... | collective-permute-start | bytes 491528 | tf_op jit(solution)/shard_map/ppermute | solution.py:595
  55.1 0.7 copy-done.10
  55.9 0.3 collective-permute-start.7
  56.1 0.7 copy-done.12
  56.9 0.7 copy-done.14
  57.6 3.5 %collective-permute-start.9 = (bf16[2,20,8,512]{3,2,1,0:T(8,128)(2,1)}, bf16[2,20,8,512]{3,2,1,0:T(8,128)(2,1)S(1)}, u32[]{:S(2)}, u32[]{:S(2)}) collective-permute-start(bf16[2,20,8,512]{3,2,1,0:T(8,128)(2,1)} %get-tuple-element.54), channel_id=1, source_target_pairs={{0,9},{1,8},{2,11},{3,10},{4,13},{5,12},{6,15},{7,14},{8,1},{9,0},... | collective-permute-start | bytes 983048 | tf_op jit(solution)/shard_map/ppermute | solution.py:595
  61.2 0.7 copy-done.16
  61.9 0.1 collective-permute-start.10
  62.0 2.2 %copy-done = bf16[512,4096]{1,0:T(8,128)(2,1)S(1)} copy-done((bf16[512,4096]{1,0:T(8,128)(2,1)S(1)}, bf16[512,4096]{1,0:T(8,128)(2,1)}, u32[]{:S(2)}) %copy-start) | copy-done | bytes 4194328
  64.2 1.2 copy-done.2
  65.4 1.0 copy-done.5
  66.4 1.0 copy-done.7
  67.3 1.0 copy-done.9
  68.3 1.0 copy-done.11
  69.3 1.0 copy-done.13
  70.3 1.0 copy-done.15
  71.2 1.0 copy-done.17
  72.2 30.1 %prefill_first.1 = (bf16[512,4096]{1,0:T(8,128)(2,1)S(1)}, f32[512,4096]{1,0:T(8,128)S(1)}, f32[512,4096]{1,0:T(8,128)S(1)}) custom-call(s32[1]{0:T(128)S(6)} %copy.32.refs_0_.refs_8_, s32[1,256]{1,0:T(1,128)S(1)} %copy-done.23, bf16[512,4096]{1,0:T(8,128)(2,1)S(1)} %copy-done, bf16[64,2,8,512]{3,2,1,0:T(8,128)(2,1)S(1)} %copy-done.2, ...), custom_call_target="tpu_custom_call" | custom-call | flops 21474836480 | bytes 1310720 | tf_op jit(solution)/shard_map/prefill_first/pallas_call | solution.py:166
  102.4 2.3 %collective-permute-start.13 = (bf16[2,20,8,256]{3,2,1,0:T(8,128)(2,1)S(1)}, bf16[2,20,8,256]{3,2,1,0:T(8,128)(2,1)S(1)}, u32[]{:S(2)}, u32[]{:S(2)}) collective-permute-start(bf16[2,20,8,256]{3,2,1,0:T(8,128)(2,1)S(1)} %copy-done.37), channel_id=1, source_target_pairs={{0,14},{1,15},{2,12},{3,13},{4,10},{5,11},{6,8},{7,9},{8,6},{9,7},... | collective-permute-start | bytes 491528 | tf_op jit(solution)/shard_map/ppermute | solution.py:595
  104.7 3.0 %collective-permute-start.14 = (bf16[2,20,8,256]{3,2,1,0:T(8,128)(2,1)S(1)}, bf16[2,20,8,256]{3,2,1,0:T(8,128)(2,1)S(1)}, u32[]{:S(2)}, u32[]{:S(2)}) collective-permute-start(bf16[2,20,8,256]{3,2,1,0:T(8,128)(2,1)S(1)} %copy-done.35), channel_id=1, source_target_pairs={{0,10},{1,11},{2,8},{3,9},{4,14},{5,15},{6,12},{7,13},{8,2},{9,3},... | collective-permute-start | bytes 491528 | tf_op jit(solution)/shard_map/ppermute | solution.py:595
  107.8 0.3 collective-permute-start.15
  108.1 1.7 %collective-permute-start.16 = (bf16[2,20,8,256]{3,2,1,0:T(8,128)(2,1)S(1)}, bf16[2,20,8,256]{3,2,1,0:T(8,128)(2,1)S(1)}, u32[]{:S(2)}, u32[]{:S(2)}) collective-permute-start(bf16[2,20,8,256]{3,2,1,0:T(8,128)(2,1)S(1)} %copy-done.31), channel_id=1, source_target_pairs={{0,11},{1,10},{2,9},{3,8},{4,15},{5,14},{6,13},{7,12},{8,3},{9,2},... | collective-permute-start | bytes 491528 | tf_op jit(solution)/shard_map/ppermute | solution.py:595
  109.9 12.3 %prefill_more.2 = (f32[512,4096]{1,0:T(8,128)S(1)}, f32[512,4096]{1,0:T(8,128)S(1)}) custom-call(s32[1]{0:T(128)S(6)} %copy.32.refs_0_.refs_8_, s32[1,256]{1,0:T(1,128)S(1)} %copy-done.23, bf16[512,4096]{1,0:T(8,128)(2,1)S(1)} %copy-done, bf16[64,2,8,512]{3,2,1,0:T(8,128)(2,1)S(1)} %copy-done.2, ...), custom_call_target="tpu_custom_call", output_to_operand_aliasing={{0}: (9, {}), {1}: (10, {})} | custom-call | flops 8589934592 | bytes 524288 | tf_op jit(solution)/shard_map/prefill_more/pallas_call | solution.py:237
  122.3 1.7 %decode_fresh.1 = (f32[4,256,128]{2,1,0:T(8,128)S(1)}, f32[4,256,128]{2,1,0:T(8,128)S(1)}, f32[4,256,128]{2,1,0:T(8,128)S(1)}) custom-call(bf16[32,4096]{1,0:T(8,128)(2,1)S(1)} %copy-done.3, f32[4,256,128]{2,1,0:T(8,128)S(1)} %copy-done.18, f32[4,256,128]{2,1,0:T(8,128)S(1)} %copy-done.19, f32[4,256,128]{2,1,0:T(8,128)S(1)} %copy-done.20, ...), custom_call_target="tpu_custom_call" | custom-call | flops 201326592 | bytes 786432 | tf_op jit(solution)/shard_map/decode_fresh/pallas_call | solution.py:369
  124.0 2.9 %collective-permute-start.12 = (bf16[2,20,8,256]{3,2,1,0:T(8,128)(2,1)S(1)}, bf16[2,20,8,256]{3,2,1,0:T(8,128)(2,1)S(1)}, u32[]{:S(2)}, u32[]{:S(2)}) collective-permute-start(bf16[2,20,8,256]{3,2,1,0:T(8,128)(2,1)S(1)} %copy-done.29), channel_id=1, source_target_pairs={{0,10},{1,11},{2,8},{3,9},{4,14},{5,15},{6,12},{7,13},{8,2},{9,3},... | collective-permute-start | bytes 491528 | tf_op jit(solution)/shard_map/ppermute | solution.py:595
  126.8 2.4 %collective-permute-done.14.refs_14_.refs_30_ = bf16[2,20,8,256]{3,2,1,0:T(8,128)(2,1)S(1)} collective-permute-done((bf16[2,20,8,256]{3,2,1,0:T(8,128)(2,1)S(1)}, bf16[2,20,8,256]{3,2,1,0:T(8,128)(2,1)S(1)}, u32[]{:S(2)}, u32[]{:S(2)}) %collective-permute-start.14) | collective-permute-done | bytes 163872 | tf_op jit(solution)/shard_map/ppermute | solution.py:595
  129.3 0.4 collective-permute-start.17
  129.7 10.7 %collective-permute-start.18 = (bf16[2,20,8,256]{3,2,1,0:T(8,128)(2,1)S(1)}, bf16[2,20,8,256]{3,2,1,0:T(8,128)(2,1)S(1)}, u32[]{:S(2)}, u32[]{:S(2)}) collective-permute-start(bf16[2,20,8,256]{3,2,1,0:T(8,128)(2,1)S(1)} %copy-done.25), channel_id=1, source_target_pairs={{0,11},{1,10},{2,9},{3,8},{4,15},{5,14},{6,13},{7,12},{8,3},{9,2},... | collective-permute-start | bytes 491528 | tf_op jit(solution)/shard_map/ppermute | solution.py:595
  140.3 2.8 %collective-permute-done.16.refs_16_.refs_32_ = bf16[2,20,8,256]{3,2,1,0:T(8,128)(2,1)S(1)} collective-permute-done((bf16[2,20,8,256]{3,2,1,0:T(8,128)(2,1)S(1)}, bf16[2,20,8,256]{3,2,1,0:T(8,128)(2,1)S(1)}, u32[]{:S(2)}, u32[]{:S(2)}) %collective-permute-start.16) | collective-permute-done | bytes 163872 | tf_op jit(solution)/shard_map/ppermute | solution.py:595
  143.1 7.8 %finish.2 = (bf16[32,4096]{1,0:T(8,128)(2,1)}, bf16[512,4096]{1,0:T(8,128)(2,1)}, f32[8,128]{1,0:T(8,128)S(1)}) custom-call(bf16[32,4096]{1,0:T(8,128)(2,1)S(1)} %copy-done.3, f32[4,256,128]{2,1,0:T(8,128)S(1)} %get-tuple-element.56.refs_1_, f32[4,256,128]{2,1,0:T(8,128)S(1)} %get-tuple-element.57.refs_2_, f32[4,256,128]{2,1,0:T(8,128)S(1)} %get-tuple-element.58.refs_3_, ...), custom_call_target="tpu_custom_call" | custom-call | flops 4294967296 | bytes 262144 | tf_op jit(solution)/shard_map/finish/pallas_call | solution.py:530
  150.9 0.0 copy-start.1
  150.9 4.5 %prefill_more.3 = (f32[512,4096]{1,0:T(8,128)S(1)}, f32[512,4096]{1,0:T(8,128)S(1)}) custom-call(s32[1]{0:T(128)S(6)} %copy.32.refs_0_.refs_8_, s32[1,256]{1,0:T(1,128)S(1)} %copy-done.23, bf16[512,4096]{1,0:T(8,128)(2,1)S(1)} %copy-done, bf16[64,2,8,512]{3,2,1,0:T(8,128)(2,1)S(1)} %copy-done.2, ...), custom_call_target="tpu_custom_call", output_to_operand_aliasing={{0}: (7, {}), {1}: (8, {})} | custom-call | flops 2147483648 | bytes 131072 | tf_op jit(solution)/shard_map/prefill_more/pallas_call | solution.py:237
  155.4 1.8 %collective-permute-done.18.refs_16_.refs_36_ = bf16[2,20,8,256]{3,2,1,0:T(8,128)(2,1)S(1)} collective-permute-done((bf16[2,20,8,256]{3,2,1,0:T(8,128)(2,1)S(1)}, bf16[2,20,8,256]{3,2,1,0:T(8,128)(2,1)S(1)}, u32[]{:S(2)}, u32[]{:S(2)}) %collective-permute-start.18) | collective-permute-done | bytes 163872 | tf_op jit(solution)/shard_map/ppermute | solution.py:595
  157.2 6.5 %finish.3 = (bf16[32,4096]{1,0:T(8,128)(2,1)}, bf16[512,4096]{1,0:T(8,128)(2,1)}, f32[8,128]{1,0:T(8,128)}) custom-call(bf16[32,4096]{1,0:T(8,128)(2,1)S(1)} %copy-done.3, f32[4,256,128]{2,1,0:T(8,128)S(1)} %get-tuple-element.56.refs_1_, f32[4,256,128]{2,1,0:T(8,128)S(1)} %get-tuple-element.57.refs_2_, ...), custom_call_target="tpu_custom_call", output_to_operand_aliasing={{0}: (37, {}), {1}: (38, {})} | custom-call | flops 2147483648 | bytes 131072 | tf_op jit(solution)/shard_map/finish/pallas_call | solution.py:530
  (86 shorter events, 0.2 us)
Async XLA Ops:
  2.4 5.6 %copy-start.21 = (bf16[2,20,8,512]{3,2,1,0:T(8,128)(2,1)}, bf16[2,20,8,512]{3,2,1,0:T(8,128)(2,1)S(1)}, u32[]{:S(2)}) copy-start(bf16[2,20,8,512]{3,2,1,0:T(8,128)(2,1)S(1)} %get-tuple-element.44.rest_0_) | copy-start | bytes 983044
  2.4 26.7 %collective-permute-start.5 = (bf16[2,20,8,512]{3,2,1,0:T(8,128)(2,1)S(1)}, bf16[2,20,8,512]{3,2,1,0:T(8,128)(2,1)S(1)}, u32[]{:S(2)}, u32[]{:S(2)}) collective-permute-start(bf16[2,20,8,512]{3,2,1,0:T(8,128)(2,1)S(1)} %get-tuple-element.50), channel_id=1, source_target_pairs={{0,8},{1,9},{2,10},{3,11},{4,12},{5,13},{6,14},{7,15},{8,0},{9,1},... | collective-permute-start | bytes 983048 | tf_op jit(solution)/shard_map/ppermute | solution.py:595
  6.5 14.0 %copy-start.41 = (s32[4]{0:T(128)S(1)}, s32[4]{0:T(128)}, u32[]{:S(2)}) copy-start(s32[4]{0:T(128)} %constant.57.clone) | copy-start | bytes 52
  6.5 14.1 %copy-start.40 = (s32[12]{0:T(128)S(1)}, s32[12]{0:T(128)}, u32[]{:S(2)}) copy-start(s32[12]{0:T(128)} %constant.58.clone) | copy-start | bytes 148
  6.5 14.1 %copy-start.39 = (s32[32]{0:T(128)S(1)}, s32[32]{0:T(128)}, u32[]{:S(2)}) copy-start(s32[32]{0:T(128)} %param.21) | copy-start | bytes 388
  6.5 15.4 %copy-start.38 = (s32[32,64]{1,0:T(8,128)S(1)}, s32[32,64]{1,0:T(8,128)}, u32[]{:S(2)}) copy-start(s32[32,64]{1,0:T(8,128)} %param.20) | copy-start | bytes 24580
  6.5 22.6 %collective-permute-start.3 = (bf16[2,20,8,512]{3,2,1,0:T(8,128)(2,1)S(1)}, bf16[2,20,8,512]{3,2,1,0:T(8,128)(2,1)S(1)}, u32[]{:S(2)}, u32[]{:S(2)}) collective-permute-start(bf16[2,20,8,512]{3,2,1,0:T(8,128)(2,1)S(1)} %get-tuple-element.44.rest_0_), channel_id=1, source_target_pairs={{0,12},{1,13},{2,14},{3,15},{4,8},{5,9},{6,10},{7,11},{8,4},{9,5},... | collective-permute-start | bytes 983048 | tf_op jit(solution)/shard_map/ppermute | solution.py:595
  12.7 0.7 copy-start.6
  13.4 0.7 copy-start.24
  14.1 0.7 copy-start.26
  14.7 0.7 copy-start.28
  15.4 0.7 copy-start.30
  16.1 0.7 copy-start.32
  16.7 0.7 copy-start.34
  17.4 0.7 copy-start.36
  18.0 32.0 %collective-permute-start = (bf16[2,20,8,512]{3,2,1,0:T(8,128)(2,1)}, bf16[2,20,8,512]{3,2,1,0:T(8,128)(2,1)S(1)}, u32[]{:S(2)}, u32[]{:S(2)}) collective-permute-start(bf16[2,20,8,512]{3,2,1,0:T(8,128)(2,1)} %get-tuple-element.46), channel_id=1, source_target_pairs={{0,1},{1,0},{2,3},{3,2},{4,5},{5,4},{6,7},{7,6},{8,9},{9,8},{10,11... | collective-permute-start | bytes 983048 | tf_op jit(solution)/shard_map/ppermute | solution.py:595
  18.0 37.1 %collective-permute-start.1 = (bf16[2,20,8,512]{3,2,1,0:T(8,128)(2,1)}, bf16[2,20,8,512]{3,2,1,0:T(8,128)(2,1)S(1)}, u32[]{:S(2)}, u32[]{:S(2)}) collective-permute-start(bf16[2,20,8,512]{3,2,1,0:T(8,128)(2,1)} %get-tuple-element.47), channel_id=1, source_target_pairs={{0,2},{1,3},{2,0},{3,1},{4,6},{5,7},{6,4},{7,5},{8,10},{9,11},{10,... | collective-permute-start | bytes 983048 | tf_op jit(solution)/shard_map/ppermute | solution.py:595
  19.5 36.6 %collective-permute-start.2 = (bf16[2,20,8,512]{3,2,1,0:T(8,128)(2,1)S(1)}, bf16[2,20,8,512]{3,2,1,0:T(8,128)(2,1)S(1)}, u32[]{:S(2)}, u32[]{:S(2)}) collective-permute-start(bf16[2,20,8,512]{3,2,1,0:T(8,128)(2,1)S(1)} %get-tuple-element.48), channel_id=1, source_target_pairs={{0,3},{1,2},{2,1},{3,0},{4,7},{5,6},{6,5},{7,4},{8,11},{9,10},{10,... | collective-permute-start | bytes 983048 | tf_op jit(solution)/shard_map/ppermute | solution.py:595
  29.1 27.7 %collective-permute-start.4 = (bf16[2,20,8,512]{3,2,1,0:T(8,128)(2,1)S(1)}, bf16[2,20,8,512]{3,2,1,0:T(8,128)(2,1)S(1)}, u32[]{:S(2)}, u32[]{:S(2)}) collective-permute-start(bf16[2,20,8,512]{3,2,1,0:T(8,128)(2,1)S(1)} %get-tuple-element.49), channel_id=1, source_target_pairs={{0,4},{1,5},{2,6},{3,7},{4,0},{5,1},{6,2},{7,3},{8,12},{9,13},{10,... | collective-permute-start | bytes 983048 | tf_op jit(solution)/shard_map/ppermute | solution.py:595
  29.1 20.9 %copy-start.4 = (bf16[2,20,8,512]{3,2,1,0:T(8,128)(2,1)}, bf16[2,20,8,512]{3,2,1,0:T(8,128)(2,1)S(1)}, u32[]{:S(2)}) copy-start(bf16[2,20,8,512]{3,2,1,0:T(8,128)(2,1)S(1)} %collective-permute-done.3.refs_11_.refs_8_.refs_18_) | copy-start | bytes 983044
  29.1 32.0 %collective-permute-start.6 = (bf16[2,20,8,512]{3,2,1,0:T(8,128)(2,1)S(1)}, bf16[2,20,8,512]{3,2,1,0:T(8,128)(2,1)S(1)}, u32[]{:S(2)}, u32[]{:S(2)}) collective-permute-start(bf16[2,20,8,512]{3,2,1,0:T(8,128)(2,1)S(1)} %get-tuple-element.51), channel_id=1, source_target_pairs={{0,5},{1,4},{2,7},{3,6},{4,1},{5,0},{6,3},{7,2},{8,13},{9,12},{10,... | collective-permute-start | bytes 983048 | tf_op jit(solution)/shard_map/ppermute | solution.py:595
  36.2 25.8 %copy-start.23 = (s32[1,256]{1,0:T(1,128)S(1)}, s32[1,256]{1,0:T(1,128)}, u32[]{:S(2)}) copy-start(s32[1,256]{1,0:T(1,128)} %refs_7_.3) | copy-start | bytes 3076
  50.1 0.7 copy-start.8
  50.8 100.1 %collective-permute-start.11 = (bf16[2,20,8,256]{3,2,1,0:T(8,128)(2,1)}, bf16[2,20,8,256]{3,2,1,0:T(8,128)(2,1)S(1)}, u32[]{:S(2)}, u32[]{:S(2)}) collective-permute-start(bf16[2,20,8,256]{3,2,1,0:T(8,128)(2,1)} %get-tuple-element.61), channel_id=1, source_target_pairs={{0,14},{1,15},{2,12},{3,13},{4,10},{5,11},{6,8},{7,9},{8,6},{9,7},... | collective-permute-start | bytes 491528 | tf_op jit(solution)/shard_map/ppermute | solution.py:595
  55.1 0.7 copy-start.10
  55.9 46.5 %collective-permute-start.7 = (bf16[2,20,8,512]{3,2,1,0:T(8,128)(2,1)}, bf16[2,20,8,512]{3,2,1,0:T(8,128)(2,1)S(1)}, u32[]{:S(2)}, u32[]{:S(2)}) collective-permute-start(bf16[2,20,8,512]{3,2,1,0:T(8,128)(2,1)} %get-tuple-element.52), channel_id=1, source_target_pairs={{0,13},{1,12},{2,15},{3,14},{4,9},{5,8},{6,11},{7,10},{8,5},{9,4},... | collective-permute-start | bytes 983048 | tf_op jit(solution)/shard_map/ppermute | solution.py:595
  56.1 0.7 copy-start.12
  56.9 47.9 %collective-permute-start.8 = (bf16[2,20,8,512]{3,2,1,0:T(8,128)(2,1)}, bf16[2,20,8,512]{3,2,1,0:T(8,128)(2,1)S(1)}, u32[]{:S(2)}, u32[]{:S(2)}) collective-permute-start(bf16[2,20,8,512]{3,2,1,0:T(8,128)(2,1)} %get-tuple-element.53), channel_id=1, source_target_pairs={{0,6},{1,7},{2,4},{3,5},{4,2},{5,3},{6,0},{7,1},{8,14},{9,15},{10,... | collective-permute-start | bytes 983048 | tf_op jit(solution)/shard_map/ppermute | solution.py:595
  56.9 0.7 copy-start.14
  57.6 50.2 %collective-permute-start.9 = (bf16[2,20,8,512]{3,2,1,0:T(8,128)(2,1)}, bf16[2,20,8,512]{3,2,1,0:T(8,128)(2,1)S(1)}, u32[]{:S(2)}, u32[]{:S(2)}) collective-permute-start(bf16[2,20,8,512]{3,2,1,0:T(8,128)(2,1)} %get-tuple-element.54), channel_id=1, source_target_pairs={{0,9},{1,8},{2,11},{3,10},{4,13},{5,12},{6,15},{7,14},{8,1},{9,0},... | collective-permute-start | bytes 983048 | tf_op jit(solution)/shard_map/ppermute | solution.py:595
  61.1 0.7 copy-start.16
  61.9 46.2 %collective-permute-start.10 = (bf16[2,20,8,512]{3,2,1,0:T(8,128)(2,1)}, bf16[2,20,8,512]{3,2,1,0:T(8,128)(2,1)S(1)}, u32[]{:S(2)}, u32[]{:S(2)}) collective-permute-start(bf16[2,20,8,512]{3,2,1,0:T(8,128)(2,1)} %get-tuple-element.55), channel_id=1, source_target_pairs={{0,7},{1,6},{2,5},{3,4},{4,3},{5,2},{6,1},{7,0},{8,15},{9,14},{10,... | collective-permute-start | bytes 983048 | tf_op jit(solution)/shard_map/ppermute | solution.py:595
  62.0 2.2 %copy-start = (bf16[512,4096]{1,0:T(8,128)(2,1)S(1)}, bf16[512,4096]{1,0:T(8,128)(2,1)}, u32[]{:S(2)}) copy-start(bf16[512,4096]{1,0:T(8,128)(2,1)} %refs_5_.3) | copy-start | bytes 12582916
  64.2 1.2 copy-start.2
  65.4 1.0 copy-start.5
  66.4 1.0 copy-start.7
  67.3 1.0 copy-start.9
  68.3 1.0 copy-start.11
  69.3 1.0 copy-start.13
  70.2 1.0 copy-start.15
  71.2 1.0 copy-start.17
  72.2 30.2 %copy-start.37 = (bf16[2,20,8,256]{3,2,1,0:T(8,128)(2,1)S(1)}, bf16[2,20,8,256]{3,2,1,0:T(8,128)(2,1)}, u32[]{:S(2)}) copy-start(bf16[2,20,8,256]{3,2,1,0:T(8,128)(2,1)} %copy-done.36) | copy-start | bytes 491524
  72.2 32.5 %copy-start.35 = (bf16[2,20,8,256]{3,2,1,0:T(8,128)(2,1)S(1)}, bf16[2,20,8,256]{3,2,1,0:T(8,128)(2,1)}, u32[]{:S(2)}) copy-start(bf16[2,20,8,256]{3,2,1,0:T(8,128)(2,1)} %copy-done.34) | copy-start | bytes 491524
  72.2 35.6 %copy-start.33 = (bf16[2,20,8,256]{3,2,1,0:T(8,128)(2,1)S(1)}, bf16[2,20,8,256]{3,2,1,0:T(8,128)(2,1)}, u32[]{:S(2)}) copy-start(bf16[2,20,8,256]{3,2,1,0:T(8,128)(2,1)} %copy-done.32) | copy-start | bytes 491524
  72.2 35.9 %copy-start.31 = (bf16[2,20,8,256]{3,2,1,0:T(8,128)(2,1)S(1)}, bf16[2,20,8,256]{3,2,1,0:T(8,128)(2,1)}, u32[]{:S(2)}) copy-start(bf16[2,20,8,256]{3,2,1,0:T(8,128)(2,1)} %copy-done.30) | copy-start | bytes 491524
  102.4 21.6 %collective-permute-start.13 = (bf16[2,20,8,256]{3,2,1,0:T(8,128)(2,1)S(1)}, bf16[2,20,8,256]{3,2,1,0:T(8,128)(2,1)S(1)}, u32[]{:S(2)}, u32[]{:S(2)}) collective-permute-start(bf16[2,20,8,256]{3,2,1,0:T(8,128)(2,1)S(1)} %copy-done.37), channel_id=1, source_target_pairs={{0,14},{1,15},{2,12},{3,13},{4,10},{5,11},{6,8},{7,9},{8,6},{9,7},... | collective-permute-start | bytes 491528 | tf_op jit(solution)/shard_map/ppermute | solution.py:595
  104.7 24.6 %collective-permute-start.14 = (bf16[2,20,8,256]{3,2,1,0:T(8,128)(2,1)S(1)}, bf16[2,20,8,256]{3,2,1,0:T(8,128)(2,1)S(1)}, u32[]{:S(2)}, u32[]{:S(2)}) collective-permute-start(bf16[2,20,8,256]{3,2,1,0:T(8,128)(2,1)S(1)} %copy-done.35), channel_id=1, source_target_pairs={{0,10},{1,11},{2,8},{3,9},{4,14},{5,15},{6,12},{7,13},{8,2},{9,3},... | collective-permute-start | bytes 491528 | tf_op jit(solution)/shard_map/ppermute | solution.py:595
  107.8 21.9 %collective-permute-start.15 = (bf16[2,20,8,256]{3,2,1,0:T(8,128)(2,1)S(1)}, bf16[2,20,8,256]{3,2,1,0:T(8,128)(2,1)S(1)}, u32[]{:S(2)}, u32[]{:S(2)}) collective-permute-start(bf16[2,20,8,256]{3,2,1,0:T(8,128)(2,1)S(1)} %copy-done.33), channel_id=1, source_target_pairs={{0,15},{1,14},{2,13},{3,12},{4,11},{5,10},{6,9},{7,8},{8,7},{9,6},... | collective-permute-start | bytes 491528 | tf_op jit(solution)/shard_map/ppermute | solution.py:595
  108.1 35.0 %collective-permute-start.16 = (bf16[2,20,8,256]{3,2,1,0:T(8,128)(2,1)S(1)}, bf16[2,20,8,256]{3,2,1,0:T(8,128)(2,1)S(1)}, u32[]{:S(2)}, u32[]{:S(2)}) collective-permute-start(bf16[2,20,8,256]{3,2,1,0:T(8,128)(2,1)S(1)} %copy-done.31), channel_id=1, source_target_pairs={{0,11},{1,10},{2,9},{3,8},{4,15},{5,14},{6,13},{7,12},{8,3},{9,2},... | collective-permute-start | bytes 491528 | tf_op jit(solution)/shard_map/ppermute | solution.py:595
  109.8 12.4 %copy-start.3 = (bf16[32,4096]{1,0:T(8,128)(2,1)S(1)}, bf16[32,4096]{1,0:T(8,128)(2,1)}, u32[]{:S(2)}) copy-start(bf16[32,4096]{1,0:T(8,128)(2,1)} %refs_0_.8) | copy-start | bytes 786436
  109.8 12.4 %copy-start.18 = (f32[4,256,128]{2,1,0:T(8,128)S(1)}, f32[4,256,128]{2,1,0:T(8,128)}, u32[]{:S(2)}) copy-start(f32[4,256,128]{2,1,0:T(8,128)} %get-tuple-element.41.refs_1_) | copy-start | bytes 1572868
  109.8 12.4 %copy-start.19 = (f32[4,256,128]{2,1,0:T(8,128)S(1)}, f32[4,256,128]{2,1,0:T(8,128)}, u32[]{:S(2)}) copy-start(f32[4,256,128]{2,1,0:T(8,128)} %get-tuple-element.42.refs_2_) | copy-start | bytes 1572868
  109.8 12.4 %copy-start.20 = (f32[4,256,128]{2,1,0:T(8,128)S(1)}, f32[4,256,128]{2,1,0:T(8,128)}, u32[]{:S(2)}) copy-start(f32[4,256,128]{2,1,0:T(8,128)} %get-tuple-element.43.refs_3_) | copy-start | bytes 1572868
  109.8 12.4 %copy-start.22 = (s32[32,1]{1,0:T(8,128)S(1)}, s32[32,1]{1,0:T(8,128)}, u32[]{:S(2)}) copy-start(s32[32,1]{1,0:T(8,128)} %copy.24.rest_ref.refs_6_) | copy-start | bytes 388
  122.2 1.8 %copy-start.29 = (bf16[2,20,8,256]{3,2,1,0:T(8,128)(2,1)S(1)}, bf16[2,20,8,256]{3,2,1,0:T(8,128)(2,1)}, u32[]{:S(2)}) copy-start(bf16[2,20,8,256]{3,2,1,0:T(8,128)(2,1)} %copy-done.28) | copy-start | bytes 491524
  122.2 7.1 %copy-start.27 = (bf16[2,20,8,256]{3,2,1,0:T(8,128)(2,1)S(1)}, bf16[2,20,8,256]{3,2,1,0:T(8,128)(2,1)}, u32[]{:S(2)}) copy-start(bf16[2,20,8,256]{3,2,1,0:T(8,128)(2,1)} %copy-done.26) | copy-start | bytes 491524
  122.2 7.4 %copy-start.25 = (bf16[2,20,8,256]{3,2,1,0:T(8,128)(2,1)S(1)}, bf16[2,20,8,256]{3,2,1,0:T(8,128)(2,1)}, u32[]{:S(2)}) copy-start(bf16[2,20,8,256]{3,2,1,0:T(8,128)(2,1)} %copy-done.24) | copy-start | bytes 491524
  124.0 26.9 %collective-permute-start.12 = (bf16[2,20,8,256]{3,2,1,0:T(8,128)(2,1)S(1)}, bf16[2,20,8,256]{3,2,1,0:T(8,128)(2,1)S(1)}, u32[]{:S(2)}, u32[]{:S(2)}) collective-permute-start(bf16[2,20,8,256]{3,2,1,0:T(8,128)(2,1)S(1)} %copy-done.29), channel_id=1, source_target_pairs={{0,10},{1,11},{2,8},{3,9},{4,14},{5,15},{6,12},{7,13},{8,2},{9,3},... | collective-permute-start | bytes 491528 | tf_op jit(solution)/shard_map/ppermute | solution.py:595
  129.3 26.1 %collective-permute-start.17 = (bf16[2,20,8,256]{3,2,1,0:T(8,128)(2,1)S(1)}, bf16[2,20,8,256]{3,2,1,0:T(8,128)(2,1)S(1)}, u32[]{:S(2)}, u32[]{:S(2)}) collective-permute-start(bf16[2,20,8,256]{3,2,1,0:T(8,128)(2,1)S(1)} %copy-done.27), channel_id=1, source_target_pairs={{0,15},{1,14},{2,13},{3,12},{4,11},{5,10},{6,9},{7,8},{8,7},{9,6},... | collective-permute-start | bytes 491528 | tf_op jit(solution)/shard_map/ppermute | solution.py:595
  129.7 27.5 %collective-permute-start.18 = (bf16[2,20,8,256]{3,2,1,0:T(8,128)(2,1)S(1)}, bf16[2,20,8,256]{3,2,1,0:T(8,128)(2,1)S(1)}, u32[]{:S(2)}, u32[]{:S(2)}) collective-permute-start(bf16[2,20,8,256]{3,2,1,0:T(8,128)(2,1)S(1)} %copy-done.25), channel_id=1, source_target_pairs={{0,11},{1,10},{2,9},{3,8},{4,15},{5,14},{6,13},{7,12},{8,3},{9,2},... | collective-permute-start | bytes 491528 | tf_op jit(solution)/shard_map/ppermute | solution.py:595
  150.9 6.3 %copy-start.1 = (bf16[512,4096]{1,0:T(8,128)(2,1)S(1)}, bf16[512,4096]{1,0:T(8,128)(2,1)}, u32[]{:S(2)}) copy-start(bf16[512,4096]{1,0:T(8,128)(2,1)} %refs_5_.3) | copy-start | bytes 12582916
